TPU v7x, 256 devices: a whole 4x4x8 slice. The times are simulated.
256 devices in a mesh: branch: 2 (over x_lo), row: 8 (over y, core), col: 16 (over x_hi, z).
Axes of the slice: x: 4 (x_hi: 2, x_lo: 2; x = x_hi * 2 + x_lo), y: 4, z: 8, core: 2. Of those that a mesh axis runs over, the one named last changes fastest.
Arguments:
- homolog_embedding: bfloat16 [256, 512, 256], P(('branch', 'row'), 'col'), may hold values from -6 to 6
- pair_representation: bfloat16 [512, 512, 128], P('col', ('branch', 'row')), may hold values from -6 to 6
- alignment_entry_mask: int32 [256, 512], P(('branch', 'row'), 'col'), may hold values 0 or 1
- residue_presence_mask: int32 [512], replicated, may hold values 0 or 1
- residue_chain_index: int32 [512], replicated, may hold values from 0 to 3, as said below
- row_projection_weights: bfloat16 [256, 1024], replicated, may hold values from -25 to 25
- horizontal_attend_merge: bfloat16 [256, 256], replicated, may hold values from -0.375 to 0.375
- pair_bias_matrix: bfloat16 [128, 8], replicated, may hold values from -0.5 to 0.5
- same_chain_bias: float32 [8], replicated, may hold values from -5 to 5
- column_projection_weights: bfloat16 [256, 1024], replicated, may hold values from -25 to 25
- vertical_attend_merge: bfloat16 [256, 256], replicated, may hold values from -0.375 to 0.375
- homolog_mlp_expand: bfloat16 [256, 1024], replicated, may hold values from -0.375 to 0.375
- homolog_mlp_contract: bfloat16 [1024, 256], replicated, may hold values from -0.1875 to 0.1875
- tensor_product_linear: bfloat16 [256, 64], replicated, may hold values from -0.375 to 0.375
- outer_output_matrix: bfloat16 [1024, 128], replicated, may hold values from -1 to 1
- triangle_input_weights: bfloat16 [128, 640], replicated, may hold values from -0.5 to 0.5
- triangle_output_matrix: bfloat16 [128, 128], replicated, may hold values from -2 to 2
- pair_up_weight: bfloat16 [128, 512], replicated, may hold values from -0.5 to 0.5
- pair_down_weight: bfloat16 [512, 128], replicated, may hold values from -0.25 to 0.25
Outputs:
- msa_out: bfloat16 [256, 512, 256], P(('branch', 'row'), 'col')
- updated_pair_state: bfloat16 [512, 512, 128], P('col', ('branch', 'row'))
Inputs may be any that keep to these rules, and one draw needn't show every extreme that they name: `residue_chain_index`: chain numbers never fall along the residues.
All inputs are finite; a program needn't handle non-finite values. No bound on the sum of `alignment_entry_mask` on one device may be relied on, other than what follows from the above.
Results may differ from a plain program's by a relative error of at most 0.025.
The roundings to bfloat16 on the way count: a program that leaves them out, or rounds other values in their place, can miss the bound.
Values may be sent and summed in bfloat16 or wider, within the bound.
A program may use at most 128 MiB of HBM per device.

v0:
```python
import math

import jax
import jax.numpy as jnp
from jax import lax
from jax.sharding import Mesh
from jax.sharding import PartitionSpec as P

HEADS = 8
PER_HEAD_WIDTH = 32
CZ = 128
PRODUCT_FEATURES = 32
COL = ("col_0", "col_1")


EPSILON = 1e-05
NEGATIVE = -1000000000.0


def in_order(blocks, dim):
    dims = list(blocks.shape[1:])
    dims[dim] *= blocks.shape[0]
    return jnp.moveaxis(blocks, 0, dim).reshape(dims)


def copy_for_each(x, axis):
    copies = jnp.broadcast_to(x, (lax.axis_size(axis), *x.shape))
    return lax.all_to_all(copies, axis, split_axis=0, concat_axis=0, tiled=True)


def gathered_copies(x, axis, dim):
    return in_order(copy_for_each(x, axis), dim)


def side_by_side(arrays, axis, split_dim, concat_dim, along):
    widths = [math.prod(a.shape[along:]) for a in arrays]
    both = jnp.concatenate(
        [a.reshape(*a.shape[:along], w) for a, w in zip(arrays, widths)], axis=along
    )
    out = lax.all_to_all(both, axis, split_axis=split_dim, concat_axis=concat_dim, tiled=True)
    blocks = jnp.split(out, [sum(widths[:k]) for k in range(1, len(widths))], axis=along)
    return tuple((b.reshape(*out.shape[:along], *a.shape[along:]) for a, b in zip(arrays, blocks)))


def gather_in_order(x, axes, turns):
    blocks = x[None]
    for k in turns:
        blocks = lax.all_gather(blocks, axes[k], axis=0, tiled=True)
    carried = [lax.axis_size(axes[k]) for k in reversed(turns)]
    blocks = blocks.reshape(*carried, *x.shape)
    turned = sorted(range(len(turns)), key=lambda place: turns[len(turns) - 1 - place])
    return blocks.transpose(*turned, *range(len(turns), blocks.ndim)).reshape(-1, *x.shape)


def gathered_by_axis(x, axes, turns, dim):
    return in_order(gather_in_order(x, axes, turns), dim)


def layer_normalize(tensor):
    tensor = tensor.astype(jnp.float32)
    centre = tensor - jnp.mean(tensor, axis=-1, keepdims=True)
    spread = jnp.mean(centre * centre, axis=-1, keepdims=True)
    return centre * lax.rsqrt(spread + EPSILON)


def split_blocks(normed, weights):
    projected = jnp.dot(normed, weights, preferred_element_type=jnp.float32)
    channel_count = weights.shape[0]
    queries = (projected[..., :channel_count] * PER_HEAD_WIDTH ** (-0.5)).astype(jnp.bfloat16)
    key_rows = projected[..., channel_count : 2 * channel_count].astype(jnp.bfloat16)
    value_rows = projected[..., 2 * channel_count : 3 * channel_count].astype(jnp.bfloat16)
    gating = jax.nn.sigmoid(projected[..., 3 * channel_count :])
    return (queries, key_rows, value_rows, gating)


def on_device(
    homolog_embedding,
    pair_representation,
    alignment_entry_mask,
    residue_presence_mask,
    residue_chain_index,
    row_projection_weights,
    horizontal_attend_merge,
    pair_bias_matrix,
    same_chain_bias,
    column_projection_weights,
    vertical_attend_merge,
    homolog_mlp_expand,
    homolog_mlp_contract,
    tensor_product_linear,
    outer_output_matrix,
    triangle_input_weights,
    triangle_output_matrix,
    pair_up_weight,
    pair_down_weight,
):
    device_local_rows, residue_total, channel_count = homolog_embedding.shape
    pair_cols = pair_representation.shape[1]
    row_place = lax.axis_index(COL)
    col_place = lax.axis_index(("branch", "row"))
    chain_here = lax.dynamic_slice_in_dim(
        residue_chain_index, row_place * residue_total, residue_total
    )
    chain_there = lax.dynamic_slice_in_dim(residue_chain_index, col_place * pair_cols, pair_cols)
    residue_keep = residue_presence_mask.astype(jnp.float32)
    keep_here = lax.dynamic_slice_in_dim(residue_keep, row_place * residue_total, residue_total)
    keep_there = lax.dynamic_slice_in_dim(residue_keep, col_place * pair_cols, pair_cols)
    pair_normed = layer_normalize(pair_representation).astype(jnp.bfloat16)
    same_chain = (chain_here[:, None] == chain_there[None, :]).astype(jnp.float32)
    bias_terms = (
        jnp.dot(pair_normed, pair_bias_matrix, preferred_element_type=jnp.float32)
        + same_chain_bias[None, None, :] * same_chain[:, :, None]
    )
    bias_tile = jnp.transpose(bias_terms, (2, 0, 1)).astype(jnp.bfloat16)
    pair_bias = gathered_copies(bias_tile, ("branch", "row"), 2)
    key_presence_mask = alignment_entry_mask.astype(jnp.bfloat16)
    row_normed_input = layer_normalize(homolog_embedding).astype(jnp.bfloat16)
    normed_whole, mask_whole = side_by_side((row_normed_input, key_presence_mask), COL, 0, 1, 2)
    full_bias = lax.all_gather(pair_bias, COL, axis=1, tiled=True).astype(jnp.float32)
    few_rows, all_residues = mask_whole.shape
    queries, key_rows, value_rows, gating = split_blocks(normed_whole, row_projection_weights)
    query_heads = queries.reshape(few_rows, all_residues, HEADS, PER_HEAD_WIDTH)
    key_heads = key_rows.reshape(few_rows, all_residues, HEADS, PER_HEAD_WIDTH)
    value_heads = value_rows.reshape(few_rows, all_residues, HEADS, PER_HEAD_WIDTH)
    scores = (
        jnp.einsum("sihd,sjhd->shij", query_heads, key_heads, preferred_element_type=jnp.float32)
        + full_bias[None]
    )
    scores = jnp.where(mask_whole[:, None, None, :] > 0, scores, NEGATIVE)
    highest = jnp.max(scores, axis=-1, keepdims=True)
    powers = jnp.exp(scores - highest)
    totals = jnp.sum(powers, axis=-1)
    summed = jnp.einsum(
        "shij,sjhd->sihd",
        powers.astype(jnp.bfloat16),
        value_heads,
        preferred_element_type=jnp.float32,
    )
    attended = (summed / jnp.transpose(totals, (0, 2, 1))[..., None]).reshape(
        few_rows, all_residues, channel_count
    )
    gated_whole = (attended * gating).astype(jnp.bfloat16)
    row_gated = lax.all_to_all(gated_whole, COL, split_axis=1, concat_axis=0, tiled=True)
    alignment_row_state = homolog_embedding.astype(jnp.float32) + jnp.dot(
        row_gated, horizontal_attend_merge, preferred_element_type=jnp.float32
    )
    column_normed_input = layer_normalize(alignment_row_state).astype(jnp.bfloat16)
    group_count = lax.axis_size(("branch", "row"))
    residue_piece = residue_total // group_count
    split_input = column_normed_input.reshape(
        device_local_rows, group_count, residue_piece, channel_count
    )
    split_mask = key_presence_mask.reshape(device_local_rows, group_count, residue_piece)
    normed_cols = lax.all_to_all(
        split_input, ("branch", "row"), split_axis=1, concat_axis=0, tiled=True
    )
    mask_cols = lax.all_to_all(
        split_mask, ("branch", "row"), split_axis=1, concat_axis=0, tiled=True
    )
    total_rows = normed_cols.shape[0]
    residue_count = normed_cols.shape[2]
    normed_flat = normed_cols.reshape(total_rows, residue_count, channel_count)
    mask_flat = mask_cols.reshape(total_rows, residue_count)
    col_queries, col_keys, col_values, col_gating = split_blocks(
        normed_flat, column_projection_weights
    )
    query_part = col_queries.reshape(total_rows, residue_count, HEADS, PER_HEAD_WIDTH)
    key_part = col_keys.reshape(total_rows, residue_count, HEADS, PER_HEAD_WIDTH)
    value_part = col_values.reshape(total_rows, residue_count, HEADS, PER_HEAD_WIDTH)
    scores = jnp.einsum("sihd,tihd->ihst", query_part, key_part, preferred_element_type=jnp.float32)
    scores = jnp.where(jnp.transpose(mask_flat)[:, None, None, :] > 0, scores, NEGATIVE)
    highest = jnp.max(scores, axis=-1, keepdims=True)
    powers = jnp.exp(scores - highest)
    totals = jnp.sum(powers, axis=-1)
    summed = jnp.einsum(
        "ihst,tihd->ihsd",
        powers.astype(jnp.bfloat16),
        value_part,
        preferred_element_type=jnp.float32,
    )
    attended = jnp.transpose(summed / totals[..., None], (2, 0, 1, 3)).reshape(
        total_rows, residue_count, channel_count
    )
    gated = (attended * col_gating).astype(jnp.bfloat16)
    gated_cols = gated.reshape(total_rows, 1, residue_count, channel_count)
    returned = lax.all_to_all(
        gated_cols, ("branch", "row"), split_axis=0, concat_axis=1, tiled=True
    )
    column_gated_output = returned.reshape(device_local_rows, residue_total, channel_count)
    alignment_column_state = alignment_row_state + jnp.dot(
        column_gated_output, vertical_attend_merge, preferred_element_type=jnp.float32
    )
    transition_normed_input = layer_normalize(alignment_column_state).astype(jnp.bfloat16)
    alignment_hidden_units = jax.nn.relu(
        jnp.dot(transition_normed_input, homolog_mlp_expand, preferred_element_type=jnp.float32)
    ).astype(jnp.bfloat16)
    alignment_final_state = alignment_column_state + jnp.dot(
        alignment_hidden_units, homolog_mlp_contract, preferred_element_type=jnp.float32
    )
    outer_normed_input = layer_normalize(alignment_final_state).astype(jnp.bfloat16)
    factors = (
        jnp.dot(outer_normed_input, tensor_product_linear, preferred_element_type=jnp.float32)
        * alignment_entry_mask.astype(jnp.float32)[:, :, None]
    )
    left_factor = (
        factors[..., :PRODUCT_FEATURES]
        .astype(jnp.bfloat16)
        .reshape(device_local_rows, residue_total * PRODUCT_FEATURES)
    )
    right_factor = (
        factors[..., PRODUCT_FEATURES:]
        .astype(jnp.bfloat16)
        .reshape(device_local_rows, residue_total * PRODUCT_FEATURES)
    )
    left_all = gathered_copies(left_factor, ("branch", "row"), 0)
    right_cols = gathered_copies(right_factor, COL, 1)
    right_rows = lax.all_to_all(
        right_cols, ("branch", "row"), split_axis=1, concat_axis=0, tiled=True
    )
    seq_total = left_all.shape[0]
    outer_sum = lax.dot_general(
        left_all, right_rows, (((0,), (0,)), ((), ())), preferred_element_type=jnp.float32
    )
    outer_sum = jnp.transpose(
        outer_sum.reshape(residue_total, PRODUCT_FEATURES, pair_cols, PRODUCT_FEATURES),
        (0, 2, 1, 3),
    ).reshape(residue_total, pair_cols, PRODUCT_FEATURES * PRODUCT_FEATURES)
    outer_mean = (outer_sum / seq_total).astype(jnp.bfloat16)
    pair_opm = pair_representation.astype(jnp.float32) + jnp.dot(
        outer_mean, outer_output_matrix, preferred_element_type=jnp.float32
    )
    tri_normed = layer_normalize(pair_opm).astype(jnp.bfloat16)
    projected = jnp.dot(tri_normed, triangle_input_weights, preferred_element_type=jnp.float32)
    pair_keep = (keep_here[:, None] * keep_there[None, :])[:, :, None]
    tri_left = (
        pair_keep * jax.nn.sigmoid(projected[..., :CZ]) * projected[..., CZ : 2 * CZ]
    ).astype(jnp.bfloat16)
    tri_right = (
        pair_keep
        * jax.nn.sigmoid(projected[..., 2 * CZ : 3 * CZ])
        * projected[..., 3 * CZ : 4 * CZ]
    ).astype(jnp.bfloat16)
    tri_gate = jax.nn.sigmoid(projected[..., 4 * CZ :])
    right_all = gathered_by_axis(tri_right, COL, (0, 1), 0)
    turned = lax.psum_scatter(
        jnp.einsum("ikc,jkc->jic", tri_left, right_all, preferred_element_type=jnp.float32).astype(
            jnp.bfloat16
        ),
        ("branch", "row"),
        scatter_dimension=0,
        tiled=True,
    ).astype(jnp.float32)
    tri_mixed = jnp.transpose(turned, (1, 0, 2))
    mixed_normed = layer_normalize(tri_mixed).astype(jnp.bfloat16)
    pair_tri = pair_opm + tri_gate * jnp.dot(
        mixed_normed, triangle_output_matrix, preferred_element_type=jnp.float32
    )
    pair_trans_in = layer_normalize(pair_tri).astype(jnp.bfloat16)
    pair_hidden = jax.nn.relu(
        jnp.dot(pair_trans_in, pair_up_weight, preferred_element_type=jnp.float32)
    ).astype(jnp.bfloat16)
    updated_pair_state = (
        pair_tri + jnp.dot(pair_hidden, pair_down_weight, preferred_element_type=jnp.float32)
    ).astype(jnp.bfloat16)
    return (alignment_final_state.astype(jnp.bfloat16), updated_pair_state)


def solution(mesh):
    split = Mesh(
        mesh.devices.reshape(mesh.shape["branch"], mesh.shape["row"], 2, 8),
        ("branch", "row", "col_0", "col_1"),
    )
    in_specs = (
        P(("branch", "row"), COL, None),
        P(COL, ("branch", "row"), None),
        P(("branch", "row"), COL),
        P(),
        P(),
        P(),
        P(),
        P(),
        P(),
        P(),
        P(),
        P(),
        P(),
        P(),
        P(),
        P(),
        P(),
        P(),
        P(),
    )
    out_specs = (P(("branch", "row"), COL, None), P(COL, ("branch", "row"), None))
    return jax.shard_map(
        on_device, mesh=split, in_specs=in_specs, out_specs=out_specs, check_vma=False
    )
```

profile of v0, /device:TPU:1, one launch (start us, length us, event | category | flops | bytes accessed | tf_op | source)
XLA Modules:
  0.0 451.7 jit_solution(14638954488284932385)
XLA Ops:
  13.6 14.0 %all_to_all.94 = bf16[16,2,4096]{2,1,0:T(2,128)(2,1)S(1)} all-to-all(bf16[16,2,4096]{2,1,0:T(2,128)(2,1)S(1)} %reshape.320), channel_id=1, replica_groups=mesh['branch'=2,'row'=8,'col_0'=2,'col_1'=8] {'branch','row'}, dimensions={0} | all-to-all | bytes 524288 | tf_op jit(solution)/shard_map/all_to_all | solution.py:28
  28.2 1.8 copy.219
  32.7 24.2 %all_to_all.95 = bf16[16,32,257]{2,1,0:T(8,128)(2,1)S(1)} all-to-all(bf16[16,32,257]{2,1,0:T(8,128)(2,1)S(1)} %pad_maximum_fusion), channel_id=1, replica_groups=mesh['branch'=2,'row'=8,'col_0'=2,'col_1'=8] {'col_0','col_1'}, dimensions={0} | all-to-all | bytes 526336 | tf_op jit(solution)/shard_map/all_to_all | solution.py:40
  58.0 72.2 %all-gather.4.cloned.1.call-done = bf16[8,512,512]{2,0,1:T(8,128)(2,1)} async-done(((bf16[8,32,512]{2,0,1:T(8,128)(2,1)}), bf16[8,512,512]{2,0,1:T(8,128)(2,1)}) %all-gather.4.cloned.1.call-update) | async-done | bytes 4194320 | tf_op jit(solution)/shard_map/all_gather | solution.py:119
  130.2 7.6 %copy.190 = bf16[8,512,512]{1,2,0:T(8,128)(2,1)} copy(bf16[8,512,512]{2,0,1:T(8,128)(2,1)} %all-gather.4.cloned.1.call-done) | data formatting | bytes 8388608 | tf_op jit(solution)/shard_map/all_gather | solution.py:119
  137.8 4.2 fusion.116
  145.9 2.2 reduce.6
  148.9 4.6 %all-to-all-start.2 = ((bf16[16,2,4096]{2,1,0:T(2,128)(2,1)}), bf16[16,2,4096]{2,1,0:T(2,128)(2,1)S(1)}, u32[]{:S(2)}, u32[]{:S(2)}) async-start(bf16[16,2,4096]{2,1,0:T(2,128)(2,1)} %reshape.322), calls=%async_computation.2 | async-start | bytes 524288 | tf_op jit(solution)/shard_map/all_to_all | solution.py:143
  154.2 8.6 %all-to-all-done.2 = bf16[16,2,4096]{2,1,0:T(2,128)(2,1)S(1)} async-done(((bf16[16,2,4096]{2,1,0:T(2,128)(2,1)}), bf16[16,2,4096]{2,1,0:T(2,128)(2,1)S(1)}, u32[]{:S(2)}, u32[]{:S(2)}) %all-to-all-start.2) | async-done | bytes 262176 | tf_op jit(solution)/shard_map/all_to_all | solution.py:143
  162.8 10.4 %all-to-all-start.3 = ((bf16[16,16,2]{0,2,1:T(2,128)(2,1)}), bf16[16,16,2]{0,2,1:T(2,128)(2,1)S(1)}, u32[]{:S(2)}, u32[]{:S(2)}) async-start(bf16[16,16,2]{0,2,1:T(2,128)(2,1)} %bitcast.17), calls=%async_computation.3 | async-start | bytes 16384 | tf_op jit(solution)/shard_map/all_to_all | solution.py:157
  175.3 3.2 all-to-all-done.3
  178.6 4.0 all-to-all-start.4
  182.7 7.1 %all-to-all-done.4 = bf16[16,16,2,256]{3,2,0,1:T(2,128)(2,1)S(1)} async-done(((bf16[16,16,2,256]{3,2,0,1:T(2,128)(2,1)}), bf16[16,16,2,256]{3,2,0,1:T(2,128)(2,1)S(1)}, u32[]{:S(2)}, u32[]{:S(2)}) %all-to-all-start.4) | async-done | bytes 262176 | tf_op jit(solution)/shard_map/all_to_all | solution.py:154
  193.3 1.7 fusion.28
  196.7 10.6 %all_to_all.96 = bf16[256,1,2,256]{3,2,1,0:T(2,128)(2,1)S(1)} all-to-all(bf16[256,1,2,256]{3,2,1,0:T(2,128)(2,1)S(1)} %copy.203), channel_id=1, replica_groups=mesh['branch'=2,'row'=8,'col_0'=2,'col_1'=8] {'branch','row'}, dimensions={0} | all-to-all | bytes 524288 | tf_op jit(solution)/shard_map/all_to_all | solution.py:186
  208.3 2.1 fusion.120
  212.9 4.3 all-to-all-start.6
  217.4 9.6 %all-to-all-done.6 = bf16[16,16,1024]{2,1,0:T(8,128)(2,1)S(1)} async-done(((bf16[16,16,1024]{2,1,0:T(8,128)(2,1)}), bf16[16,16,1024]{2,1,0:T(8,128)(2,1)S(1)}, u32[]{:S(2)}, u32[]{:S(2)}) %all-to-all-start.6) | async-done | bytes 524320 | tf_op jit(solution)/shard_map/all_to_all | solution.py:28
  227.0 19.1 %all_to_all.97 = bf16[16,16,1024]{2,1,0:T(8,128)(2,1)} all-to-all(bf16[16,16,1024]{2,1,0:T(8,128)(2,1)S(1)} %broadcast_in_dim.38), channel_id=1, replica_groups=mesh['branch'=2,'row'=8,'col_0'=2,'col_1'=8] {'col_0','col_1'}, dimensions={0} | all-to-all | bytes 1048576 | tf_op jit(solution)/shard_map/all_to_all | solution.py:28
  246.1 6.6 %all-to-all-start.8 = ((bf16[16,16,1024]{2,0,1:T(8,128)(2,1)}), bf16[16,16,1024]{2,0,1:T(8,128)(2,1)S(1)}, u32[]{:S(2)}, u32[]{:S(2)}) async-start(bf16[16,16,1024]{2,0,1:T(8,128)(2,1)} %bitcast.43), calls=%async_computation.8 | async-start | bytes 1048576 | tf_op jit(solution)/shard_map/all_to_all | solution.py:217
  253.4 9.0 %all-to-all-done.8 = bf16[16,16,1024]{2,0,1:T(8,128)(2,1)S(1)} async-done(((bf16[16,16,1024]{2,0,1:T(8,128)(2,1)}), bf16[16,16,1024]{2,0,1:T(8,128)(2,1)S(1)}, u32[]{:S(2)}, u32[]{:S(2)}) %all-to-all-start.8) | async-done | bytes 524320 | tf_op jit(solution)/shard_map/all_to_all | solution.py:217
  262.6 4.5 fusion.2
  267.1 11.4 %convert_element_type.135 = bf16[32,32,1024]{2,1,0:T(8,128)(2,1)S(1)} reshape(bf16[32,32,32,32]{3,2,1,0:T(8,128)(2,1)} %fusion.2) | data formatting | bytes 4194304 | tf_op jit(solution)/shard_map/convert_element_type | solution.py:228
  280.7 8.9 %all-gather = bf16[64,32,128]{2,1,0:T(8,128)(2,1)} all-gather(bf16[32,32,128]{2,1,0:T(8,128)(2,1)S(1)} %get-tuple-element.2), channel_id=2, replica_groups=mesh['branch'=2,'row'=8,'col_0'=2,'col_1'=8] {'col_0'}, dimensions={0}, use_global_device_ids=true | all-gather | bytes 786432 | tf_op jit(solution)/shard_map/all_gather | solution.py:48
  289.9 2.4 copy.209
  292.3 49.2 %all-gather.6.cloned.1.call-done = bf16[16,32,32,128]{3,2,1,0:T(8,128)(2,1)} async-done(((bf16[2,32,32,128]{3,2,1,0:T(8,128)(2,1)}), bf16[16,32,32,128]{3,2,1,0:T(8,128)(2,1)}) %all-gather.6.cloned.1.call-update) | async-done | bytes 4194320 | tf_op jit(solution)/shard_map/all_gather | solution.py:48
  341.6 5.1 %copy.207 = bf16[2,8,32,32,128]{4,3,2,1,0:T(8,128)(2,1)} copy(bf16[2,8,32,32,128]{4,3,2,0,1:T(8,128)(2,1)} %bitcast.183) | data formatting | bytes 8388608 | tf_op jit(solution)/shard_map/transpose | solution.py:52
  346.6 8.6 %copy.208 = bf16[512,32,128]{0,1,2:T(8,128)(2,1)} copy(bf16[512,32,128]{2,1,0:T(8,128)(2,1)} %bitcast.182) | data formatting | bytes 8388608 | tf_op jit(solution)/shard_map/reshape;reshape | solution.py:23
  355.3 5.7 %convert_bitcast_fusion = bf16[512,32,128]{0,1,2:T(8,128)(2,1)} fusion(bf16[32,32,128]{1,0,2:T(8,128)(2,1)} %copy.209, bf16[512,32,128]{0,1,2:T(8,128)(2,1)} %copy.208), kind=kOutput, calls=%fused_computation.7 | convolution fusion | flops 136314880 | bytes 8650752 | tf_op jit(solution)/shard_map/ikc,jkc->jic/dot_general | solution.py:246
  361.0 9.1 %copy.210 = bf16[512,32,128]{2,1,0:T(8,128)(2,1)} copy(bf16[512,32,128]{0,1,2:T(8,128)(2,1)} %convert_bitcast_fusion) | data formatting | bytes 8388608 | tf_op jit(solution)/shard_map/convert_element_type | solution.py:246
  370.2 65.6 %reduce-scatter.2.cloned.1.call-done = bf16[32,32,128]{2,1,0:T(8,128)(2,1)} async-done(((bf16[512,32,128]{2,1,0:T(8,128)(2,1)}), bf16[32,32,128]{2,1,0:T(8,128)(2,1)}) %reduce-scatter.2.cloned.1.call-update) | async-done | bytes 262160 | tf_op jit(solution)/shard_map/reduce_scatter | solution.py:245
  442.5 2.7 fusion.24
  (143 shorter events, 36.8 us)
Async XLA Ops:
  7.2 49.7 %copy-start = (bf16[256,1024]{1,0:T(8,128)(2,1)S(1)}, bf16[256,1024]{1,0:T(8,128)(2,1)}, u32[]{:S(2)}) copy-start(bf16[256,1024]{1,0:T(8,128)(2,1)} %param.24) | copy-start | bytes 1572868
  7.2 123.0 %all-gather.4.cloned.1.call-start = ((), (), s32[]{:S(2)}) async-start(), calls=%async_computation.10 | async-start | bytes 4456448 | tf_op jit(solution)/shard_map/all_gather | solution.py:119
  12.5 19.2 %copy-start.13 = (s32[16,32]{1,0:T(8,128)S(1)}, s32[16,32]{1,0:T(8,128)}, u32[]{:S(2)}) copy-start(s32[16,32]{1,0:T(8,128)} %param.21) | copy-start | bytes 6148
  13.5 18.4 %copy-start.3 = (bf16[16,32,256]{2,1,0:T(8,128)(2,1)S(1)}, bf16[16,32,256]{2,1,0:T(8,128)(2,1)}, u32[]{:S(2)}) copy-start(bf16[16,32,256]{2,1,0:T(8,128)(2,1)} %param.19) | copy-start | bytes 786436
  144.6 28.8 %copy-start.10 = (bf16[256,256]{1,0:T(8,128)(2,1)S(1)}, bf16[256,256]{1,0:T(8,128)(2,1)}, u32[]{:S(2)}) copy-start(bf16[256,256]{1,0:T(8,128)(2,1)} %param.25) | copy-start | bytes 393220
  145.4 44.4 %copy-start.5 = (bf16[256,1024]{1,0:T(8,128)(2,1)S(1)}, bf16[256,1024]{1,0:T(8,128)(2,1)}, u32[]{:S(2)}) copy-start(bf16[256,1024]{1,0:T(8,128)(2,1)} %param.28) | copy-start | bytes 1572868
  148.9 13.8 %all-to-all-start.2 = ((bf16[16,2,4096]{2,1,0:T(2,128)(2,1)}), bf16[16,2,4096]{2,1,0:T(2,128)(2,1)S(1)}, u32[]{:S(2)}, u32[]{:S(2)}) async-start(bf16[16,2,4096]{2,1,0:T(2,128)(2,1)} %reshape.322), calls=%async_computation.2 | async-start | bytes 524288 | tf_op jit(solution)/shard_map/all_to_all | solution.py:143
  162.8 15.8 %all-to-all-start.3 = ((bf16[16,16,2]{0,2,1:T(2,128)(2,1)}), bf16[16,16,2]{0,2,1:T(2,128)(2,1)S(1)}, u32[]{:S(2)}, u32[]{:S(2)}) async-start(bf16[16,16,2]{0,2,1:T(2,128)(2,1)} %bitcast.17), calls=%async_computation.3 | async-start | bytes 16384 | tf_op jit(solution)/shard_map/all_to_all | solution.py:157
  178.6 11.3 %all-to-all-start.4 = ((bf16[16,16,2,256]{3,2,0,1:T(2,128)(2,1)}), bf16[16,16,2,256]{3,2,0,1:T(2,128)(2,1)S(1)}, u32[]{:S(2)}, u32[]{:S(2)}) async-start(bf16[16,16,2,256]{3,2,0,1:T(2,128)(2,1)} %copy.196), calls=%async_computation.4 | async-start | bytes 524288 | tf_op jit(solution)/shard_map/all_to_all | solution.py:154
  191.5 1.8 copy-start.8
  193.3 14.4 %copy-start.11 = (bf16[256,256]{1,0:T(8,128)(2,1)S(1)}, bf16[256,256]{1,0:T(8,128)(2,1)}, u32[]{:S(2)}) copy-start(bf16[256,256]{1,0:T(8,128)(2,1)} %param.29) | copy-start | bytes 393220
  196.4 15.0 %copy-start.12 = (bf16[256,64]{0,1:T(8,128)(2,1)S(1)}, bf16[256,64]{0,1:T(8,128)(2,1)}, u32[]{:S(2)}) copy-start(bf16[256,64]{0,1:T(8,128)(2,1)} %param.32) | copy-start | bytes 98308
  208.3 44.7 %copy-start.14 = (s32[512]{0:T(512)S(1)}, s32[512]{0:T(512)}, u32[]{:S(2)}) copy-start(s32[512]{0:T(512)} %param.22) | copy-start | bytes 6148
  212.9 14.1 %all-to-all-start.6 = ((bf16[16,16,1024]{2,1,0:T(8,128)(2,1)}), bf16[16,16,1024]{2,1,0:T(8,128)(2,1)S(1)}, u32[]{:S(2)}, u32[]{:S(2)}) async-start(bf16[16,16,1024]{2,1,0:T(8,128)(2,1)} %broadcast_in_dim.37), calls=%async_computation.6 | async-start | bytes 1048576 | tf_op jit(solution)/shard_map/all_to_all | solution.py:28
  246.1 16.2 %all-to-all-start.8 = ((bf16[16,16,1024]{2,0,1:T(8,128)(2,1)}), bf16[16,16,1024]{2,0,1:T(8,128)(2,1)S(1)}, u32[]{:S(2)}, u32[]{:S(2)}) async-start(bf16[16,16,1024]{2,0,1:T(8,128)(2,1)} %bitcast.43), calls=%async_computation.8 | async-start | bytes 1048576 | tf_op jit(solution)/shard_map/all_to_all | solution.py:217
  252.7 88.8 %all-gather.6.cloned.1.call-start = ((), (), s32[]{:S(2)}) async-start(), calls=%async_computation.11 | async-start | bytes 4718592 | tf_op jit(solution)/shard_map/all_gather | solution.py:48
  267.1 11.4 %copy-start.4 = (bf16[32,32,128]{2,1,0:T(8,128)(2,1)S(1)}, bf16[32,32,128]{2,1,0:T(8,128)(2,1)}, u32[]{:S(2)}) copy-start(bf16[32,32,128]{2,1,0:T(8,128)(2,1)} %param.20) | copy-start | bytes 786436
  267.1 11.4 %copy-start.7 = (bf16[1024,128]{1,0:T(8,128)(2,1)S(1)}, bf16[1024,128]{1,0:T(8,128)(2,1)}, u32[]{:S(2)}) copy-start(bf16[1024,128]{1,0:T(8,128)(2,1)} %param.33) | copy-start | bytes 786436
  267.1 12.6 %copy-start.9 = (bf16[128,640]{1,0:T(8,128)(2,1)S(1)}, bf16[128,640]{1,0:T(8,128)(2,1)}, u32[]{:S(2)}) copy-start(bf16[128,640]{1,0:T(8,128)(2,1)} %param.34) | copy-start | bytes 491524
  279.3 13.0 %copy-start.2 = (f32[32,32,128]{2,1,0:T(8,128)}, f32[32,32,128]{2,1,0:T(8,128)S(1)}, u32[]{:S(2)}) copy-start(f32[32,32,128]{2,1,0:T(8,128)S(1)} %get-tuple-element.33) | copy-start | bytes 1572868
  289.6 146.2 %reduce-scatter.2.cloned.1.call-start = ((), (), s32[]{:S(2)}) async-start(), calls=%async_computation.12 | async-start | bytes 4456448 | tf_op jit(solution)/shard_map/reduce_scatter | solution.py:245
  370.1 69.8 %copy-start.17 = (bf16[128,128]{1,0:T(8,128)(2,1)S(1)}, bf16[128,128]{1,0:T(8,128)(2,1)}, u32[]{:S(2)}) copy-start(bf16[128,128]{1,0:T(8,128)(2,1)} %param.35) | copy-start | bytes 98308
  370.1 72.4 %copy-start.15 = (bf16[512,128]{1,0:T(8,128)(2,1)S(1)}, bf16[512,128]{1,0:T(8,128)(2,1)}, u32[]{:S(2)}) copy-start(bf16[512,128]{1,0:T(8,128)(2,1)} %param.37) | copy-start | bytes 393220
  370.1 72.4 %copy-start.16 = (bf16[128,512]{1,0:T(8,128)(2,1)S(1)}, bf16[128,512]{1,0:T(8,128)(2,1)}, u32[]{:S(2)}) copy-start(bf16[128,512]{1,0:T(8,128)(2,1)} %param.36) | copy-start | bytes 393220
  370.2 75.0 %copy-start.1 = (bf16[256,1024]{1,0:T(8,128)(2,1)S(1)}, bf16[256,1024]{1,0:T(8,128)(2,1)}, u32[]{:S(2)}) copy-start(bf16[256,1024]{1,0:T(8,128)(2,1)} %param.24) | copy-start | bytes 1572868
  441.3 0.8 copy-start.6
Sparse Core Ops, SparseCore 0:
  31.9 98.3 all-gather.3
  289.7 51.8 all-gather.5
  370.3 65.4 reduce-scatter.1
where the time goes:
time: 456 us; the launch traced here: 452 us
  waiting for transfers between devices  225 us (49%)
  blocking collectives  76.8 us (17%)
  local copies, waits for them, and re-layouts  61.3 us (13%)
  starting transfers between devices  30.5 us (7%)
  matrix products  29.4 us (6%)
  other arithmetic  14.6 us (3%)
  between operations  14.5 us (3%)
    all_gather x1, waiting for transfers between devices, on_device(): lax.all_gather(pair_bias, COL, axis=1, tiled=True).astype(jnp.float32)  72.2 us
    reduce_scatter x1, waiting for transfers between devices, on_device(): lax.psum_scatter(jnp.einsum('ikc,jkc->jic', tri_left, right_all, preferre...  65.6 us
    all_gather x1, waiting for transfers between devices, gather_in_order(): blocks = lax.all_gather(blocks, axes[k], axis=0, tiled=True)  49.2 us
    all_to_all x2, blocking collectives, copy_for_each(): return lax.all_to_all(copies, axis, split_axis=0, concat_axis=0, tiled=True)  33.2 us
    all_to_all x1, blocking collectives, side_by_side(): lax.all_to_all(both, axis, split_axis=split_dim, concat_axis=concat_dim,...  24.2 us
    convert_element_type x1, local copies, waits for them, and re-layouts, on_device(): outer_mean = (outer_sum / seq_total).astype(jnp.bfloat16)  11.4 us
    all_to_all x1, blocking collectives, on_device(): lax.all_to_all(gated_cols, ('branch', 'row'), split_axis=0, concat_axis=1...  10.6 us
    all_to_all x1, starting transfers between devices, on_device(): lax.all_to_all(split_mask, ('branch', 'row'), split_axis=1, concat_axis=0...  10.4 us
  transfers between devices with their start and end apart: 8, of which 8 were waited for; matrix products, arithmetic and copies ran while one was open for 2% of the time, Pallas kernels for 0%

commit v1 on v0

--- a/solution.py
+++ b/solution.py
@@ -1,8 +1,8 @@
-import math
-
 import jax
 import jax.numpy as jnp
 from jax import lax
+from jax.experimental import pallas as pl
+from jax.experimental.pallas import tpu as pltpu
 from jax.sharding import Mesh
 from jax.sharding import PartitionSpec as P
 
@@ -17,29 +17,292 @@
 NEGATIVE = -1000000000.0
 
 
-def in_order(blocks, dim):
-    dims = list(blocks.shape[1:])
-    dims[dim] *= blocks.shape[0]
-    return jnp.moveaxis(blocks, 0, dim).reshape(dims)
-
-
-def copy_for_each(x, axis):
-    copies = jnp.broadcast_to(x, (lax.axis_size(axis), *x.shape))
-    return lax.all_to_all(copies, axis, split_axis=0, concat_axis=0, tiled=True)
-
-
-def gathered_copies(x, axis, dim):
-    return in_order(copy_for_each(x, axis), dim)
-
-
-def side_by_side(arrays, axis, split_dim, concat_dim, along):
-    widths = [math.prod(a.shape[along:]) for a in arrays]
-    both = jnp.concatenate(
-        [a.reshape(*a.shape[:along], w) for a, w in zip(arrays, widths)], axis=along
-    )
-    out = lax.all_to_all(both, axis, split_axis=split_dim, concat_axis=concat_dim, tiled=True)
-    blocks = jnp.split(out, [sum(widths[:k]) for k in range(1, len(widths))], axis=along)
-    return tuple((b.reshape(*out.shape[:along], *a.shape[along:]) for a, b in zip(arrays, blocks)))
+MESH = pl.DeviceIdType.MESH
+GROUP = 16
+RING = 8
+
+
+def place():
+    axes = [lax.axis_index(a) for a in ("branch", "row", *COL)]
+    return (*axes, axes[0] * 8 + axes[1], axes[2] * 8 + axes[3])
+
+
+def across(b, c):
+    return (b // 8, lax.rem(b, 8), c // 8, lax.rem(c, 8))
+
+
+def remote(src, dst, send, recv, to):
+    return pltpu.make_async_remote_copy(
+        src_ref=src, dst_ref=dst, send_sem=send, recv_sem=recv, device_id=to, device_id_type=MESH
+    )
+
+
+def call_exchange(kernel, out_shape, scratch, collective_id, sent, *args):
+    return pl.pallas_call(
+        kernel,
+        out_shape=out_shape,
+        in_specs=[pl.BlockSpec(memory_space=pltpu.VMEM)] * len(args),
+        out_specs=jax.tree.map(lambda _: pl.BlockSpec(memory_space=pltpu.VMEM), out_shape),
+        scratch_shapes=scratch,
+        compiler_params=pltpu.CompilerParams(
+            collective_id=collective_id, has_side_effects=True, vmem_limit_bytes=48 << 20
+        ),
+        cost_estimate=pl.CostEstimate(flops=0, bytes_accessed=2 * sent, transcendentals=0),
+    )(*args)
+
+
+class Pushes:
+    def __init__(self, over, ins, outs, picks, puts, send, recv):
+        b, c = place()[4:]
+        self.me = b if over == "b" else c
+        self.device = (lambda k: across(k, c)) if over == "b" else (lambda k: across(b, k))
+        self.parts = list(zip(ins, outs, picks, puts))
+        self.send, self.recv = send, recv
+
+    def greet(self, barrier):
+        def one(d, carry):
+            pl.semaphore_signal(
+                barrier, inc=1, device_id=self.device(lax.rem(self.me + d, GROUP)), device_id_type=MESH
+            )
+            return carry
+
+        lax.fori_loop(1, GROUP, one, 0)
+
+    def copies(self, d, sender):
+        peer = lax.rem(self.me + (GROUP - d if sender else d), GROUP)
+        for k, (src, dst, pick, put) in enumerate(self.parts):
+            yield remote(
+                pick(src, self.me if sender else peer),
+                put(dst, peer if sender else self.me),
+                self.send.at[k, d],
+                self.recv.at[k, d],
+                self.device(peer),
+            )
+
+    def start(self):
+        def one(d, carry):
+            for copy in self.copies(d, False):
+                copy.start()
+            return carry
+
+        lax.fori_loop(1, GROUP, one, 0)
+        for src, dst, pick, put in self.parts:
+            put(dst, self.me)[...] = pick(src, self.me)[...]
+
+    def finish(self):
+        def one(d, carry):
+            for copy in self.copies(d, True):
+                copy.wait_recv()
+            for copy in self.copies(d, False):
+                copy.wait_send()
+            return carry
+
+        lax.fori_loop(1, GROUP, one, 0)
+
+
+def exchange(over, arrays, shapes, picks, puts, collective_id):
+    n = len(arrays)
+
+    def kernel(*refs):
+        pushes = Pushes(over, refs[:n], refs[n : 2 * n], picks, puts, refs[2 * n], refs[2 * n + 1])
+        barrier = pltpu.get_barrier_semaphore()
+        pushes.greet(barrier)
+        pl.semaphore_wait(barrier, GROUP - 1)
+        pushes.start()
+        pushes.finish()
+
+    out_shape = [jax.ShapeDtypeStruct(s, jnp.bfloat16) for s in shapes]
+    scratch = [pltpu.SemaphoreType.DMA((n, GROUP))] * 2
+    return call_exchange(kernel, out_shape, scratch, collective_id, 1 << 18, *arrays)
+
+
+def ring_gather(start, whole, own, view, twins, greeted, send, recv):
+    br, ro, x, z, _, c = place()
+    at = lambda xx, zz: xx * RING + lax.rem(zz + RING, RING)
+    right = (br, ro, x, lax.rem(z + 1, RING))
+    left = (br, ro, x, lax.rem(z + RING - 1, RING))
+    cross = (br, ro, 1 - x, z)
+    twin = (br, ro + 1 - 2 * lax.rem(ro, 2), x, z)
+    core = lax.rem(ro, 2)
+    copies, handed = [], []
+
+    def push(src, block, half, to):
+        k = len(copies)
+        copies.append(remote(src, view(whole, block, half, core), send.at[k], recv.at[k], to))
+        copies[-1].start()
+        return k
+
+    def arrived(k, block, half):
+        there = view(whole, block, half, core)
+        remote(there, there, send.at[k], recv.at[k], right).wait_recv()
+
+    def hand(block, half):
+        if twins:
+            handed.append((push(view(whole, block, half, core), block, half, twin), block, half))
+
+    mine = own(start, core)
+    k_cross = push(mine, c, None, cross)
+    going = {(0, +1): push(mine, c, None, right), (0, -1): push(mine, c, None, left)}
+    greeted()
+    there = at(1 - x, z)
+    arrived(k_cross, there, None)
+    for way, to in ((+1, right), (-1, left)):
+        going[1, way] = push(view(whole, there, None, core), there, None, to)
+    hand(there, None)
+    for step in (1, 2, 3):
+        coming = {}
+        for other in (0, 1):
+            for way, to in ((+1, right), (-1, left)):
+                block = at((1 - x) if other else x, z - way * step)
+                arrived(going[other, way], block, None)
+                half = None if step < 3 else (0 if way > 0 else 1)
+                coming[other, way] = push(view(whole, block, half, core), block, half, to)
+                hand(block, None)
+        going = coming
+    for other in (0, 1):
+        for way in (+1, -1):
+            block, half = at((1 - x) if other else x, z - way * 4), 0 if way > 0 else 1
+            arrived(going[other, way], block, half)
+            hand(block, half)
+    for k, block, half in handed:
+        there = view(whole, block, half, 1 - core)
+        remote(there, there, send.at[k], recv.at[k], twin).wait_recv()
+    for copy in copies:
+        copy.wait_send()
+
+
+def ring_copies(twins):
+    return 19 + (17 if twins else 0)
+
+
+def greet_ring(barrier, twins, cross_and_ring):
+    br, ro, x, z, _, _ = place()
+    to = []
+    if cross_and_ring:
+        to += [
+            (br, ro, x, lax.rem(z + 1, RING)),
+            (br, ro, x, lax.rem(z + RING - 1, RING)),
+            (br, ro, 1 - x, z),
+        ]
+    if twins:
+        to.append((br, ro + 1 - 2 * lax.rem(ro, 2), x, z))
+    for device in to:
+        pl.semaphore_signal(barrier, inc=1, device_id=device, device_id_type=MESH)
+    return len(to)
+
+
+def gather_bias_and_rows(bias, rows, mask):
+    heads, some, all_ = bias.shape
+    half_heads = heads // 2
+
+    def own(ref, core):
+        return ref.at[pl.ds(core * half_heads, half_heads)]
+
+    def view(ref, block, half, core):
+        first, count = core * half_heads, half_heads
+        if half is not None:
+            count = half_heads // 2
+            first = first + half * count
+        return ref.at[pl.ds(first, count), pl.ds(pl.multiple_of(block * some, some), some)]
+
+    picks = [lambda ref, k: ref.at[k]] * 2
+    puts = [
+        lambda ref, k: ref.at[pl.ds(pl.multiple_of(k * some, some), some)],
+        lambda ref, k: ref.at[k],
+    ]
+
+    def kernel(b_ref, r_ref, m_ref, ob_ref, or_ref, om_ref, psend, precv, rsend, rrecv):
+        pushes = Pushes("c", (r_ref, m_ref), (or_ref, om_ref), picks, puts, psend, precv)
+        barrier = pltpu.get_barrier_semaphore()
+        pushes.greet(barrier)
+        more = greet_ring(barrier, True, False)
+        pl.semaphore_wait(barrier, GROUP - 1 + more)
+        c = place()[5]
+
+        def meanwhile():
+            pushes.start()
+            ob_ref[:, pl.ds(pl.multiple_of(c * some, some), some)] = b_ref[...]
+
+        ring_gather(b_ref, ob_ref, own, view, True, meanwhile, rsend, rrecv)
+        pushes.finish()
+
+    out_shape = [
+        jax.ShapeDtypeStruct((heads, GROUP * some, all_), jnp.bfloat16),
+        jax.ShapeDtypeStruct((GROUP * some, rows.shape[2]), jnp.bfloat16),
+        jax.ShapeDtypeStruct(mask.shape, jnp.bfloat16),
+    ]
+    scratch = [pltpu.SemaphoreType.DMA((2, GROUP))] * 2
+    scratch += [pltpu.SemaphoreType.DMA((ring_copies(True),))] * 2
+    return call_exchange(kernel, out_shape, scratch, 1, 4 << 20, bias, rows, mask)
+
+
+def gather_factors(left, right):
+    rows = left.shape[0]
+
+    def kernel(l_ref, r_ref, ol_ref, or_ref, lsend, lrecv, rsend, rrecv):
+        put = lambda ref, k: ref.at[pl.ds(pl.multiple_of(k * rows, rows), rows)]
+        b, c = place()[4:]
+        pushes = Pushes("b", (l_ref,), (ol_ref,), [lambda ref, k: ref], [put], lsend, lrecv)
+        barrier = pltpu.get_barrier_semaphore()
+        pushes.greet(barrier)
+
+        def others(act):
+            def one(d, carry):
+                k = lax.rem(c + d, GROUP)
+
+                @pl.when(jnp.logical_or(b != c, k != c))
+                def _():
+                    act(k)
+
+                return carry
+
+            lax.fori_loop(0, GROUP, one, 0)
+
+        def senders(act):
+            def one(d, carry):
+                k = lax.rem(b + d, GROUP)
+
+                @pl.when(jnp.logical_or(b != c, k != b))
+                def _():
+                    act(k)
+
+                return carry
+
+            lax.fori_loop(0, GROUP, one, 0)
+
+        others(
+            lambda k: pl.semaphore_signal(
+                barrier, inc=1, device_id=across(c, k), device_id_type=MESH
+            )
+        )
+        senders(
+            lambda k: pl.semaphore_signal(
+                barrier, inc=1, device_id=across(k, b), device_id_type=MESH
+            )
+        )
+        pl.semaphore_wait(barrier, GROUP - 1 + 2 * jnp.where(b == c, GROUP - 1, GROUP))
+
+        def copy(k):
+            return remote(r_ref, put(or_ref, b), rsend.at[k], rrecv.at[b], across(c, k))
+
+        def coming(k):
+            there = put(or_ref, k)
+            return remote(r_ref, there, rsend.at[k], rrecv.at[k], across(k, b))
+
+        others(lambda k: copy(k).start())
+        pushes.start()
+
+        @pl.when(b == c)
+        def _():
+            put(or_ref, b)[...] = r_ref[...]
+
+        pushes.finish()
+        senders(lambda k: coming(k).wait_recv())
+        others(lambda k: copy(k).wait_send())
+
+    shape = jax.ShapeDtypeStruct((GROUP * rows, left.shape[1]), jnp.bfloat16)
+    scratch = [pltpu.SemaphoreType.DMA((1, GROUP))] * 2 + [pltpu.SemaphoreType.DMA((GROUP,))] * 2
+    return call_exchange(kernel, [shape, shape], scratch, 6, 1 << 20, left, right)
 
 
 def gather_in_order(x, axes, turns):
@@ -53,7 +316,10 @@
 
 
 def gathered_by_axis(x, axes, turns, dim):
-    return in_order(gather_in_order(x, axes, turns), dim)
+    blocks = gather_in_order(x, axes, turns)
+    dims = list(blocks.shape[1:])
+    dims[dim] *= blocks.shape[0]
+    return jnp.moveaxis(blocks, 0, dim).reshape(dims)
 
 
 def layer_normalize(tensor):
@@ -107,16 +373,46 @@
     keep_there = lax.dynamic_slice_in_dim(residue_keep, col_place * pair_cols, pair_cols)
     pair_normed = layer_normalize(pair_representation).astype(jnp.bfloat16)
     same_chain = (chain_here[:, None] == chain_there[None, :]).astype(jnp.float32)
-    bias_terms = (
-        jnp.dot(pair_normed, pair_bias_matrix, preferred_element_type=jnp.float32)
-        + same_chain_bias[None, None, :] * same_chain[:, :, None]
-    )
-    bias_tile = jnp.transpose(bias_terms, (2, 0, 1)).astype(jnp.bfloat16)
-    pair_bias = gathered_copies(bias_tile, ("branch", "row"), 2)
+    weights = lax.dot_general(
+        pair_bias_matrix,
+        pair_normed.reshape(residue_total * pair_cols, -1),
+        (((0,), (1,)), ((), ())),
+        preferred_element_type=jnp.float32,
+    )
+    bias_tile = (
+        weights + same_chain_bias[:, None] * same_chain.reshape(1, residue_total * pair_cols)
+    ).astype(jnp.bfloat16)
+    group_count = GROUP
+    residue_piece = residue_total // group_count
     key_presence_mask = alignment_entry_mask.astype(jnp.bfloat16)
+    row_presence = jnp.pad(key_presence_mask[:, None, :], ((0, 0), (0, 7), (0, 96)))
+    col_presence = jnp.transpose(
+        key_presence_mask.reshape(device_local_rows, group_count, residue_piece), (1, 2, 0)
+    )
+    col_presence = jnp.pad(
+        col_presence, ((0, 0), (0, 8 - residue_piece), (0, 128 - device_local_rows))
+    )
+    bias_blocks, mask_cols = exchange(
+        "b",
+        (bias_tile, col_presence),
+        ((GROUP, *bias_tile.shape), col_presence.shape),
+        [lambda ref, k: ref, lambda ref, k: ref.at[k]],
+        [lambda ref, k: ref.at[k]] * 2,
+        0,
+    )
+    pair_bias = jnp.transpose(
+        bias_blocks.reshape(GROUP, HEADS, residue_total, pair_cols), (1, 2, 0, 3)
+    ).reshape(HEADS, residue_total, GROUP * pair_cols)
+    mask_cols = jnp.transpose(
+        mask_cols[:, :residue_piece, :device_local_rows], (1, 0, 2)
+    ).reshape(residue_piece, GROUP * device_local_rows)
     row_normed_input = layer_normalize(homolog_embedding).astype(jnp.bfloat16)
-    normed_whole, mask_whole = side_by_side((row_normed_input, key_presence_mask), COL, 0, 1, 2)
-    full_bias = lax.all_gather(pair_bias, COL, axis=1, tiled=True).astype(jnp.float32)
+    full_bias, normed_whole, mask_whole = gather_bias_and_rows(
+        pair_bias, row_normed_input, row_presence
+    )
+    normed_whole = normed_whole[None]
+    mask_whole = mask_whole[:, 0, :residue_total].reshape(1, GROUP * residue_total)
+    full_bias = full_bias.astype(jnp.float32)
     few_rows, all_residues = mask_whole.shape
     queries, key_rows, value_rows, gating = split_blocks(normed_whole, row_projection_weights)
     query_heads = queries.reshape(few_rows, all_residues, HEADS, PER_HEAD_WIDTH)
@@ -140,53 +436,63 @@
         few_rows, all_residues, channel_count
     )
     gated_whole = (attended * gating).astype(jnp.bfloat16)
-    row_gated = lax.all_to_all(gated_whole, COL, split_axis=1, concat_axis=0, tiled=True)
+    (row_gated,) = exchange(
+        "c",
+        (gated_whole[0],),
+        ((GROUP, residue_total, channel_count),),
+        [lambda ref, k: ref.at[pl.ds(pl.multiple_of(k * residue_total, residue_total), residue_total)]],
+        [lambda ref, k: ref.at[k]],
+        2,
+    )
     alignment_row_state = homolog_embedding.astype(jnp.float32) + jnp.dot(
         row_gated, horizontal_attend_merge, preferred_element_type=jnp.float32
     )
     column_normed_input = layer_normalize(alignment_row_state).astype(jnp.bfloat16)
-    group_count = lax.axis_size(("branch", "row"))
-    residue_piece = residue_total // group_count
-    split_input = column_normed_input.reshape(
-        device_local_rows, group_count, residue_piece, channel_count
-    )
-    split_mask = key_presence_mask.reshape(device_local_rows, group_count, residue_piece)
-    normed_cols = lax.all_to_all(
-        split_input, ("branch", "row"), split_axis=1, concat_axis=0, tiled=True
-    )
-    mask_cols = lax.all_to_all(
-        split_mask, ("branch", "row"), split_axis=1, concat_axis=0, tiled=True
-    )
-    total_rows = normed_cols.shape[0]
-    residue_count = normed_cols.shape[2]
-    normed_flat = normed_cols.reshape(total_rows, residue_count, channel_count)
-    mask_flat = mask_cols.reshape(total_rows, residue_count)
+    split_input = jnp.transpose(column_normed_input, (1, 0, 2))
+    rows_of = lambda ref, k: ref.at[
+        :, pl.ds(pl.multiple_of(k * device_local_rows, device_local_rows), device_local_rows)
+    ]
+    residues_of = lambda ref, k: ref.at[pl.ds(k * residue_piece, residue_piece)]
+    (normed_cols,) = exchange(
+        "b",
+        (split_input,),
+        ((residue_piece, GROUP * device_local_rows, channel_count),),
+        [residues_of],
+        [rows_of],
+        3,
+    )
+    residue_count, total_rows = mask_cols.shape
+    normed_flat = normed_cols
     col_queries, col_keys, col_values, col_gating = split_blocks(
         normed_flat, column_projection_weights
     )
-    query_part = col_queries.reshape(total_rows, residue_count, HEADS, PER_HEAD_WIDTH)
-    key_part = col_keys.reshape(total_rows, residue_count, HEADS, PER_HEAD_WIDTH)
-    value_part = col_values.reshape(total_rows, residue_count, HEADS, PER_HEAD_WIDTH)
-    scores = jnp.einsum("sihd,tihd->ihst", query_part, key_part, preferred_element_type=jnp.float32)
-    scores = jnp.where(jnp.transpose(mask_flat)[:, None, None, :] > 0, scores, NEGATIVE)
+    query_part = col_queries.reshape(residue_count, total_rows, HEADS, PER_HEAD_WIDTH)
+    key_part = col_keys.reshape(residue_count, total_rows, HEADS, PER_HEAD_WIDTH)
+    value_part = col_values.reshape(residue_count, total_rows, HEADS, PER_HEAD_WIDTH)
+    scores = jnp.einsum("ishd,ithd->ihst", query_part, key_part, preferred_element_type=jnp.float32)
+    scores = jnp.where(mask_cols[:, None, None, :] > 0, scores, NEGATIVE)
     highest = jnp.max(scores, axis=-1, keepdims=True)
     powers = jnp.exp(scores - highest)
     totals = jnp.sum(powers, axis=-1)
     summed = jnp.einsum(
-        "ihst,tihd->ihsd",
+        "ihst,ithd->ihsd",
         powers.astype(jnp.bfloat16),
         value_part,
         preferred_element_type=jnp.float32,
     )
-    attended = jnp.transpose(summed / totals[..., None], (2, 0, 1, 3)).reshape(
-        total_rows, residue_count, channel_count
+    attended = jnp.transpose(summed / totals[..., None], (0, 2, 1, 3)).reshape(
+        residue_count, total_rows, channel_count
     )
     gated = (attended * col_gating).astype(jnp.bfloat16)
-    gated_cols = gated.reshape(total_rows, 1, residue_count, channel_count)
-    returned = lax.all_to_all(
-        gated_cols, ("branch", "row"), split_axis=0, concat_axis=1, tiled=True
-    )
-    column_gated_output = returned.reshape(device_local_rows, residue_total, channel_count)
+    (returned,) = exchange(
+        "b",
+        (gated,),
+        ((residue_total, device_local_rows, channel_count),),
+        [rows_of],
+        [residues_of],
+        4,
+    )
+    column_gated_output = jnp.transpose(returned, (1, 0, 2))
     alignment_column_state = alignment_row_state + jnp.dot(
         column_gated_output, vertical_attend_merge, preferred_element_type=jnp.float32
     )
@@ -212,11 +518,7 @@
         .astype(jnp.bfloat16)
         .reshape(device_local_rows, residue_total * PRODUCT_FEATURES)
     )
-    left_all = gathered_copies(left_factor, ("branch", "row"), 0)
-    right_cols = gathered_copies(right_factor, COL, 1)
-    right_rows = lax.all_to_all(
-        right_cols, ("branch", "row"), split_axis=1, concat_axis=0, tiled=True
-    )
+    left_all, right_rows = gather_factors(left_factor, right_factor)
     seq_total = left_all.shape[0]
     outer_sum = lax.dot_general(
         left_all, right_rows, (((0,), (0,)), ((), ())), preferred_element_type=jnp.float32

time: 456 us -> 363 us (0.80)
  waiting for transfers between devices: 225 us -> 115 us
  Pallas kernels: 0 us -> 107 us
  blocking collectives: 76.8 us -> 8.88 us
  starting transfers between devices: 30.5 us -> 0.08 us
  local copies, waits for them, and re-layouts: 61.3 us -> 69.4 us
    pallas_call x0 -> x6, Pallas kernels: none -> 107 us  [call_exchange(): pl.pallas_call(kernel, out_shape=out_shape, in_specs=[pl.BlockSpec(memory...]
    all_gather x1 -> x0, waiting for transfers between devices: 72.2 us -> none  [on_device(): lax.all_gather(pair_bias, COL, axis=1, tiled=True).astype(jnp.float32)]
    all_to_all x4 -> x0, blocking collectives: 67.9 us -> none  [the longest x2 33.2 us: copy_for_each(): return lax.all_to_all(copies, axis, split_axis=0, concat_axis=0, tiled=True)]
    all_to_all x5 -> x0, waiting for transfers between devices: 37.5 us -> none  [the longest x1 9.58 us: copy_for_each(): return lax.all_to_all(copies, axis, split_axis=0, concat_axis=0, tiled=True)]
    all_to_all x5 -> x0, starting transfers between devices: 29.8 us -> none  [the longest x1 10.4 us: on_device(): lax.all_to_all(split_mask, ('branch', 'row'), split_axis=1, concat_axis=0...]
    convert_element_type x1 -> x3, local copies, waits for them, and re-layouts: 11.4 us -> 29.8 us  [on_device(): outer_mean = (outer_sum / seq_total).astype(jnp.bfloat16)]
    all_gather x1 -> x0, local copies, waits for them, and re-layouts: 7.6 us -> none  [on_device(): lax.all_gather(pair_bias, COL, axis=1, tiled=True).astype(jnp.float32)]
  transfers between devices with their start and end apart: 8 -> 2, of which waited for: 8 -> 2; matrix products, arithmetic and copies ran while one was open for 2% -> 1% of each run, Pallas kernels for 0% -> 0%
where the time goes in v1:
time: 363 us; the launch traced here: 360 us
  waiting for transfers between devices  115 us (32%)
  Pallas kernels  107 us (29%)
  local copies, waits for them, and re-layouts  69.4 us (19%)
  matrix products  27 us (7%)
  other arithmetic  17.9 us (5%)
  between operations  14.7 us (4%)
  blocking collectives  8.88 us (2%)
    pallas_call x6, Pallas kernels, call_exchange(): pl.pallas_call(kernel, out_shape=out_shape, in_specs=[pl.BlockSpec(memory...  107 us
    reduce_scatter x1, waiting for transfers between devices, on_device(): lax.psum_scatter(jnp.einsum('ikc,jkc->jic', tri_left, right_all, preferre...  63.7 us
    all_gather x1, waiting for transfers between devices, gather_in_order(): blocks = lax.all_gather(blocks, axes[k], axis=0, tiled=True)  51.1 us
    convert_element_type x3, local copies, waits for them, and re-layouts, on_device(): outer_mean = (outer_sum / seq_total).astype(jnp.bfloat16)  29.8 us
    convert_element_type x1, local copies, waits for them, and re-layouts, on_device(): jnp.einsum('ikc,jkc->jic', tri_left, right_all, preferred_element_type=jn...  9.13 us
    all_gather x1, blocking collectives, gather_in_order(): blocks = lax.all_gather(blocks, axes[k], axis=0, tiled=True)  8.88 us
    another operation x1, local copies, waits for them, and re-layouts, gathered_by_axis(): return jnp.moveaxis(blocks, 0, dim).reshape(dims)  8.64 us
  transfers between devices with their start and end apart: 2, of which 2 were waited for; matrix products, arithmetic and copies ran while one was open for 1% of the time, Pallas kernels for 0%

profile of v1, /device:TPU:1, one launch (start us, length us, event | category | flops | bytes accessed | tf_op | source)
XLA Modules:
  0.0 359.8 jit_solution(15721181034811574477)
XLA Ops:
  7.2 1.2 convert_reduce_fusion
  8.5 1.3 fusion.37
  9.8 1.3 fusion.38
  13.9 11.3 %shard_map.194 = (bf16[16,8,1024]{2,1,0:T(8,128)(2,1)S(1)}, bf16[16,8,128]{2,1,0:T(8,128)(2,1)S(1)}) custom-call(bf16[8,1024]{1,0:T(8,128)(2,1)S(1)} %fusion.24.refs_0_, bf16[16,8,128]{2,1,0:T(8,128)(2,1)S(1)} %pad.8.refs_1_), custom_call_target="tpu_custom_call" | custom-call | bytes 524288 | tf_op jit(solution)/shard_map/pallas_call | solution.py:41
  28.6 40.9 %shard_map.195 = (bf16[8,512,512]{2,1,0:T(8,128)(2,1)S(1)}, bf16[512,256]{1,0:T(8,128)(2,1)S(1)}, bf16[16,8,128]{2,1,0:T(8,128)(2,1)S(1)}) custom-call(bf16[8,32,512]{2,1,0:T(8,128)(2,1)S(1)} %reshape.254.b_ref, bf16[16,32,256]{2,1,0:T(8,128)(2,1)S(1)} %copy.207.r_ref, bf16[16,8,128]{2,1,0:T(8,128)(2,1)S(1)} %pad.9.m_ref), custom_call_target="tpu_custom_call" | custom-call | bytes 8388608 | tf_op jit(solution)/shard_map/pallas_call | solution.py:41
  69.5 1.9 copy-done.2
  74.2 3.9 %fusion.106 = (f32[8,512]{1,0:T(8,128)S(1)}, f32[8,512,512]{2,1,0:T(8,128)S(1)}) fusion(bf16[8,512,512]{2,1,0:T(8,128)(2,1)} %copy-done.2, bf16[512,8,32]{0,2,1:T(8,128)(2,1)S(1)} %bitcast.143, bf16[512,8,32]{0,2,1:T(8,128)(2,1)S(1)} %bitcast.144, pred[512]{0:T(512)(128)(4,1)S(1)} %gt.33), kind=kOutput, calls=%fused_computation.155 | convolution fusion | flops 142602240 | bytes 13124096 | tf_op jit(solution)/shard_map/sihd,sjhd->shij/dot_general | solution.py:422
  78.1 2.1 fusion
  80.2 2.4 fusion.30
  83.6 1.2 fusion.88.refs_0_
  84.8 11.7 %shard_map.196 = bf16[16,32,256]{2,1,0:T(8,128)(2,1)S(1)} custom-call(bf16[512,256]{1,0:T(8,128)(2,1)S(1)} %fusion.88.refs_0_), custom_call_target="tpu_custom_call" | custom-call | bytes 524288 | tf_op jit(solution)/shard_map/pallas_call | solution.py:41
  97.3 9.3 %shard_map.197 = bf16[2,256,256]{2,1,0:T(8,128)(2,1)S(1)} custom-call(bf16[32,16,256]{2,1,0:T(8,128)(2,1)S(1)} %fusion.74.refs_0_), custom_call_target="tpu_custom_call" | custom-call | bytes 524288 | tf_op jit(solution)/shard_map/pallas_call | solution.py:41
  106.7 1.5 fusion.108
  114.4 8.5 %shard_map.198 = bf16[32,16,256]{2,1,0:T(8,128)(2,1)S(1)} custom-call(bf16[2,256,256]{2,1,0:T(8,128)(2,1)S(1)} %fusion.73.refs_0_), custom_call_target="tpu_custom_call" | custom-call | bytes 524288 | tf_op jit(solution)/shard_map/pallas_call | solution.py:41
  123.8 1.5 maximum_convert_fusion.1
  125.3 1.8 fusion.110
  128.9 25.2 %shard_map.199 = (bf16[256,1024]{1,0:T(8,128)(2,1)S(1)}, bf16[256,1024]{1,0:T(8,128)(2,1)S(1)}) custom-call(bf16[16,1024]{1,0:T(8,128)(2,1)S(1)} %reshape.263.l_ref, bf16[16,1024]{1,0:T(8,128)(2,1)S(1)} %reshape.264.r_ref), custom_call_target="tpu_custom_call" | custom-call | bytes 2097152 | tf_op jit(solution)/shard_map/pallas_call | solution.py:41
  154.9 7.9 %convert_element_type.145 = bf16[32,32,32,32]{3,2,1,0:T(8,128)(2,1)} reshape(bf16[1024,1024]{1,0:T(8,128)(2,1)S(1)} %multiply_convert_fusion) | data formatting | bytes 4194304 | tf_op jit(solution)/shard_map/convert_element_type | solution.py:530
  162.8 10.5 %copy.225 = bf16[32,32,32,32]{3,2,1,0:T(8,128)(2,1)} copy(bf16[32,32,32,32]{3,1,2,0:T(8,128)(2,1)} %bitcast.136) | data formatting | bytes 4194304 | tf_op jit(solution)/shard_map/convert_element_type | solution.py:530
  173.3 11.4 %convert_element_type.147 = bf16[32,32,1024]{2,1,0:T(8,128)(2,1)S(1)} reshape(bf16[32,32,32,32]{3,2,1,0:T(8,128)(2,1)} %copy.225) | data formatting | bytes 4194304 | tf_op jit(solution)/shard_map/convert_element_type | solution.py:530
  187.0 8.9 %all-gather = bf16[64,32,128]{2,1,0:T(8,128)(2,1)} all-gather(bf16[32,32,128]{2,1,0:T(8,128)(2,1)S(1)} %get-tuple-element.30), channel_id=2, replica_groups=mesh['branch'=2,'row'=8,'col_0'=2,'col_1'=8] {'col_0'}, dimensions={0}, use_global_device_ids=true | all-gather | bytes 786432 | tf_op jit(solution)/shard_map/all_gather | solution.py:311
  196.0 2.4 copy.228
  198.4 51.1 %all-gather.3.cloned.1.call-done = bf16[16,32,32,128]{3,2,1,0:T(8,128)(2,1)} async-done(((bf16[2,32,32,128]{3,2,1,0:T(8,128)(2,1)}), bf16[16,32,32,128]{3,2,1,0:T(8,128)(2,1)}) %all-gather.3.cloned.1.call-update) | async-done | bytes 4194320 | tf_op jit(solution)/shard_map/all_gather | solution.py:311
  249.4 5.1 %copy.226 = bf16[2,8,32,32,128]{4,3,2,1,0:T(8,128)(2,1)} copy(bf16[2,8,32,32,128]{4,3,2,0,1:T(8,128)(2,1)} %bitcast.139) | data formatting | bytes 8388608 | tf_op jit(solution)/shard_map/transpose | solution.py:315
  254.5 8.6 %copy.227 = bf16[512,32,128]{0,1,2:T(8,128)(2,1)} copy(bf16[512,32,128]{2,1,0:T(8,128)(2,1)} %bitcast.137) | data formatting | bytes 8388608 | tf_op jit(solution)/shard_map/reshape;reshape | solution.py:322
  263.2 5.7 %convert_bitcast_fusion = bf16[512,32,128]{0,1,2:T(8,128)(2,1)} fusion(bf16[32,32,128]{1,0,2:T(8,128)(2,1)} %copy.228, bf16[512,32,128]{0,1,2:T(8,128)(2,1)} %copy.227), kind=kOutput, calls=%fused_computation.5 | convolution fusion | flops 136314880 | bytes 8650752 | tf_op jit(solution)/shard_map/ikc,jkc->jic/dot_general | solution.py:548
  268.9 9.1 %copy.229 = bf16[512,32,128]{2,1,0:T(8,128)(2,1)} copy(bf16[512,32,128]{0,1,2:T(8,128)(2,1)} %convert_bitcast_fusion) | data formatting | bytes 8388608 | tf_op jit(solution)/shard_map/convert_element_type | solution.py:548
  279.7 63.7 %reduce-scatter.2.cloned.1.call-done = bf16[32,32,128]{2,1,0:T(8,128)(2,1)} async-done(((bf16[512,32,128]{2,1,0:T(8,128)(2,1)}), bf16[32,32,128]{2,1,0:T(8,128)(2,1)}) %reduce-scatter.2.cloned.1.call-update) | async-done | bytes 262160 | tf_op jit(solution)/shard_map/reduce_scatter | solution.py:547
  344.8 1.3 fusion.66
  346.3 1.3 fusion.67
  347.6 1.4 fusion.112
  350.3 2.7 fusion.21
  (118 shorter events, 26.8 us)
Async XLA Ops:
  7.2 64.2 %copy-start = (bf16[256,1024]{1,0:T(8,128)(2,1)S(1)}, bf16[256,1024]{1,0:T(8,128)(2,1)}, u32[]{:S(2)}) copy-start(bf16[256,1024]{1,0:T(8,128)(2,1)} %param.24) | copy-start | bytes 1572868
  7.2 20.5 %copy-start.5 = (bf16[16,32,256]{2,1,0:T(8,128)(2,1)S(1)}, bf16[16,32,256]{2,1,0:T(8,128)(2,1)}, u32[]{:S(2)}) copy-start(bf16[16,32,256]{2,1,0:T(8,128)(2,1)} %param.19) | copy-start | bytes 786436
  7.2 242.2 %all-gather.3.cloned.1.call-start = ((), (), s32[]{:S(2)}) async-start(), calls=%async_computation.1 | async-start | bytes 4718592 | tf_op jit(solution)/shard_map/all_gather | solution.py:311
  69.5 1.9 copy-start.2
  80.2 16.3 %copy-start.11 = (bf16[256,256]{1,0:T(8,128)(2,1)S(1)}, bf16[256,256]{1,0:T(8,128)(2,1)}, u32[]{:S(2)}) copy-start(bf16[256,256]{1,0:T(8,128)(2,1)} %param.25) | copy-start | bytes 393220
  109.5 1.8 copy-start.9
  111.3 11.7 %copy-start.12 = (bf16[256,256]{1,0:T(8,128)(2,1)S(1)}, bf16[256,256]{1,0:T(8,128)(2,1)}, u32[]{:S(2)}) copy-start(bf16[256,256]{1,0:T(8,128)(2,1)} %param.29) | copy-start | bytes 393220
  123.0 5.3 %copy-start.16 = (bf16[256,64]{0,1:T(8,128)(2,1)S(1)}, bf16[256,64]{0,1:T(8,128)(2,1)}, u32[]{:S(2)}) copy-start(bf16[256,64]{0,1:T(8,128)(2,1)} %param.32) | copy-start | bytes 98308
  173.3 11.4 %copy-start.4 = (bf16[32,32,128]{2,1,0:T(8,128)(2,1)S(1)}, bf16[32,32,128]{2,1,0:T(8,128)(2,1)}, u32[]{:S(2)}) copy-start(bf16[32,32,128]{2,1,0:T(8,128)(2,1)} %param.20) | copy-start | bytes 786436
  173.3 11.4 %copy-start.8 = (bf16[1024,128]{1,0:T(8,128)(2,1)S(1)}, bf16[1024,128]{1,0:T(8,128)(2,1)}, u32[]{:S(2)}) copy-start(bf16[1024,128]{1,0:T(8,128)(2,1)} %param.33) | copy-start | bytes 786436
  173.3 12.6 %copy-start.13 = (s32[512]{0:T(512)S(1)}, s32[512]{0:T(512)}, u32[]{:S(2)}) copy-start(s32[512]{0:T(512)} %param.22) | copy-start | bytes 6148
  173.3 12.7 %copy-start.10 = (bf16[128,640]{1,0:T(8,128)(2,1)S(1)}, bf16[128,640]{1,0:T(8,128)(2,1)}, u32[]{:S(2)}) copy-start(bf16[128,640]{1,0:T(8,128)(2,1)} %param.34) | copy-start | bytes 491524
  185.5 12.9 %copy-start.3 = (f32[32,32,128]{2,1,0:T(8,128)}, f32[32,32,128]{2,1,0:T(8,128)S(1)}, u32[]{:S(2)}) copy-start(f32[32,32,128]{2,1,0:T(8,128)S(1)} %get-tuple-element.61) | copy-start | bytes 1572868
  195.9 147.6 %reduce-scatter.2.cloned.1.call-start = ((), (), s32[]{:S(2)}) async-start(), calls=%async_computation.2 | async-start | bytes 4456448 | tf_op jit(solution)/shard_map/reduce_scatter | solution.py:547
  278.0 0.9 copy-start.6
  278.0 72.2 %copy-start.14 = (bf16[512,128]{1,0:T(8,128)(2,1)S(1)}, bf16[512,128]{1,0:T(8,128)(2,1)}, u32[]{:S(2)}) copy-start(bf16[512,128]{1,0:T(8,128)(2,1)} %param.37) | copy-start | bytes 393220
  278.0 74.9 %copy-start.1 = (bf16[256,1024]{1,0:T(8,128)(2,1)S(1)}, bf16[256,1024]{1,0:T(8,128)(2,1)}, u32[]{:S(2)}) copy-start(bf16[256,1024]{1,0:T(8,128)(2,1)} %param.24) | copy-start | bytes 1572868
  279.7 70.5 %copy-start.15 = (bf16[128,512]{1,0:T(8,128)(2,1)S(1)}, bf16[128,512]{1,0:T(8,128)(2,1)}, u32[]{:S(2)}) copy-start(bf16[128,512]{1,0:T(8,128)(2,1)} %param.36) | copy-start | bytes 393220
  349.1 0.8 copy-start.7
Sparse Core Ops, SparseCore 0:
  196.1 53.3 all-gather.2
  278.2 65.2 reduce-scatter.1

commit v2 on v1

--- a/solution.py
+++ b/solution.py
@@ -305,21 +305,132 @@
     return call_exchange(kernel, [shape, shape], scratch, 6, 1 << 20, left, right)
 
 
-def gather_in_order(x, axes, turns):
-    blocks = x[None]
-    for k in turns:
-        blocks = lax.all_gather(blocks, axes[k], axis=0, tiled=True)
-    carried = [lax.axis_size(axes[k]) for k in reversed(turns)]
-    blocks = blocks.reshape(*carried, *x.shape)
-    turned = sorted(range(len(turns)), key=lambda place: turns[len(turns) - 1 - place])
-    return blocks.transpose(*turned, *range(len(turns), blocks.ndim)).reshape(-1, *x.shape)
-
-
-def gathered_by_axis(x, axes, turns, dim):
-    blocks = gather_in_order(x, axes, turns)
-    dims = list(blocks.shape[1:])
-    dims[dim] *= blocks.shape[0]
-    return jnp.moveaxis(blocks, 0, dim).reshape(dims)
+def norm_channels(x):
+    centre = x - jnp.mean(x, axis=0, keepdims=True)
+    spread = jnp.mean(centre * centre, axis=0, keepdims=True)
+    return centre * lax.rsqrt(spread + EPSILON)
+
+
+def pair_front(left, right, pair, mix, weights, keep):
+    rows, wide = left.shape
+    channels = pair.shape[0]
+    lanes = 128
+    per = lanes // PRODUCT_FEATURES
+    some = 8
+    chunk = some * PRODUCT_FEATURES
+    count = wide // chunk
+    groups = channels // 8
+
+    def kernel(l_ref, r_ref, p_ref, m_ref, w_ref, k_ref, opm_ref, tl_ref, tr_ref, gate_ref):
+        lane = lax.broadcasted_iota(jnp.int32, (channels, lanes), 1) // PRODUCT_FEATURES
+
+        def one(g, carry):
+            cols = pl.ds(pl.multiple_of(g * chunk, chunk), chunk)
+            outer = lax.dot_general(
+                l_ref[:, cols], r_ref[...], (((0,), (0,)), ((), ())), preferred_element_type=jnp.float32
+            )
+            outer = (outer * (1.0 / rows)).astype(jnp.bfloat16)
+            stacked = jnp.concatenate(
+                [
+                    jnp.concatenate(
+                        [
+                            outer[
+                                i * PRODUCT_FEATURES : (i + 1) * PRODUCT_FEATURES,
+                                q * lanes : (q + 1) * lanes,
+                            ]
+                            for q in range(wide // lanes)
+                        ],
+                        axis=0,
+                    )
+                    for i in range(some)
+                ],
+                axis=1,
+            )
+            mixed = lax.dot_general(
+                m_ref[...], stacked, (((0,), (0,)), ((), ())), preferred_element_type=jnp.float32
+            )
+            pieces = []
+            for h in range(some // per):
+                piece = jnp.zeros((channels, lanes), jnp.float32)
+                for i in range(per):
+                    at = (h * per + i) * lanes
+                    total = None
+                    for y in range(per):
+                        part = mixed[y * channels : (y + 1) * channels, at : at + lanes]
+                        shift = (PRODUCT_FEATURES * (i - y)) % lanes
+                        part = pltpu.roll(part, shift, 1) if shift else part
+                        total = part if total is None else total + part
+                    piece = jnp.where(lane == i, total, piece)
+                pieces.append(piece)
+            opm = p_ref[:, cols].astype(jnp.float32) + jnp.concatenate(pieces, axis=1)
+            opm_ref[:, cols] = opm
+            normed = norm_channels(opm).astype(jnp.bfloat16)
+            projected = lax.dot_general(
+                w_ref[...], normed, (((0,), (0,)), ((), ())), preferred_element_type=jnp.float32
+            )
+            block = lambda k: projected[k * channels : (k + 1) * channels]
+            here = k_ref[:, cols]
+            tri_left = (here * jax.nn.sigmoid(block(0)) * block(1)).astype(jnp.bfloat16)
+            tri_right = (here * jax.nn.sigmoid(block(2)) * block(3)).astype(jnp.bfloat16)
+            tl_ref[:, :, cols] = tri_left.reshape(groups, 8, chunk)
+            tr_ref[:, :, cols] = tri_right.reshape(groups, 8, chunk)
+            gate_ref[:, cols] = jax.nn.sigmoid(block(4))
+            return carry
+
+        lax.fori_loop(0, count, one, 0)
+
+    tokens = pair.shape[1]
+    return pl.pallas_call(
+        kernel,
+        out_shape=[
+            jax.ShapeDtypeStruct((channels, tokens), jnp.float32),
+            jax.ShapeDtypeStruct((groups, 8, tokens), jnp.bfloat16),
+            jax.ShapeDtypeStruct((groups, 8, tokens), jnp.bfloat16),
+            jax.ShapeDtypeStruct((channels, tokens), jnp.float32),
+        ],
+        in_specs=[pl.BlockSpec(memory_space=pltpu.VMEM)] * 6,
+        out_specs=[pl.BlockSpec(memory_space=pltpu.VMEM)] * 4,
+        compiler_params=pltpu.CompilerParams(vmem_limit_bytes=40 << 20),
+    )(left, right, pair, mix, weights, keep)
+
+
+def triangle(tri_left, tri_right):
+    groups, few, tokens = tri_left.shape
+    side = int(tokens**0.5)
+    at = lambda ref, k: ref.at[k]
+    split = (few, 2, GROUP // 2, tokens)
+    left, right = exchange("c", (tri_left, tri_right), (tri_left.shape,) * 2, [at] * 2, [at] * 2, 7)
+    left = jnp.transpose(left, (1, 0, 2)).reshape(split)
+    right = jnp.transpose(right, (1, 0, 2)).reshape(split)
+    left, right = exchange(
+        "b",
+        (left, right),
+        ((GROUP, *split[2:]), (GROUP, *split[1:])),
+        [lambda ref, k: ref.at[k // 2, lax.rem(k, 2)], lambda ref, k: ref.at[k // 2]],
+        [at] * 2,
+        8,
+    )
+    whole = GROUP * side
+    left = jnp.transpose(left.reshape(GROUP, GROUP // 2, side, side), (1, 2, 0, 3))
+    right = jnp.transpose(right.reshape(GROUP, GROUP, side, side), (1, 2, 0, 3))
+    mixed = lax.dot_general(
+        left.reshape(whole // 2, whole),
+        right.reshape(whole, whole),
+        (((1,), (1,)), ((), ())),
+        preferred_element_type=jnp.float32,
+    ).astype(jnp.bfloat16)
+    mixed = jnp.transpose(mixed.reshape(GROUP // 2, side, GROUP, side), (2, 0, 1, 3))
+    (mixed,) = exchange(
+        "b",
+        (mixed.reshape(GROUP, GROUP // 2, tokens),),
+        (split,),
+        [at],
+        [lambda ref, k: ref.at[k // 2, lax.rem(k, 2)]],
+        9,
+    )
+    mixed = jnp.transpose(mixed.reshape(few, GROUP, tokens), (1, 0, 2))
+    (mixed,) = exchange("c", (mixed,), ((GROUP, few, tokens),), [at], [at], 10)
+    return mixed.reshape(groups * few, tokens)
 
 
 def layer_normalize(tensor):
@@ -513,57 +624,34 @@
         .astype(jnp.bfloat16)
         .reshape(device_local_rows, residue_total * PRODUCT_FEATURES)
     )
-    right_factor = (
-        factors[..., PRODUCT_FEATURES:]
-        .astype(jnp.bfloat16)
-        .reshape(device_local_rows, residue_total * PRODUCT_FEATURES)
-    )
+    right_factor = jnp.transpose(
+        factors[..., PRODUCT_FEATURES:].astype(jnp.bfloat16), (0, 2, 1)
+    ).reshape(device_local_rows, residue_total * PRODUCT_FEATURES)
     left_all, right_rows = gather_factors(left_factor, right_factor)
-    seq_total = left_all.shape[0]
-    outer_sum = lax.dot_general(
-        left_all, right_rows, (((0,), (0,)), ((), ())), preferred_element_type=jnp.float32
-    )
-    outer_sum = jnp.transpose(
-        outer_sum.reshape(residue_total, PRODUCT_FEATURES, pair_cols, PRODUCT_FEATURES),
-        (0, 2, 1, 3),
-    ).reshape(residue_total, pair_cols, PRODUCT_FEATURES * PRODUCT_FEATURES)
-    outer_mean = (outer_sum / seq_total).astype(jnp.bfloat16)
-    pair_opm = pair_representation.astype(jnp.float32) + jnp.dot(
-        outer_mean, outer_output_matrix, preferred_element_type=jnp.float32
-    )
-    tri_normed = layer_normalize(pair_opm).astype(jnp.bfloat16)
-    projected = jnp.dot(tri_normed, triangle_input_weights, preferred_element_type=jnp.float32)
-    pair_keep = (keep_here[:, None] * keep_there[None, :])[:, :, None]
-    tri_left = (
-        pair_keep * jax.nn.sigmoid(projected[..., :CZ]) * projected[..., CZ : 2 * CZ]
-    ).astype(jnp.bfloat16)
-    tri_right = (
-        pair_keep
-        * jax.nn.sigmoid(projected[..., 2 * CZ : 3 * CZ])
-        * projected[..., 3 * CZ : 4 * CZ]
-    ).astype(jnp.bfloat16)
-    tri_gate = jax.nn.sigmoid(projected[..., 4 * CZ :])
-    right_all = gathered_by_axis(tri_right, COL, (0, 1), 0)
-    turned = lax.psum_scatter(
-        jnp.einsum("ikc,jkc->jic", tri_left, right_all, preferred_element_type=jnp.float32).astype(
-            jnp.bfloat16
-        ),
-        ("branch", "row"),
-        scatter_dimension=0,
-        tiled=True,
-    ).astype(jnp.float32)
-    tri_mixed = jnp.transpose(turned, (1, 0, 2))
-    mixed_normed = layer_normalize(tri_mixed).astype(jnp.bfloat16)
-    pair_tri = pair_opm + tri_gate * jnp.dot(
-        mixed_normed, triangle_output_matrix, preferred_element_type=jnp.float32
-    )
-    pair_trans_in = layer_normalize(pair_tri).astype(jnp.bfloat16)
+    tokens = residue_total * pair_cols
+    pair_first = jnp.transpose(pair_representation.reshape(tokens, CZ))
+    mix = jnp.transpose(
+        outer_output_matrix.reshape(PRODUCT_FEATURES, PRODUCT_FEATURES // 4, 4 * CZ), (1, 0, 2)
+    ).reshape(PRODUCT_FEATURES * PRODUCT_FEATURES // 4, 4 * CZ)
+    pair_keep = (keep_here[:, None] * keep_there[None, :]).reshape(1, tokens)
+    pair_opm, tri_left, tri_right, tri_gate = pair_front(
+        left_all, right_rows, pair_first, mix, triangle_input_weights, pair_keep
+    )
+    tri_mixed = triangle(tri_left, tri_right).astype(jnp.float32)
+    contract = (((0,), (0,)), ((), ()))
+    mixed_normed = norm_channels(tri_mixed).astype(jnp.bfloat16)
+    pair_tri = pair_opm + tri_gate * lax.dot_general(
+        triangle_output_matrix, mixed_normed, contract, preferred_element_type=jnp.float32
+    )
+    pair_trans_in = norm_channels(pair_tri).astype(jnp.bfloat16)
     pair_hidden = jax.nn.relu(
-        jnp.dot(pair_trans_in, pair_up_weight, preferred_element_type=jnp.float32)
+        lax.dot_general(pair_up_weight, pair_trans_in, contract, preferred_element_type=jnp.float32)
     ).astype(jnp.bfloat16)
     updated_pair_state = (
-        pair_tri + jnp.dot(pair_hidden, pair_down_weight, preferred_element_type=jnp.float32)
+        jnp.transpose(pair_tri)
+        + lax.dot_general(pair_hidden, pair_down_weight, contract, preferred_element_type=jnp.float32)
     ).astype(jnp.bfloat16)
+    updated_pair_state = updated_pair_state.reshape(residue_total, pair_cols, CZ)
     return (alignment_final_state.astype(jnp.bfloat16), updated_pair_state)
 
 

time: 363 us -> 242 us (0.67)
  waiting for transfers between devices: 115 us -> 0 us
  Pallas kernels: 107 us -> 169 us
  local copies, waits for them, and re-layouts: 69.4 us -> 41.1 us
  between operations: 14.7 us -> 1.4 us
  matrix products: 27 us -> 16.4 us
  blocking collectives: 8.88 us -> 0 us
  other arithmetic: 17.9 us -> 13.4 us
    reduce_scatter x1 -> x0, waiting for transfers between devices: 63.7 us -> none  [on_device(): lax.psum_scatter(jnp.einsum('ikc,jkc->jic', tri_left, right_all, preferre...]
    pallas_call x6 -> x10, Pallas kernels: 107 us -> 164 us  [call_exchange(): pl.pallas_call(kernel, out_shape=out_shape, in_specs=[pl.BlockSpec(memory...]
    all_gather x1 -> x0, waiting for transfers between devices: 51.1 us -> none  [gather_in_order(): blocks = lax.all_gather(blocks, axes[k], axis=0, tiled=True)]
    convert_element_type x5 -> x1, local copies, waits for them, and re-layouts: 41.3 us -> 0.84 us  [on_device(): updated_pair_state = (jnp.transpose(pair_tri) + lax.dot_general(pair_hidd...]
    reshape x1 -> x14, local copies, waits for them, and re-layouts: 0.17 us -> 19.9 us  [the longest x2 6.85 us: triangle(): right = jnp.transpose(right.reshape(GROUP, GROUP, side, side), (1, 2, 0, 3))]
    dot_general x6 -> x3, matrix products: 12 us -> 1.36 us  [the longest x1 0.74 us: on_device(): lax.dot_general(pair_hidden, pair_down_weight, contract, preferred_elemen...]
    all_gather x1 -> x0, blocking collectives: 8.88 us -> none  [gather_in_order(): blocks = lax.all_gather(blocks, axes[k], axis=0, tiled=True)]
    another operation x1 -> x0, local copies, waits for them, and re-layouts: 8.64 us -> none  [gathered_by_axis(): return jnp.moveaxis(blocks, 0, dim).reshape(dims)]
  transfers between devices with their start and end apart: 2 -> 0, of which waited for: 2 -> 0; matrix products, arithmetic and copies ran while one was open for 1% -> 0% of each run, Pallas kernels for 0% -> 0%
where the time goes in v2:
time: 242 us
  Pallas kernels  169 us (70%)
  local copies, waits for them, and re-layouts  41.1 us (17%)
  matrix products  16.4 us (7%)
  other arithmetic  13.4 us (6%)
    pallas_call x10, Pallas kernels, call_exchange(): pl.pallas_call(kernel, out_shape=out_shape, in_specs=[pl.BlockSpec(memory...  164 us
    reshape x2, local copies, waits for them, and re-layouts, triangle(): right = jnp.transpose(right.reshape(GROUP, GROUP, side, side), (1, 2, 0, 3))  6.85 us
    pallas_call x1, Pallas kernels, pair_front(): pl.pallas_call(kernel, out_shape=[jax.ShapeDtypeStruct((channels, tokens)...  5.14 us

profile of v2, /device:TPU:1, one launch (start us, length us, event | category | flops | bytes accessed | tf_op | source)
XLA Modules:
  0.0 241.7 jit_solution(7785321311380302381)
XLA Ops:
  1.9 1.3 fusion.40
  3.2 1.3 fusion.41
  7.3 11.4 %shard_map.194 = (bf16[16,8,1024]{2,1,0:T(8,128)(2,1)S(1)}, bf16[16,8,128]{2,1,0:T(8,128)(2,1)S(1)}) custom-call(bf16[8,1024]{1,0:T(8,128)(2,1)S(1)} %fusion.25.refs_0_, bf16[16,8,128]{2,1,0:T(8,128)(2,1)S(1)} %pad.8.refs_1_), custom_call_target="tpu_custom_call" | custom-call | bytes 524288 | tf_op jit(solution)/shard_map/pallas_call | solution.py:41
  22.0 40.9 %shard_map.195 = (bf16[8,512,512]{2,1,0:T(8,128)(2,1)S(1)}, bf16[512,256]{1,0:T(8,128)(2,1)S(1)}, bf16[16,8,128]{2,1,0:T(8,128)(2,1)S(1)}) custom-call(bf16[8,32,512]{2,1,0:T(8,128)(2,1)S(1)} %reshape.276.b_ref, bf16[16,32,256]{2,1,0:T(8,128)(2,1)S(1)} %copy.90.r_ref, bf16[16,8,128]{2,1,0:T(8,128)(2,1)S(1)} %pad.9.m_ref), custom_call_target="tpu_custom_call" | custom-call | bytes 8388608 | tf_op jit(solution)/shard_map/pallas_call | solution.py:41
  62.9 1.9 copy-done.1
  68.0 1.8 copy.92
  69.8 1.8 copy.93
  71.7 4.1 %fusion.87 = (f32[8,512]{1,0:T(8,128)S(1)}, f32[8,512,512]{2,1,0:T(8,128)S(1)}) fusion(bf16[8,512,512]{2,1,0:T(8,128)(2,1)} %copy-done.1, bf16[512,8,32]{0,2,1:T(8,128)(2,1)} %bitcast.160, bf16[512,8,32]{0,2,1:T(8,128)(2,1)} %bitcast.161, pred[512]{0:T(512)(128)(4,1)S(1)} %gt.33), kind=kOutput, calls=%fused_computation.132 | convolution fusion | flops 142602240 | bytes 13124096 | tf_op jit(solution)/shard_map/sihd,sjhd->shij/dot_general | solution.py:533
  75.8 2.1 fusion
  77.9 2.6 %fusion.31 = f32[1,512,8,32]{1,3,2,0:T(8,128)} fusion(bf16[512,8,32]{0,2,1:T(8,128)(2,1)S(1)} %bitcast.159, f32[8,512,512]{2,1,0:T(8,128)S(1)} %get-tuple-element.55, f32[8,512]{1,0:T(8,128)S(1)} %get-tuple-element.54, f32[512,8]{0,1:T(8,128)S(1)} %bitcast.168), kind=kOutput, calls=%fused_computation.41 | convolution fusion | flops 138543104 | bytes 9207808 | tf_op jit(solution)/shard_map/shij,sjhd->sihd/dot_general | solution.py:540
  80.4 2.1 copy.95
  83.7 11.7 %shard_map.196 = bf16[16,32,256]{2,1,0:T(8,128)(2,1)S(1)} custom-call(bf16[512,256]{1,0:T(8,128)(2,1)S(1)} %fusion.75.refs_0_), custom_call_target="tpu_custom_call" | custom-call | bytes 524288 | tf_op jit(solution)/shard_map/pallas_call | solution.py:41
  96.2 9.3 %shard_map.197 = bf16[2,256,256]{2,1,0:T(8,128)(2,1)S(1)} custom-call(bf16[32,16,256]{2,1,0:T(8,128)(2,1)S(1)} %fusion.63.refs_0_), custom_call_target="tpu_custom_call" | custom-call | bytes 524288 | tf_op jit(solution)/shard_map/pallas_call | solution.py:41
  105.6 1.5 fusion.89
  110.8 1.8 select_reduce_fusion
  113.5 1.7 fusion.26
  115.2 2.1 copy.102
  117.3 1.3 fusion.62.refs_0_
  118.6 8.6 %shard_map.198 = bf16[32,16,256]{2,1,0:T(8,128)(2,1)S(1)} custom-call(bf16[2,256,256]{2,1,0:T(8,128)(2,1)S(1)} %fusion.62.refs_0_), custom_call_target="tpu_custom_call" | custom-call | bytes 524288 | tf_op jit(solution)/shard_map/pallas_call | solution.py:41
  131.4 25.1 %shard_map.199 = (bf16[256,1024]{1,0:T(8,128)(2,1)S(1)}, bf16[256,1024]{1,0:T(8,128)(2,1)S(1)}) custom-call(bf16[16,1024]{1,0:T(8,128)(2,1)S(1)} %reshape.285.l_ref, bf16[16,1024]{1,0:T(8,128)(2,1)S(1)} %reshape.286.r_ref), custom_call_target="tpu_custom_call" | custom-call | bytes 2097152 | tf_op jit(solution)/shard_map/pallas_call | solution.py:41
  157.2 5.1 %shard_map.200 = (f32[128,1024]{1,0:T(8,128)S(1)}, bf16[16,8,1024]{2,1,0:T(8,128)(2,1)S(1)}, bf16[16,8,1024]{2,1,0:T(8,128)(2,1)S(1)}, f32[128,1024]{1,0:T(8,128)S(1)}) custom-call(bf16[256,1024]{1,0:T(8,128)(2,1)S(1)} %get-tuple-element.22.l_ref, bf16[256,1024]{1,0:T(8,128)(2,1)S(1)} %get-tuple-element.23.r_ref, bf16[128,1024]{1,0:T(8,128)(2,1)S(1)} %bitcast.149, ...), custom_call_target="tpu_custom_call" | custom-call | tf_op jit(solution)/shard_map/pallas_call | solution.py:383
  162.4 19.8 %shard_map.201 = (bf16[16,8,1024]{2,1,0:T(8,128)(2,1)S(1)}, bf16[16,8,1024]{2,1,0:T(8,128)(2,1)S(1)}) custom-call(bf16[16,8,1024]{2,1,0:T(8,128)(2,1)S(1)} %get-tuple-element.26.refs_0_, bf16[16,8,1024]{2,1,0:T(8,128)(2,1)S(1)} %get-tuple-element.27.refs_1_), custom_call_target="tpu_custom_call" | custom-call | bytes 524288 | tf_op jit(solution)/shard_map/pallas_call | solution.py:41
  182.5 14.7 %shard_map.202 = (bf16[16,8,1024]{2,1,0:T(8,128)(2,1)S(1)}, bf16[16,2,8,1024]{3,2,1,0:T(8,128)(2,1)S(1)}) custom-call(bf16[8,2,8,1024]{3,2,1,0:T(8,128)(2,1)S(1)} %get-tuple-element.69.refs_0_, bf16[8,2,8,1024]{3,2,1,0:T(8,128)(2,1)S(1)} %get-tuple-element.68.refs_1_), custom_call_target="tpu_custom_call" | custom-call | bytes 524288 | tf_op jit(solution)/shard_map/pallas_call | solution.py:41
  198.0 1.7 copy.155
  199.6 2.2 reshape.293
  201.9 2.6 %reshape.294 = bf16[16,16,32,32]{3,2,1,0:T(8,128)(2,1)} reshape(bf16[16,2,8,1024]{3,2,1,0:T(8,128)(2,1)S(1)} %get-tuple-element.31) | data formatting | bytes 1048576 | tf_op jit(solution)/shard_map/reshape | solution.py:415
  204.5 4.2 %copy.153 = bf16[16,16,32,32]{3,0,2,1:T(8,128)(2,1)} copy(bf16[16,16,32,32]{3,2,1,0:T(8,128)(2,1)} %reshape.294) | data formatting | bytes 1048576 | tf_op jit(solution)/shard_map/reshape | solution.py:415
  208.7 3.4 %reshape.295 = bf16[512,512]{1,0:T(8,128)(2,1)S(1)} reshape(bf16[16,32,16,32]{3,2,1,0:T(8,128)(2,1)} %bitcast.153) | data formatting | bytes 1048576 | tf_op jit(solution)/shard_map/reshape | solution.py:418
  213.0 1.3 copy.154
  214.3 2.3 reshape.297.refs_0_
  216.6 9.9 %shard_map.203 = bf16[8,2,8,1024]{3,2,1,0:T(8,128)(2,1)S(1)} custom-call(bf16[16,8,1024]{2,1,0:T(8,128)(2,1)S(1)} %reshape.297.refs_0_), custom_call_target="tpu_custom_call" | custom-call | bytes 524288 | tf_op jit(solution)/shard_map/pallas_call | solution.py:41
  226.7 12.8 %shard_map.204 = bf16[16,8,1024]{2,1,0:T(8,128)(2,1)S(1)} custom-call(bf16[16,8,1024]{2,1,0:T(8,128)(2,1)S(1)} %bitcast.148), custom_call_target="tpu_custom_call" | custom-call | bytes 524288 | tf_op jit(solution)/shard_map/pallas_call | solution.py:41
  (112 shorter events, 26.1 us)
Async XLA Ops:
  0.6 64.2 %copy-start = (bf16[256,1024]{1,0:T(8,128)(2,1)S(1)}, bf16[256,1024]{1,0:T(8,128)(2,1)}, u32[]{:S(2)}) copy-start(bf16[256,1024]{1,0:T(8,128)(2,1)} %param.24) | copy-start | bytes 1572868
  0.6 20.5 %copy-start.4 = (bf16[16,32,256]{2,1,0:T(8,128)(2,1)S(1)}, bf16[16,32,256]{2,1,0:T(8,128)(2,1)}, u32[]{:S(2)}) copy-start(bf16[16,32,256]{2,1,0:T(8,128)(2,1)} %param.19) | copy-start | bytes 786436
  62.9 1.9 copy-start.1
  77.8 17.5 %copy-start.9 = (bf16[256,256]{1,0:T(8,128)(2,1)S(1)}, bf16[256,256]{1,0:T(8,128)(2,1)}, u32[]{:S(2)}) copy-start(bf16[256,256]{1,0:T(8,128)(2,1)} %param.25) | copy-start | bytes 393220
  110.8 2.7 %copy-start.8 = (bf16[2,256,256]{1,2,0:T(8,128)(2,1)S(1)}, bf16[2,256,256]{1,2,0:T(8,128)(2,1)}, u32[]{:S(2)}) copy-start(bf16[2,256,256]{1,2,0:T(8,128)(2,1)} %copy.100) | copy-start | bytes 786436
  113.5 13.6 %copy-start.10 = (bf16[256,256]{1,0:T(8,128)(2,1)S(1)}, bf16[256,256]{1,0:T(8,128)(2,1)}, u32[]{:S(2)}) copy-start(bf16[256,256]{1,0:T(8,128)(2,1)} %param.29) | copy-start | bytes 393220
  117.3 10.7 %copy-start.5 = (bf16[256,1024]{1,0:T(8,128)(2,1)S(1)}, bf16[256,1024]{1,0:T(8,128)(2,1)}, u32[]{:S(2)}) copy-start(bf16[256,1024]{1,0:T(8,128)(2,1)} %param.30) | copy-start | bytes 1572868
  117.3 11.2 %copy-start.6 = (bf16[1024,256]{1,0:T(8,128)(2,1)S(1)}, bf16[1024,256]{1,0:T(8,128)(2,1)}, u32[]{:S(2)}) copy-start(bf16[1024,256]{1,0:T(8,128)(2,1)} %param.31) | copy-start | bytes 1572868
  127.5 3.1 %copy-start.15 = (bf16[256,64]{0,1:T(8,128)(2,1)S(1)}, bf16[256,64]{0,1:T(8,128)(2,1)}, u32[]{:S(2)}) copy-start(bf16[256,64]{0,1:T(8,128)(2,1)} %param.32) | copy-start | bytes 98308
  128.0 28.6 %copy-start.3 = (bf16[32,32,128]{2,1,0:T(8,128)(2,1)S(1)}, bf16[32,32,128]{2,1,0:T(8,128)(2,1)}, u32[]{:S(2)}) copy-start(bf16[32,32,128]{2,1,0:T(8,128)(2,1)} %param.20) | copy-start | bytes 786436
  128.0 28.7 %copy-start.7 = (bf16[1024,128]{1,0:T(8,128)(2,1)S(1)}, bf16[1024,128]{1,0:T(8,128)(2,1)}, u32[]{:S(2)}) copy-start(bf16[1024,128]{1,0:T(8,128)(2,1)} %param.33) | copy-start | bytes 786436
  128.5 28.5 %copy-start.12 = (s32[512]{0:T(512)S(1)}, s32[512]{0:T(512)}, u32[]{:S(2)}) copy-start(s32[512]{0:T(512)} %param.22) | copy-start | bytes 6148
  128.5 28.8 %copy-start.2 = (bf16[128,640]{1,0:T(8,128)(2,1)S(1)}, bf16[128,640]{1,0:T(8,128)(2,1)}, u32[]{:S(2)}) copy-start(bf16[128,640]{1,0:T(8,128)(2,1)} %w_ref.1) | copy-start | bytes 491524
  212.1 27.6 %copy-start.11 = (bf16[128,128]{1,0:T(8,128)(2,1)S(1)}, bf16[128,128]{1,0:T(8,128)(2,1)}, u32[]{:S(2)}) copy-start(bf16[128,128]{1,0:T(8,128)(2,1)} %param.35) | copy-start | bytes 98308
  213.0 27.0 %copy-start.13 = (bf16[512,128]{1,0:T(8,128)(2,1)S(1)}, bf16[512,128]{1,0:T(8,128)(2,1)}, u32[]{:S(2)}) copy-start(bf16[512,128]{1,0:T(8,128)(2,1)} %param.37) | copy-start | bytes 393220
  213.0 27.0 %copy-start.14 = (bf16[128,512]{1,0:T(8,128)(2,1)S(1)}, bf16[128,512]{1,0:T(8,128)(2,1)}, u32[]{:S(2)}) copy-start(bf16[128,512]{1,0:T(8,128)(2,1)} %param.36) | copy-start | bytes 393220

commit v3 on v2

--- a/solution.py
+++ b/solution.py
@@ -20,6 +20,7 @@
 MESH = pl.DeviceIdType.MESH
 GROUP = 16
 RING = 8
+SIZES = {"b": 16, "c": 16, "z": 8}
 
 
 def place():
@@ -53,27 +54,33 @@
 
 class Pushes:
     def __init__(self, over, ins, outs, picks, puts, send, recv):
-        b, c = place()[4:]
-        self.me = b if over == "b" else c
-        self.device = (lambda k: across(k, c)) if over == "b" else (lambda k: across(b, k))
+        br, ro, x, z, b, c = place()
+        self.count = SIZES[over]
+        self.me, self.device = {
+            "b": (b, lambda k: across(k, c)),
+            "c": (c, lambda k: across(b, k)),
+            "z": (z, lambda k: (br, ro, x, k)),
+        }[over]
         self.parts = list(zip(ins, outs, picks, puts))
         self.send, self.recv = send, recv
 
     def greet(self, barrier):
         def one(d, carry):
-            pl.semaphore_signal(
-                barrier, inc=1, device_id=self.device(lax.rem(self.me + d, GROUP)), device_id_type=MESH
-            )
+            to = self.device(lax.rem(self.me + d, self.count))
+            pl.semaphore_signal(barrier, inc=1, device_id=to, device_id_type=MESH)
             return carry
 
-        lax.fori_loop(1, GROUP, one, 0)
-
-    def copies(self, d, sender):
-        peer = lax.rem(self.me + (GROUP - d if sender else d), GROUP)
+        lax.fori_loop(1, self.count, one, 0)
+
+    def sender(self, d):
+        return lax.rem(self.me + (self.count - d), self.count)
+
+    def copies(self, d, coming):
+        peer = self.sender(d) if coming else lax.rem(self.me + d, self.count)
         for k, (src, dst, pick, put) in enumerate(self.parts):
             yield remote(
-                pick(src, self.me if sender else peer),
-                put(dst, peer if sender else self.me),
+                pick(src, self.me if coming else peer),
+                put(dst, peer if coming else self.me),
                 self.send.at[k, d],
                 self.recv.at[k, d],
                 self.device(peer),
@@ -85,19 +92,25 @@
                 copy.start()
             return carry
 
-        lax.fori_loop(1, GROUP, one, 0)
+        lax.fori_loop(1, self.count, one, 0)
         for src, dst, pick, put in self.parts:
             put(dst, self.me)[...] = pick(src, self.me)[...]
 
+    def arrive(self, d):
+        for copy in self.copies(d, True):
+            copy.wait_recv()
+
+    def sent(self, d):
+        for copy in self.copies(d, False):
+            copy.wait_send()
+
     def finish(self):
         def one(d, carry):
-            for copy in self.copies(d, True):
-                copy.wait_recv()
-            for copy in self.copies(d, False):
-                copy.wait_send()
+            self.arrive(d)
+            self.sent(d)
             return carry
 
-        lax.fori_loop(1, GROUP, one, 0)
+        lax.fori_loop(1, self.count, one, 0)
 
 
 def exchange(over, arrays, shapes, picks, puts, collective_id):
@@ -107,7 +120,7 @@
         pushes = Pushes(over, refs[:n], refs[n : 2 * n], picks, puts, refs[2 * n], refs[2 * n + 1])
         barrier = pltpu.get_barrier_semaphore()
         pushes.greet(barrier)
-        pl.semaphore_wait(barrier, GROUP - 1)
+        pl.semaphore_wait(barrier, SIZES[over] - 1)
         pushes.start()
         pushes.finish()
 
@@ -116,124 +129,225 @@
     return call_exchange(kernel, out_shape, scratch, collective_id, 1 << 18, *arrays)
 
 
-def ring_gather(start, whole, own, view, twins, greeted, send, recv):
-    br, ro, x, z, _, c = place()
-    at = lambda xx, zz: xx * RING + lax.rem(zz + RING, RING)
-    right = (br, ro, x, lax.rem(z + 1, RING))
-    left = (br, ro, x, lax.rem(z + RING - 1, RING))
-    cross = (br, ro, 1 - x, z)
-    twin = (br, ro + 1 - 2 * lax.rem(ro, 2), x, z)
-    core = lax.rem(ro, 2)
-    copies, handed = [], []
-
-    def push(src, block, half, to):
-        k = len(copies)
-        copies.append(remote(src, view(whole, block, half, core), send.at[k], recv.at[k], to))
-        copies[-1].start()
-        return k
-
-    def arrived(k, block, half):
-        there = view(whole, block, half, core)
-        remote(there, there, send.at[k], recv.at[k], right).wait_recv()
-
-    def hand(block, half):
-        if twins:
-            handed.append((push(view(whole, block, half, core), block, half, twin), block, half))
-
-    mine = own(start, core)
-    k_cross = push(mine, c, None, cross)
-    going = {(0, +1): push(mine, c, None, right), (0, -1): push(mine, c, None, left)}
-    greeted()
-    there = at(1 - x, z)
-    arrived(k_cross, there, None)
-    for way, to in ((+1, right), (-1, left)):
-        going[1, way] = push(view(whole, there, None, core), there, None, to)
-    hand(there, None)
-    for step in (1, 2, 3):
-        coming = {}
-        for other in (0, 1):
-            for way, to in ((+1, right), (-1, left)):
-                block = at((1 - x) if other else x, z - way * step)
-                arrived(going[other, way], block, None)
-                half = None if step < 3 else (0 if way > 0 else 1)
-                coming[other, way] = push(view(whole, block, half, core), block, half, to)
-                hand(block, None)
-        going = coming
-    for other in (0, 1):
-        for way in (+1, -1):
-            block, half = at((1 - x) if other else x, z - way * 4), 0 if way > 0 else 1
-            arrived(going[other, way], block, half)
-            hand(block, half)
-    for k, block, half in handed:
-        there = view(whole, block, half, 1 - core)
-        remote(there, there, send.at[k], recv.at[k], twin).wait_recv()
-    for copy in copies:
-        copy.wait_send()
-
-
-def ring_copies(twins):
-    return 19 + (17 if twins else 0)
-
-
-def greet_ring(barrier, twins, cross_and_ring):
-    br, ro, x, z, _, _ = place()
-    to = []
-    if cross_and_ring:
-        to += [
-            (br, ro, x, lax.rem(z + 1, RING)),
-            (br, ro, x, lax.rem(z + RING - 1, RING)),
-            (br, ro, 1 - x, z),
-        ]
-    if twins:
-        to.append((br, ro + 1 - 2 * lax.rem(ro, 2), x, z))
-    for device in to:
-        pl.semaphore_signal(barrier, inc=1, device_id=device, device_id_type=MESH)
-    return len(to)
-
-
-def gather_bias_and_rows(bias, rows, mask):
+def crosswise():
+    br, ro, x, z = place()[:4]
+    return (br, ro, 1 - x, z)
+
+
+def gather_bias_and_rows(bias, rows):
     heads, some, all_ = bias.shape
-    half_heads = heads // 2
-
-    def own(ref, core):
-        return ref.at[pl.ds(core * half_heads, half_heads)]
-
-    def view(ref, block, half, core):
-        first, count = core * half_heads, half_heads
-        if half is not None:
-            count = half_heads // 2
-            first = first + half * count
-        return ref.at[pl.ds(first, count), pl.ds(pl.multiple_of(block * some, some), some)]
-
-    picks = [lambda ref, k: ref.at[k]] * 2
-    puts = [
-        lambda ref, k: ref.at[pl.ds(pl.multiple_of(k * some, some), some)],
-        lambda ref, k: ref.at[k],
-    ]
-
-    def kernel(b_ref, r_ref, m_ref, ob_ref, or_ref, om_ref, psend, precv, rsend, rrecv):
-        pushes = Pushes("c", (r_ref, m_ref), (or_ref, om_ref), picks, puts, psend, precv)
+    carried = heads // 2
+    pair, _, tall, channels = rows.shape
+    n_copies = 32
+
+    def kernel(b_ref, r_ref, ob_ref, or_ref, psend, precv, xsend, xrecv, rsend, rrecv):
+        br, ro, x, z, _, c = place()
+        core = lax.rem(ro, 2)
+        right = (br, ro, x, lax.rem(z + 1, RING))
+        left = (br, ro, x, lax.rem(z + RING - 1, RING))
+        twin = (br, ro + 1 - 2 * core, x, z)
+        cross = crosswise()
+        put = lambda ref, k: ref.at[:, x * RING + k]
+        pushes = Pushes("z", (r_ref,), (or_ref,), [lambda ref, k: ref.at[:, k]], [put], psend, precv)
         barrier = pltpu.get_barrier_semaphore()
         pushes.greet(barrier)
-        more = greet_ring(barrier, True, False)
-        pl.semaphore_wait(barrier, GROUP - 1 + more)
-        c = place()[5]
-
-        def meanwhile():
-            pushes.start()
-            ob_ref[:, pl.ds(pl.multiple_of(c * some, some), some)] = b_ref[...]
-
-        ring_gather(b_ref, ob_ref, own, view, True, meanwhile, rsend, rrecv)
-        pushes.finish()
+        for device in (twin, cross):
+            pl.semaphore_signal(barrier, inc=1, device_id=device, device_id_type=MESH)
+        pl.semaphore_wait(barrier, RING - 1 + 2)
+
+        def view(block, half, mine):
+            first, count = mine * carried, carried
+            if half is not None:
+                count = carried // 2
+                first = first + half * count
+            rows_at = pl.multiple_of(lax.rem(block + RING, RING) * some, some)
+            return ob_ref.at[pl.ds(first, count), pl.ds(rows_at, some)]
+
+        copies, handed = [], []
+
+        def push(src, block, half, to):
+            k = len(copies)
+            copies.append(remote(src, view(block, half, core), rsend.at[k], rrecv.at[k], to))
+            copies[-1].start()
+            return k
+
+        def arrived(k, block, half):
+            there = view(block, half, core)
+            remote(there, there, rsend.at[k], rrecv.at[k], right).wait_recv()
+
+        def hand(block, half):
+            handed.append((push(view(block, half, core), block, half, twin), block, half))
+
+        def over(d, coming):
+            k = pushes.sender(d)
+            place_at = (1 - x if coming else x) * RING + k
+            there = or_ref.at[:, place_at]
+            return remote(there, there, xsend.at[d], xrecv.at[d], cross)
+
+        mine = b_ref.at[pl.ds(core * carried, carried)]
+        pushes.start()
+        going = {+1: push(mine, z, None, right), -1: push(mine, z, None, left)}
+        first = remote(r_ref.at[:, z], or_ref.at[:, c], xsend.at[0], xrecv.at[0], cross)
+        first.start()
+        ob_ref[:, pl.ds(pl.multiple_of(z * some, some), some)] = b_ref[...]
+        for step in (1, 2, 3):
+            coming = {}
+            for way, to in ((+1, right), (-1, left)):
+                block = z - way * step
+                arrived(going[way], block, None)
+                half = None if step < 3 else (0 if way > 0 else 1)
+                coming[way] = push(view(block, half, core), block, half, to)
+                hand(block, None)
+            going = coming
+            for d in (step, RING - step):
+                pushes.arrive(d)
+                over(d, False).start()
+        pushes.arrive(4)
+        over(4, False).start()
+        for way in (+1, -1):
+            half = 0 if way > 0 else 1
+            arrived(going[way], z - way * 4, half)
+            hand(z - way * 4, half)
+        for k, block, half in handed:
+            there = view(block, half, 1 - core)
+            remote(there, there, rsend.at[k], rrecv.at[k], twin).wait_recv()
+        for d in range(RING):
+            over(d, True).wait_recv()
+        for copy in copies:
+            copy.wait_send()
+        first.wait_send()
+        for d in range(1, RING):
+            pushes.sent(d)
+            over(d, False).wait_send()
 
     out_shape = [
-        jax.ShapeDtypeStruct((heads, GROUP * some, all_), jnp.bfloat16),
-        jax.ShapeDtypeStruct((GROUP * some, rows.shape[2]), jnp.bfloat16),
-        jax.ShapeDtypeStruct(mask.shape, jnp.bfloat16),
+        jax.ShapeDtypeStruct((heads, RING * some, all_), jnp.bfloat16),
+        jax.ShapeDtypeStruct((pair, GROUP, tall, channels), jnp.bfloat16),
     ]
-    scratch = [pltpu.SemaphoreType.DMA((2, GROUP))] * 2
-    scratch += [pltpu.SemaphoreType.DMA((ring_copies(True),))] * 2
-    return call_exchange(kernel, out_shape, scratch, 1, 4 << 20, bias, rows, mask)
+    scratch = [pltpu.SemaphoreType.DMA((1, RING))] * 2
+    scratch += [pltpu.SemaphoreType.DMA((RING,))] * 2
+    scratch += [pltpu.SemaphoreType.DMA((n_copies,))] * 2
+    return call_exchange(kernel, out_shape, scratch, 1, 2 << 20, bias, rows)
+
+
+def compute(kernel, out_shape, *args, scratch=(), limit=40):
+    return pl.pallas_call(
+        kernel,
+        out_shape=out_shape,
+        in_specs=[pl.BlockSpec(memory_space=pltpu.VMEM)] * len(args),
+        out_specs=jax.tree.map(lambda _: pl.BlockSpec(memory_space=pltpu.VMEM), out_shape),
+        scratch_shapes=list(scratch),
+        compiler_params=pltpu.CompilerParams(vmem_limit_bytes=limit << 20),
+    )(*args)
+
+
+def heads_attend(queries, keys, values, present, bias_of):
+    lanes = 128
+    per = lanes // PER_HEAD_WIDTH
+    lane = lax.broadcasted_iota(jnp.int32, (1, lanes), 1) // PER_HEAD_WIDTH
+    blocks = []
+    for block in range(HEADS // per):
+        cols = slice(block * lanes, (block + 1) * lanes)
+        total = jnp.zeros((queries.shape[0], lanes), jnp.float32)
+        for h in range(per):
+            here = (lane == h).astype(jnp.float32)
+            query = queries[:, cols] * here.astype(jnp.bfloat16)
+            scores = lax.dot_general(
+                query, keys[:, cols], (((1,), (1,)), ((), ())), preferred_element_type=jnp.float32
+            )
+            if bias_of is not None:
+                scores = scores + bias_of(block * per + h).astype(jnp.float32)
+            scores = jnp.where(present, scores, NEGATIVE)
+            powers = jnp.exp(scores - jnp.max(scores, axis=-1, keepdims=True))
+            totals = jnp.sum(powers, axis=-1, keepdims=True)
+            summed = jnp.dot(
+                powers.astype(jnp.bfloat16), values[:, cols], preferred_element_type=jnp.float32
+            )
+            total = total + (summed / totals) * here
+        blocks.append(total)
+    return jnp.concatenate(blocks, axis=1)
+
+
+def row_attention(rows, bias, weights):
+    pair, blocks, tall, channels = rows.shape
+    some = tall - 8
+    residues = blocks * some
+    step = 128
+
+    def kernel(r_ref, b_ref, w_ref, o_ref, q_ref, g_ref):
+        x = place()[2]
+        for r in range(pair):
+            whole = r_ref[r, :, :some].reshape(residues, channels)
+            keys_values = jnp.dot(
+                whole, w_ref[:, channels : 3 * channels], preferred_element_type=jnp.float32
+            ).astype(jnp.bfloat16)
+            keys, values = keys_values[:, :channels], keys_values[:, channels:]
+            own = r_ref[r, pl.ds(x * RING, RING), :some].reshape(residues // 2, channels)
+            q = jnp.dot(own, w_ref[:, :channels], preferred_element_type=jnp.float32)
+            q_ref[...] = (q * PER_HEAD_WIDTH ** (-0.5)).astype(jnp.bfloat16)
+            gate = jnp.dot(own, w_ref[:, 3 * channels :], preferred_element_type=jnp.float32)
+            g_ref[...] = jax.nn.sigmoid(gate)
+            present = []
+            for half in range(2):
+                total = jnp.zeros((8, channels), jnp.float32)
+                for k in range(RING):
+                    total = total + r_ref[r, half * RING + k, some:].astype(jnp.float32)
+                present.append(total[:1])
+            present = jnp.concatenate(present, axis=1) > 0
+
+            def one(t, carry):
+                at = pl.ds(pl.multiple_of(t * step, step), step)
+                attended = heads_attend(
+                    q_ref[at], keys, values, present, lambda h: b_ref[h, at, :]
+                )
+                gated = (attended * g_ref[at]).astype(jnp.bfloat16)
+                o_ref[r, pl.ds(t * (step // some), step // some)] = gated.reshape(
+                    step // some, some, channels
+                )
+                return carry
+
+            lax.fori_loop(0, residues // 2 // step, one, 0)
+
+    out_shape = jax.ShapeDtypeStruct((pair, RING, some, channels), jnp.bfloat16)
+    scratch = [
+        pltpu.VMEM((residues // 2, channels), jnp.bfloat16),
+        pltpu.VMEM((residues // 2, channels), jnp.float32),
+    ]
+    return compute(kernel, out_shape, rows, bias, weights, scratch=scratch)
+
+
+def column_attention(cols, presence, weights):
+    few, rows, channels = cols.shape
+    step = 128
+
+    def kernel(c_ref, p_ref, w_ref, o_ref, q_ref, g_ref):
+        halves = []
+        for half in range(2):
+            total = jnp.zeros((8, 128), jnp.float32)
+            for k in range(RING):
+                total = total + p_ref[half * RING + k].astype(jnp.float32)
+            halves.append(total)
+        there = jnp.concatenate(halves, axis=1)
+        for r in range(few):
+            whole = c_ref[r]
+            projected = jnp.dot(whole, w_ref[...], preferred_element_type=jnp.float32)
+            q_ref[...] = (projected[:, :channels] * PER_HEAD_WIDTH ** (-0.5)).astype(jnp.bfloat16)
+            keys = projected[:, channels : 2 * channels].astype(jnp.bfloat16)
+            values = projected[:, 2 * channels : 3 * channels].astype(jnp.bfloat16)
+            g_ref[...] = jax.nn.sigmoid(projected[:, 3 * channels :])
+            present = there[r : r + 1] > 0
+
+            def one(t, carry):
+                at = pl.ds(pl.multiple_of(t * step, step), step)
+                attended = heads_attend(q_ref[at], keys, values, present, None)
+                o_ref[r, at] = (attended * g_ref[at]).astype(jnp.bfloat16)
+                return carry
+
+            lax.fori_loop(0, rows // step, one, 0)
+
+    out_shape = jax.ShapeDtypeStruct((few, rows, channels), jnp.bfloat16)
+    scratch = [pltpu.VMEM((rows, channels), jnp.bfloat16), pltpu.VMEM((rows, channels), jnp.float32)]
+    return compute(kernel, out_shape, cols, presence, weights, scratch=scratch)
 
 
 def gather_factors(left, right):
@@ -319,7 +433,8 @@
     some = 8
     chunk = some * PRODUCT_FEATURES
     count = wide // chunk
-    groups = channels // 8
+    groups = RING
+    deep = channels // groups
 
     def kernel(l_ref, r_ref, p_ref, m_ref, w_ref, k_ref, opm_ref, tl_ref, tr_ref, gate_ref):
         lane = lax.broadcasted_iota(jnp.int32, (channels, lanes), 1) // PRODUCT_FEATURES
@@ -372,8 +487,8 @@
             here = k_ref[:, cols]
             tri_left = (here * jax.nn.sigmoid(block(0)) * block(1)).astype(jnp.bfloat16)
             tri_right = (here * jax.nn.sigmoid(block(2)) * block(3)).astype(jnp.bfloat16)
-            tl_ref[:, :, cols] = tri_left.reshape(groups, 8, chunk)
-            tr_ref[:, :, cols] = tri_right.reshape(groups, 8, chunk)
+            tl_ref[:, :, cols] = tri_left.reshape(groups, deep, chunk)
+            tr_ref[:, :, cols] = tri_right.reshape(groups, deep, chunk)
             gate_ref[:, cols] = jax.nn.sigmoid(block(4))
             return carry
 
@@ -384,8 +499,8 @@
         kernel,
         out_shape=[
             jax.ShapeDtypeStruct((channels, tokens), jnp.float32),
-            jax.ShapeDtypeStruct((groups, 8, tokens), jnp.bfloat16),
-            jax.ShapeDtypeStruct((groups, 8, tokens), jnp.bfloat16),
+            jax.ShapeDtypeStruct((groups, deep, tokens), jnp.bfloat16),
+            jax.ShapeDtypeStruct((groups, deep, tokens), jnp.bfloat16),
             jax.ShapeDtypeStruct((channels, tokens), jnp.float32),
         ],
         in_specs=[pl.BlockSpec(memory_space=pltpu.VMEM)] * 6,
@@ -394,43 +509,140 @@
     )(left, right, pair, mix, weights, keep)
 
 
+def exchange_channels(left, right):
+    channels, few, tokens = left.shape
+
+    def kernel(l_ref, r_ref, ol_ref, or_ref, send, recv, xsend, xrecv):
+        x = place()[2]
+        cross = crosswise()
+        at = lambda ref, k: ref.at[k]
+        here = lambda ref, k: ref.at[x, k]
+        pushes = Pushes("b", (l_ref, r_ref), (ol_ref, or_ref), [at] * 2, [at, here], send, recv)
+        barrier = pltpu.get_barrier_semaphore()
+        pushes.greet(barrier)
+        pl.semaphore_signal(barrier, inc=1, device_id=cross, device_id_type=MESH)
+        pl.semaphore_wait(barrier, GROUP)
+
+        def over(d, coming):
+            there = or_ref.at[1 - x if coming else x, pushes.sender(d)]
+            return remote(there, there, xsend.at[d], xrecv.at[d], cross)
+
+        pushes.start()
+        me = pushes.me
+        first = remote(r_ref.at[me], or_ref.at[x, me], xsend.at[0], xrecv.at[0], cross)
+        first.start()
+
+        def one(d, carry):
+            pushes.arrive(d)
+            over(d, False).start()
+            return carry
+
+        lax.fori_loop(1, GROUP, one, 0)
+
+        def last(d, carry):
+            pushes.sent(d)
+            over(d, True).wait_recv()
+            over(d, False).wait_send()
+            return carry
+
+        lax.fori_loop(1, GROUP, last, 0)
+        over(0, True).wait_recv()
+        first.wait_send()
+
+    out_shape = [
+        jax.ShapeDtypeStruct((GROUP, few, tokens), jnp.bfloat16),
+        jax.ShapeDtypeStruct((2, GROUP, few, tokens), jnp.bfloat16),
+    ]
+    scratch = [pltpu.SemaphoreType.DMA((2, GROUP))] * 2 + [pltpu.SemaphoreType.DMA((GROUP,))] * 2
+    return call_exchange(kernel, out_shape, scratch, 8, 1 << 20, left, right)
+
+
+def multiply_channel(left, right):
+    blocks, few, tokens = left.shape
+    side = int(tokens**0.5)
+    lanes = 128
+    per = lanes // side
+    wide = blocks * side
+    tall = few * side
+
+    def kernel(l_ref, r_ref, o_ref, a_ref, b_ref, y_ref):
+        lane = lax.broadcasted_iota(jnp.int32, (few, lanes), 1) // side
+
+        def unfold(block, put):
+            def one(v, carry):
+                x = block(pl.ds(pl.multiple_of(v * lanes, lanes), lanes)).astype(jnp.float32)
+                x = x.reshape(blocks * few, lanes)
+                turned = [x] + [pltpu.roll(x, side * s, 1) for s in range(1, per)]
+                for n in range(per):
+                    line = []
+                    for q in range(blocks // per):
+                        piece = jnp.zeros((few, lanes), jnp.float32)
+                        for m in range(per):
+                            k = (q * per + m) * few
+                            piece = jnp.where(lane == m, turned[(m - n) % per][k : k + few], piece)
+                        line.append(piece)
+                    put(v * per + n, jnp.concatenate(line, axis=1))
+                return carry
+
+            lax.fori_loop(0, side // per, one, 0)
+
+        def put_left(i, line):
+            a_ref[pl.ds(pl.multiple_of(i * few, few), few)] = line
+
+        unfold(lambda cols: l_ref[:, :, cols], put_left)
+        for h in range(2):
+
+            def put_right(j, line):
+                b_ref[h, pl.ds(pl.multiple_of(j * few, few), few)] = line
+
+            unfold(lambda cols: r_ref[h, :, :, cols], put_right)
+        a = a_ref[...].astype(jnp.bfloat16)
+        to = lax.broadcasted_iota(jnp.int32, (tall, tall), 0)
+        of = lax.broadcasted_iota(jnp.int32, (tall, tall), 1)
+        order = (of == lax.rem(to, side) * few + to // side).astype(jnp.float32).astype(jnp.bfloat16)
+        for h in range(2):
+            b = b_ref[h].astype(jnp.bfloat16)
+            b = jnp.dot(order, b, preferred_element_type=jnp.float32).astype(jnp.bfloat16)
+            y_ref[:, h * tall : (h + 1) * tall] = lax.dot_general(
+                a, b, (((1,), (1,)), ((), ())), preferred_element_type=jnp.float32
+            )
+
+        def fold(v, carry):
+            cols = pl.ds(pl.multiple_of(v * lanes, lanes), lanes)
+            y = y_ref[pl.ds(pl.multiple_of(v * per * few, per * few), per * few)]
+            for q in range(wide // lanes):
+                x = y[:, q * lanes : (q + 1) * lanes]
+                turned = [x] + [pltpu.roll(x, side * s, 1) for s in range(1, per)]
+                for m in range(per):
+                    piece = jnp.zeros((few, lanes), jnp.float32)
+                    for n in range(per):
+                        piece = jnp.where(
+                            lane == n, turned[(n - m) % per][n * few : (n + 1) * few], piece
+                        )
+                    o_ref[q * per + m, :, cols] = piece.astype(jnp.bfloat16)
+            return carry
+
+        lax.fori_loop(0, side // per, fold, 0)
+
+    out_shape = jax.ShapeDtypeStruct((blocks, few, tokens), jnp.bfloat16)
+    scratch = [
+        pltpu.VMEM((tall, wide), jnp.float32),
+        pltpu.VMEM((2, tall, wide), jnp.float32),
+        pltpu.VMEM((tall, wide), jnp.float32),
+    ]
+    return compute(kernel, out_shape, left, right, scratch=scratch)
+
+
 def triangle(tri_left, tri_right):
-    groups, few, tokens = tri_left.shape
-    side = int(tokens**0.5)
+    groups, deep, tokens = tri_left.shape
     at = lambda ref, k: ref.at[k]
-    split = (few, 2, GROUP // 2, tokens)
-    left, right = exchange("c", (tri_left, tri_right), (tri_left.shape,) * 2, [at] * 2, [at] * 2, 7)
-    left = jnp.transpose(left, (1, 0, 2)).reshape(split)
-    right = jnp.transpose(right, (1, 0, 2)).reshape(split)
-    left, right = exchange(
-        "b",
-        (left, right),
-        ((GROUP, *split[2:]), (GROUP, *split[1:])),
-        [lambda ref, k: ref.at[k // 2, lax.rem(k, 2)], lambda ref, k: ref.at[k // 2]],
-        [at] * 2,
-        8,
-    )
-    whole = GROUP * side
-    left = jnp.transpose(left.reshape(GROUP, GROUP // 2, side, side), (1, 2, 0, 3))
-    right = jnp.transpose(right.reshape(GROUP, GROUP, side, side), (1, 2, 0, 3))
-    mixed = lax.dot_general(
-        left.reshape(whole // 2, whole),
-        right.reshape(whole, whole),
-        (((1,), (1,)), ((), ())),
-        preferred_element_type=jnp.float32,
-    ).astype(jnp.bfloat16)
-    mixed = jnp.transpose(mixed.reshape(GROUP // 2, side, GROUP, side), (2, 0, 1, 3))
-    (mixed,) = exchange(
-        "b",
-        (mixed.reshape(GROUP, GROUP // 2, tokens),),
-        (split,),
-        [at],
-        [lambda ref, k: ref.at[k // 2, lax.rem(k, 2)]],
-        9,
-    )
-    mixed = jnp.transpose(mixed.reshape(few, GROUP, tokens), (1, 0, 2))
-    (mixed,) = exchange("c", (mixed,), ((GROUP, few, tokens),), [at], [at], 10)
-    return mixed.reshape(groups * few, tokens)
+    left, right = exchange("z", (tri_left, tri_right), (tri_left.shape,) * 2, [at] * 2, [at] * 2, 7)
+    left, right = exchange_channels(jnp.transpose(left, (1, 0, 2)), jnp.transpose(right, (1, 0, 2)))
+    mixed = multiply_channel(left, right)
+    (mixed,) = exchange("b", (mixed,), ((deep, groups, tokens),), [at], [at], 9)
+    mixed = jnp.transpose(mixed, (1, 0, 2))
+    (mixed,) = exchange("z", (mixed,), ((groups, deep, tokens),), [at], [at], 10)
+    return mixed.reshape(groups * deep, tokens)
 
 
 def layer_normalize(tensor):
@@ -438,16 +650,6 @@
     centre = tensor - jnp.mean(tensor, axis=-1, keepdims=True)
     spread = jnp.mean(centre * centre, axis=-1, keepdims=True)
     return centre * lax.rsqrt(spread + EPSILON)
-
-
-def split_blocks(normed, weights):
-    projected = jnp.dot(normed, weights, preferred_element_type=jnp.float32)
-    channel_count = weights.shape[0]
-    queries = (projected[..., :channel_count] * PER_HEAD_WIDTH ** (-0.5)).astype(jnp.bfloat16)
-    key_rows = projected[..., channel_count : 2 * channel_count].astype(jnp.bfloat16)
-    value_rows = projected[..., 2 * channel_count : 3 * channel_count].astype(jnp.bfloat16)
-    gating = jax.nn.sigmoid(projected[..., 3 * channel_count :])
-    return (queries, key_rows, value_rows, gating)
 
 
 def on_device(
@@ -496,13 +698,18 @@
     group_count = GROUP
     residue_piece = residue_total // group_count
     key_presence_mask = alignment_entry_mask.astype(jnp.bfloat16)
-    row_presence = jnp.pad(key_presence_mask[:, None, :], ((0, 0), (0, 7), (0, 96)))
+    ring_place = lax.axis_index("col_1")
+    row_presence = jnp.tile(key_presence_mask, (1, channel_count // residue_total))
+    row_lane = lax.broadcasted_iota(jnp.int32, row_presence.shape, 1) // residue_total
+    row_presence = jnp.where(row_lane == ring_place, row_presence, 0)
+    row_presence = jnp.pad(row_presence[:, None, :], ((0, 0), (0, 7), (0, 0)))
     col_presence = jnp.transpose(
         key_presence_mask.reshape(device_local_rows, group_count, residue_piece), (1, 2, 0)
     )
-    col_presence = jnp.pad(
-        col_presence, ((0, 0), (0, 8 - residue_piece), (0, 128 - device_local_rows))
-    )
+    col_presence = jnp.tile(col_presence, (1, 1, 128 // device_local_rows))
+    col_lane = lax.broadcasted_iota(jnp.int32, col_presence.shape, 2) // device_local_rows
+    col_presence = jnp.where(col_lane == lax.rem(col_place, 8), col_presence, 0)
+    col_presence = jnp.pad(col_presence, ((0, 0), (0, 8 - residue_piece), (0, 0)))
     bias_blocks, mask_cols = exchange(
         "b",
         (bias_tile, col_presence),
@@ -514,47 +721,15 @@
     pair_bias = jnp.transpose(
         bias_blocks.reshape(GROUP, HEADS, residue_total, pair_cols), (1, 2, 0, 3)
     ).reshape(HEADS, residue_total, GROUP * pair_cols)
-    mask_cols = jnp.transpose(
-        mask_cols[:, :residue_piece, :device_local_rows], (1, 0, 2)
-    ).reshape(residue_piece, GROUP * device_local_rows)
     row_normed_input = layer_normalize(homolog_embedding).astype(jnp.bfloat16)
-    full_bias, normed_whole, mask_whole = gather_bias_and_rows(
-        pair_bias, row_normed_input, row_presence
-    )
-    normed_whole = normed_whole[None]
-    mask_whole = mask_whole[:, 0, :residue_total].reshape(1, GROUP * residue_total)
-    full_bias = full_bias.astype(jnp.float32)
-    few_rows, all_residues = mask_whole.shape
-    queries, key_rows, value_rows, gating = split_blocks(normed_whole, row_projection_weights)
-    query_heads = queries.reshape(few_rows, all_residues, HEADS, PER_HEAD_WIDTH)
-    key_heads = key_rows.reshape(few_rows, all_residues, HEADS, PER_HEAD_WIDTH)
-    value_heads = value_rows.reshape(few_rows, all_residues, HEADS, PER_HEAD_WIDTH)
-    scores = (
-        jnp.einsum("sihd,sjhd->shij", query_heads, key_heads, preferred_element_type=jnp.float32)
-        + full_bias[None]
-    )
-    scores = jnp.where(mask_whole[:, None, None, :] > 0, scores, NEGATIVE)
-    highest = jnp.max(scores, axis=-1, keepdims=True)
-    powers = jnp.exp(scores - highest)
-    totals = jnp.sum(powers, axis=-1)
-    summed = jnp.einsum(
-        "shij,sjhd->sihd",
-        powers.astype(jnp.bfloat16),
-        value_heads,
-        preferred_element_type=jnp.float32,
-    )
-    attended = (summed / jnp.transpose(totals, (0, 2, 1))[..., None]).reshape(
-        few_rows, all_residues, channel_count
-    )
-    gated_whole = (attended * gating).astype(jnp.bfloat16)
-    (row_gated,) = exchange(
-        "c",
-        (gated_whole[0],),
-        ((GROUP, residue_total, channel_count),),
-        [lambda ref, k: ref.at[pl.ds(pl.multiple_of(k * residue_total, residue_total), residue_total)]],
-        [lambda ref, k: ref.at[k]],
-        2,
-    )
+    rows_sent = jnp.concatenate([row_normed_input, row_presence], axis=1)
+    full_bias, rows_whole = gather_bias_and_rows(
+        pair_bias, rows_sent.reshape(2, RING, *rows_sent.shape[1:])
+    )
+    gated_whole = row_attention(rows_whole, full_bias, row_projection_weights)
+    along = lambda ref, k: ref.at[:, k]
+    (row_gated,) = exchange("z", (gated_whole,), (gated_whole.shape,), [along], [along], 2)
+    row_gated = row_gated.reshape(device_local_rows, residue_total, channel_count)
     alignment_row_state = homolog_embedding.astype(jnp.float32) + jnp.dot(
         row_gated, horizontal_attend_merge, preferred_element_type=jnp.float32
     )
@@ -572,29 +747,7 @@
         [rows_of],
         3,
     )
-    residue_count, total_rows = mask_cols.shape
-    normed_flat = normed_cols
-    col_queries, col_keys, col_values, col_gating = split_blocks(
-        normed_flat, column_projection_weights
-    )
-    query_part = col_queries.reshape(residue_count, total_rows, HEADS, PER_HEAD_WIDTH)
-    key_part = col_keys.reshape(residue_count, total_rows, HEADS, PER_HEAD_WIDTH)
-    value_part = col_values.reshape(residue_count, total_rows, HEADS, PER_HEAD_WIDTH)
-    scores = jnp.einsum("ishd,ithd->ihst", query_part, key_part, preferred_element_type=jnp.float32)
-    scores = jnp.where(mask_cols[:, None, None, :] > 0, scores, NEGATIVE)
-    highest = jnp.max(scores, axis=-1, keepdims=True)
-    powers = jnp.exp(scores - highest)
-    totals = jnp.sum(powers, axis=-1)
-    summed = jnp.einsum(
-        "ihst,ithd->ihsd",
-        powers.astype(jnp.bfloat16),
-        value_part,
-        preferred_element_type=jnp.float32,
-    )
-    attended = jnp.transpose(summed / totals[..., None], (0, 2, 1, 3)).reshape(
-        residue_count, total_rows, channel_count
-    )
-    gated = (attended * col_gating).astype(jnp.bfloat16)
+    gated = column_attention(normed_cols, mask_cols, column_projection_weights)
     (returned,) = exchange(
         "b",
         (gated,),

time: 242 us -> 199 us (0.82)
  local copies, waits for them, and re-layouts: 41.1 us -> 7.1 us
  matrix products: 16.4 us -> 4.02 us
  Pallas kernels: 169 us -> 177 us
  other arithmetic: 13.4 us -> 9.13 us
    reshape x12 -> x1, local copies, waits for them, and re-layouts: 23.4 us -> 0.1 us  [on_device(): rows_sent.reshape(2, RING, *rows_sent.shape[1:])]
    pallas_call x0 -> x3, Pallas kernels: none -> 17.6 us  [compute(): pl.pallas_call(kernel, out_shape=out_shape, in_specs=[pl.BlockSpec(memory...]
    dot_general x7 -> x0, matrix products: 12.4 us -> none  [the longest x1 4.08 us: on_device(): jnp.einsum('sihd,sjhd->shij', query_heads, key_heads, preferred_element_t...]
    pallas_call x10, Pallas kernels: 164 us -> 154 us  [call_exchange(): pl.pallas_call(kernel, out_shape=out_shape, in_specs=[pl.BlockSpec(memory...]
    slice x6 -> x0, local copies, waits for them, and re-layouts: 6.37 us -> none  [the longest x4 4.44 us: split_blocks(): projected[..., channel_count:2 * channel_count].astype(jnp.bfloat16)]
    reduce_sum x2 -> x0, other arithmetic: 2.93 us -> none  [on_device(): totals = jnp.sum(powers, axis=-1)]
    convert_element_type x3 -> x0, local copies, waits for them, and re-layouts: 2.69 us -> none  [the longest x2 2.61 us: split_blocks(): (projected[..., :channel_count] * PER_HEAD_WIDTH ** (-0.5)).astype(jnp.bf...]
where the time goes in v3:
time: 199 us
  Pallas kernels  177 us (89%)
  other arithmetic  9.13 us (5%)
  local copies, waits for them, and re-layouts  7.1 us (4%)
  matrix products  4.02 us (2%)
    pallas_call x10, Pallas kernels, call_exchange(): pl.pallas_call(kernel, out_shape=out_shape, in_specs=[pl.BlockSpec(memory...  154 us
    pallas_call x3, Pallas kernels, compute(): pl.pallas_call(kernel, out_shape=out_shape, in_specs=[pl.BlockSpec(memory...  17.6 us
    pallas_call x1, Pallas kernels, pair_front(): pl.pallas_call(kernel, out_shape=[jax.ShapeDtypeStruct((channels, tokens)...  5.14 us

profile of v3, /device:TPU:1, one launch (start us, length us, event | category | flops | bytes accessed | tf_op | source)
XLA Modules:
  0.0 198.5 jit_solution(7880176324871459068)
XLA Ops:
  0.6 1.2 convert_reduce_fusion.1
  1.9 1.3 fusion.17
  3.2 1.3 fusion.18
  4.5 0.8 fusion.41
  5.5 0.9 fusion.7.refs_0_
  6.4 0.8 fusion.39
  7.4 11.4 %shard_map.194 = (bf16[16,8,1024]{2,1,0:T(8,128)(2,1)S(1)}, bf16[16,8,128]{2,1,0:T(8,128)(2,1)S(1)}) custom-call(bf16[8,1024]{1,0:T(8,128)(2,1)S(1)} %fusion.7.refs_0_, bf16[16,8,128]{2,1,0:T(8,128)(2,1)S(1)} %pad.8.refs_1_), custom_call_target="tpu_custom_call" | custom-call | bytes 524288 | tf_op jit(solution)/shard_map/pallas_call | solution.py:42
  18.8 0.8 reshape.259
  19.6 0.7 copy.108
  20.3 1.0 reshape.260.b_ref
  21.4 1.2 convert_reduce_fusion
  22.6 1.2 fusion.15
  24.2 33.4 %shard_map.195 = (bf16[8,256,512]{2,1,0:T(8,128)(2,1)S(1)}, bf16[2,16,40,256]{3,2,1,0:T(8,128)(2,1)S(1)}) custom-call(bf16[8,32,512]{2,1,0:T(8,128)(2,1)S(1)} %reshape.260.b_ref, bf16[2,8,40,256]{3,2,1,0:T(8,128)(2,1)S(1)} %copy.63.r_ref), custom_call_target="tpu_custom_call" | custom-call | bytes 4194304 | tf_op jit(solution)/shard_map/pallas_call | solution.py:42
  57.6 9.7 %shard_map.196.refs_0_ = bf16[2,8,32,256]{3,2,1,0:T(8,128)(2,1)S(1)} custom-call(bf16[2,16,40,256]{3,2,1,0:T(8,128)(2,1)S(1)} %get-tuple-element.17.r_ref, bf16[8,256,512]{2,1,0:T(8,128)(2,1)S(1)} %get-tuple-element.18.b_ref, bf16[256,1024]{1,0:T(8,128)(2,1)S(1)} %copy-done.1), custom_call_target="tpu_custom_call" | custom-call | tf_op jit(solution)/shard_map/pallas_call | solution.py:234
  67.4 9.0 %shard_map.197 = bf16[2,8,32,256]{3,2,1,0:T(8,128)(2,1)S(1)} custom-call(bf16[2,8,32,256]{3,2,1,0:T(8,128)(2,1)S(1)} %shard_map.196.refs_0_), custom_call_target="tpu_custom_call" | custom-call | bytes 524288 | tf_op jit(solution)/shard_map/pallas_call | solution.py:42
  76.4 0.4 fusion.42
  77.3 11.4 %shard_map.198.c_ref = bf16[2,256,256]{2,1,0:T(8,128)(2,1)S(1)} custom-call(bf16[32,16,256]{2,1,0:T(8,128)(2,1)S(1)} %fusion.25.refs_0_), custom_call_target="tpu_custom_call" | custom-call | bytes 524288 | tf_op jit(solution)/shard_map/pallas_call | solution.py:42
  88.7 4.0 %shard_map.199.refs_0_ = bf16[2,256,256]{2,1,0:T(8,128)(2,1)S(1)} custom-call(bf16[2,256,256]{2,1,0:T(8,128)(2,1)S(1)} %shard_map.198.c_ref, bf16[16,8,128]{2,1,0:T(8,128)(2,1)S(1)} %get-tuple-element.19.p_ref, bf16[256,1024]{1,0:T(8,128)(2,1)S(1)} %copy-done.2), custom_call_target="tpu_custom_call" | custom-call | tf_op jit(solution)/shard_map/pallas_call | solution.py:234
  92.7 8.7 %shard_map.200 = bf16[32,16,256]{2,1,0:T(8,128)(2,1)S(1)} custom-call(bf16[2,256,256]{2,1,0:T(8,128)(2,1)S(1)} %shard_map.199.refs_0_), custom_call_target="tpu_custom_call" | custom-call | bytes 524288 | tf_op jit(solution)/shard_map/pallas_call | solution.py:42
  101.4 0.3 fusion.43
  102.2 0.4 maximum_convert_fusion.1
  102.7 0.8 fusion.44
  104.0 0.8 copy.79
  105.6 22.6 %shard_map.201 = (bf16[256,1024]{1,0:T(8,128)(2,1)S(1)}, bf16[256,1024]{1,0:T(8,128)(2,1)S(1)}) custom-call(bf16[16,1024]{1,0:T(8,128)(2,1)S(1)} %reshape.263.l_ref, bf16[16,1024]{1,0:T(8,128)(2,1)S(1)} %reshape.264.r_ref), custom_call_target="tpu_custom_call" | custom-call | bytes 2097152 | tf_op jit(solution)/shard_map/pallas_call | solution.py:42
  128.9 5.1 %shard_map.202 = (f32[128,1024]{1,0:T(8,128)S(1)}, bf16[8,16,1024]{2,1,0:T(8,128)(2,1)S(1)}, bf16[8,16,1024]{2,1,0:T(8,128)(2,1)S(1)}, f32[128,1024]{1,0:T(8,128)S(1)}) custom-call(bf16[256,1024]{1,0:T(8,128)(2,1)S(1)} %get-tuple-element.20.l_ref, bf16[256,1024]{1,0:T(8,128)(2,1)S(1)} %get-tuple-element.21.r_ref, bf16[128,1024]{1,0:T(8,128)(2,1)S(1)} %bitcast.88, ...), custom_call_target="tpu_custom_call" | custom-call | tf_op jit(solution)/shard_map/pallas_call | solution.py:498
  134.1 17.9 %shard_map.203 = (bf16[8,16,1024]{2,1,0:T(8,128)(2,1)S(1)}, bf16[8,16,1024]{2,1,0:T(8,128)(2,1)S(1)}) custom-call(bf16[8,16,1024]{2,1,0:T(8,128)(2,1)S(1)} %get-tuple-element.24.refs_0_, bf16[8,16,1024]{2,1,0:T(8,128)(2,1)S(1)} %get-tuple-element.25.refs_1_), custom_call_target="tpu_custom_call" | custom-call | bytes 524288 | tf_op jit(solution)/shard_map/pallas_call | solution.py:42
  152.3 20.6 %shard_map.204 = (bf16[16,8,1024]{2,1,0:T(8,128)(2,1)S(1)}, bf16[2,16,8,1024]{3,2,1,0:T(8,128)(2,1)S(1)}) custom-call(bf16[16,8,1024]{2,1,0:T(8,128)(2,1)S(1)} %bitcast.85, bf16[16,8,1024]{2,1,0:T(8,128)(2,1)S(1)} %bitcast.86), custom_call_target="tpu_custom_call" | custom-call | bytes 2097152 | tf_op jit(solution)/shard_map/pallas_call | solution.py:42
  172.8 3.9 %shard_map.205.refs_0_ = bf16[16,8,1024]{2,1,0:T(8,128)(2,1)S(1)} custom-call(bf16[16,8,1024]{2,1,0:T(8,128)(2,1)S(1)} %get-tuple-element.28.l_ref, bf16[2,16,8,1024]{3,2,1,0:T(8,128)(2,1)S(1)} %get-tuple-element.29.r_ref), custom_call_target="tpu_custom_call" | custom-call | tf_op jit(solution)/shard_map/pallas_call | solution.py:234
  176.8 8.1 %shard_map.206 = bf16[16,8,1024]{2,1,0:T(8,128)(2,1)S(1)} custom-call(bf16[16,8,1024]{2,1,0:T(8,128)(2,1)S(1)} %shard_map.205.refs_0_), custom_call_target="tpu_custom_call" | custom-call | bytes 524288 | tf_op jit(solution)/shard_map/pallas_call | solution.py:42
  185.0 11.2 %shard_map.207 = bf16[8,16,1024]{2,1,0:T(8,128)(2,1)S(1)} custom-call(bf16[8,16,1024]{2,1,0:T(8,128)(2,1)S(1)} %bitcast.87), custom_call_target="tpu_custom_call" | custom-call | bytes 524288 | tf_op jit(solution)/shard_map/pallas_call | solution.py:42
  196.9 0.8 fusion.4
  197.7 0.8 copy.78
  (87 shorter events, 4.8 us)
Async XLA Ops:
  0.6 101.5 %copy-start = (bf16[256,1024]{1,0:T(8,128)(2,1)S(1)}, bf16[256,1024]{1,0:T(8,128)(2,1)}, u32[]{:S(2)}) copy-start(bf16[256,1024]{1,0:T(8,128)(2,1)} %param.30) | copy-start | bytes 1572868
  20.3 3.6 %copy-start.5 = (bf16[16,32,256]{2,1,0:T(8,128)(2,1)S(1)}, bf16[16,32,256]{2,1,0:T(8,128)(2,1)}, u32[]{:S(2)}) copy-start(bf16[16,32,256]{2,1,0:T(8,128)(2,1)} %param.19) | copy-start | bytes 786436
  20.3 37.3 %copy-start.1 = (bf16[256,1024]{1,0:T(8,128)(2,1)S(1)}, bf16[256,1024]{1,0:T(8,128)(2,1)}, u32[]{:S(2)}) copy-start(bf16[256,1024]{1,0:T(8,128)(2,1)} %w_ref.3) | copy-start | bytes 1572868
  57.6 18.7 %copy-start.8 = (bf16[256,256]{1,0:T(8,128)(2,1)S(1)}, bf16[256,256]{1,0:T(8,128)(2,1)}, u32[]{:S(2)}) copy-start(bf16[256,256]{1,0:T(8,128)(2,1)} %param.25) | copy-start | bytes 393220
  67.4 21.3 %copy-start.2 = (bf16[256,1024]{1,0:T(8,128)(2,1)S(1)}, bf16[256,1024]{1,0:T(8,128)(2,1)}, u32[]{:S(2)}) copy-start(bf16[256,1024]{1,0:T(8,128)(2,1)} %w_ref.4) | copy-start | bytes 1572868
  76.4 25.0 %copy-start.9 = (bf16[256,256]{1,0:T(8,128)(2,1)S(1)}, bf16[256,256]{1,0:T(8,128)(2,1)}, u32[]{:S(2)}) copy-start(bf16[256,256]{1,0:T(8,128)(2,1)} %param.29) | copy-start | bytes 393220
  101.4 1.3 copy-start.6
  102.6 2.1 %copy-start.14 = (bf16[256,64]{0,1:T(8,128)(2,1)S(1)}, bf16[256,64]{0,1:T(8,128)(2,1)}, u32[]{:S(2)}) copy-start(bf16[256,64]{0,1:T(8,128)(2,1)} %param.32) | copy-start | bytes 98308
  103.4 24.8 %copy-start.4 = (bf16[32,32,128]{2,1,0:T(8,128)(2,1)S(1)}, bf16[32,32,128]{2,1,0:T(8,128)(2,1)}, u32[]{:S(2)}) copy-start(bf16[32,32,128]{2,1,0:T(8,128)(2,1)} %param.20) | copy-start | bytes 786436
  103.5 24.9 %copy-start.7 = (bf16[1024,128]{1,0:T(8,128)(2,1)S(1)}, bf16[1024,128]{1,0:T(8,128)(2,1)}, u32[]{:S(2)}) copy-start(bf16[1024,128]{1,0:T(8,128)(2,1)} %param.33) | copy-start | bytes 786436
  104.0 24.7 %copy-start.11 = (s32[512]{0:T(512)S(1)}, s32[512]{0:T(512)}, u32[]{:S(2)}) copy-start(s32[512]{0:T(512)} %param.22) | copy-start | bytes 6148
  104.0 25.0 %copy-start.3 = (bf16[128,640]{1,0:T(8,128)(2,1)S(1)}, bf16[128,640]{1,0:T(8,128)(2,1)}, u32[]{:S(2)}) copy-start(bf16[128,640]{1,0:T(8,128)(2,1)} %w_ref.5) | copy-start | bytes 491524
  152.3 44.3 %copy-start.10 = (bf16[128,128]{1,0:T(8,128)(2,1)S(1)}, bf16[128,128]{1,0:T(8,128)(2,1)}, u32[]{:S(2)}) copy-start(bf16[128,128]{1,0:T(8,128)(2,1)} %param.35) | copy-start | bytes 98308
  185.0 11.9 %copy-start.12 = (bf16[512,128]{1,0:T(8,128)(2,1)S(1)}, bf16[512,128]{1,0:T(8,128)(2,1)}, u32[]{:S(2)}) copy-start(bf16[512,128]{1,0:T(8,128)(2,1)} %param.37) | copy-start | bytes 393220
  185.0 11.9 %copy-start.13 = (bf16[128,512]{1,0:T(8,128)(2,1)S(1)}, bf16[128,512]{1,0:T(8,128)(2,1)}, u32[]{:S(2)}) copy-start(bf16[128,512]{1,0:T(8,128)(2,1)} %param.36) | copy-start | bytes 393220

commit v4 on v3

--- a/solution.py
+++ b/solution.py
@@ -134,40 +134,100 @@
     return (br, ro, 1 - x, z)
 
 
-def gather_bias_and_rows(bias, rows):
-    heads, some, all_ = bias.shape
+def normal(x):
+    x = x.astype(jnp.float32)
+    centre = x - jnp.mean(x, axis=-1, keepdims=True)
+    spread = jnp.mean(centre * centre, axis=-1, keepdims=True)
+    return (centre * lax.rsqrt(spread + EPSILON)).astype(jnp.bfloat16)
+
+
+def gather_bias_and_rows(pair, weights, same, chain_bias, entries, presence, col_presence):
+    some, others, pair_channels = pair.shape
+    heads = weights.shape[1]
+    msa_rows, _, channels = entries.shape
     carried = heads // 2
-    pair, _, tall, channels = rows.shape
+    tall = some + 8
+    lanes = 128
+    fold = lanes // others
     n_copies = 32
 
-    def kernel(b_ref, r_ref, ob_ref, or_ref, psend, precv, xsend, xrecv, rsend, rrecv):
+    def kernel(
+        p_ref, w_ref, s_ref, h_ref, e_ref, k_ref, m_ref, ob_ref, or_ref, om_ref,
+        turn, tile, tiles, rows, bsend, brecv, psend, precv, xsend, xrecv, rsend, rrecv,
+    ):
         br, ro, x, z, _, c = place()
         core = lax.rem(ro, 2)
         right = (br, ro, x, lax.rem(z + 1, RING))
         left = (br, ro, x, lax.rem(z + RING - 1, RING))
         twin = (br, ro + 1 - 2 * core, x, z)
         cross = crosswise()
+        at = lambda ref, k: ref.at[k]
         put = lambda ref, k: ref.at[:, x * RING + k]
-        pushes = Pushes("z", (r_ref,), (or_ref,), [lambda ref, k: ref.at[:, k]], [put], psend, precv)
+        spread = Pushes("b", (tile, m_ref), (tiles, om_ref), [lambda ref, k: ref, at], [at] * 2, bsend, brecv)
+        pushes = Pushes("z", (rows,), (or_ref,), [lambda ref, k: ref.at[:, k]], [put], psend, precv)
         barrier = pltpu.get_barrier_semaphore()
+        spread.greet(barrier)
         pushes.greet(barrier)
-        for device in (twin, cross):
-            pl.semaphore_signal(barrier, inc=1, device_id=device, device_id_type=MESH)
-        pl.semaphore_wait(barrier, RING - 1 + 2)
+        pl.semaphore_signal(barrier, inc=1, device_id=cross, device_id_type=MESH)
+
+        normed = normal(p_ref[...].reshape(some * others, pair_channels))
+        for low in range(8):
+            tokens = jnp.concatenate(
+                [normed[(high * 8 + low) * others :][:others] for high in range(fold)], axis=0
+            )
+            bias = lax.dot_general(
+                w_ref[...], tokens, (((0,), (1,)), ((), ())), preferred_element_type=jnp.float32
+            )
+            turn[low * heads : (low + 1) * heads] = bias + h_ref[...] * s_ref[low : low + 1]
+        for head in range(heads):
+            tile[head] = turn[pl.ds(head, 8, stride=heads)].astype(jnp.bfloat16)
+        pl.semaphore_wait(barrier, GROUP - 1 + RING - 1 + 1)
+        spread.start()
+        normed = normal(e_ref[...].reshape(msa_rows * some, channels))
+        for half in range(2):
+            for k in range(RING):
+                row = half * RING + k
+                rows[half, k, :some] = normed[row * some : (row + 1) * some]
+                rows[half, k, some:] = k_ref[row]
+        pushes.start()
+        first = remote(rows.at[:, z], or_ref.at[:, c], xsend.at[0], xrecv.at[0], cross)
+        first.start()
+        spread.finish()
+        lane = lax.broadcasted_iota(jnp.int32, (8, lanes), 1) // others
+
+        def set_out(head, carry):
+            t = tiles[:, head].astype(jnp.float32).reshape(GROUP * 8, lanes)
+            turned = [t] + [pltpu.roll(t, others * s, 1) for s in range(1, fold)]
+            lines = []
+            for n in range(fold):
+                line = []
+                for q in range(GROUP // fold):
+                    piece = jnp.zeros((8, lanes), jnp.float32)
+                    for m in range(fold):
+                        k = (q * fold + m) * 8
+                        piece = jnp.where(lane == m, turned[(m - n) % fold][k : k + 8], piece)
+                    line.append(piece)
+                lines.append(jnp.concatenate(line, axis=1))
+            whole = jnp.concatenate(lines, axis=0).astype(jnp.bfloat16)
+            ob_ref[head, pl.ds(pl.multiple_of(z * some, some), some)] = whole
+            return carry
+
+        lax.fori_loop(0, heads, set_out, 0)
 
         def view(block, half, mine):
-            first, count = mine * carried, carried
+            at_head, count = mine * carried, carried
             if half is not None:
                 count = carried // 2
-                first = first + half * count
+                at_head = at_head + half * count
             rows_at = pl.multiple_of(lax.rem(block + RING, RING) * some, some)
-            return ob_ref.at[pl.ds(first, count), pl.ds(rows_at, some)]
+            return ob_ref.at[pl.ds(at_head, count), pl.ds(rows_at, some)]
 
         copies, handed = [], []
 
-        def push(src, block, half, to):
+        def push(block, half, to):
             k = len(copies)
-            copies.append(remote(src, view(block, half, core), rsend.at[k], rrecv.at[k], to))
+            there = view(block, half, core)
+            copies.append(remote(there, there, rsend.at[k], rrecv.at[k], to))
             copies[-1].start()
             return k
 
@@ -176,32 +236,27 @@
             remote(there, there, rsend.at[k], rrecv.at[k], right).wait_recv()
 
         def hand(block, half):
-            handed.append((push(view(block, half, core), block, half, twin), block, half))
+            handed.append((push(block, half, twin), block, half))
 
         def over(d, coming):
             k = pushes.sender(d)
-            place_at = (1 - x if coming else x) * RING + k
-            there = or_ref.at[:, place_at]
+            there = or_ref.at[:, (1 - x if coming else x) * RING + k]
             return remote(there, there, xsend.at[d], xrecv.at[d], cross)
 
-        mine = b_ref.at[pl.ds(core * carried, carried)]
-        pushes.start()
-        going = {+1: push(mine, z, None, right), -1: push(mine, z, None, left)}
-        first = remote(r_ref.at[:, z], or_ref.at[:, c], xsend.at[0], xrecv.at[0], cross)
-        first.start()
-        ob_ref[:, pl.ds(pl.multiple_of(z * some, some), some)] = b_ref[...]
         for step in (1, 2, 3):
+            for d in (step, RING - step):
+                pushes.arrive(d)
+                over(d, False).start()
+            if step == 1:
+                going = {+1: push(z, None, right), -1: push(z, None, left)}
             coming = {}
             for way, to in ((+1, right), (-1, left)):
                 block = z - way * step
                 arrived(going[way], block, None)
                 half = None if step < 3 else (0 if way > 0 else 1)
-                coming[way] = push(view(block, half, core), block, half, to)
+                coming[way] = push(block, half, to)
                 hand(block, None)
             going = coming
-            for d in (step, RING - step):
-                pushes.arrive(d)
-                over(d, False).start()
         pushes.arrive(4)
         over(4, False).start()
         for way in (+1, -1):
@@ -220,14 +275,26 @@
             pushes.sent(d)
             over(d, False).wait_send()
 
+    wide = GROUP * others
     out_shape = [
-        jax.ShapeDtypeStruct((heads, RING * some, all_), jnp.bfloat16),
-        jax.ShapeDtypeStruct((pair, GROUP, tall, channels), jnp.bfloat16),
+        jax.ShapeDtypeStruct((heads, RING * some, wide), jnp.bfloat16),
+        jax.ShapeDtypeStruct((2, GROUP, tall, channels), jnp.bfloat16),
+        jax.ShapeDtypeStruct(col_presence.shape, jnp.bfloat16),
     ]
-    scratch = [pltpu.SemaphoreType.DMA((1, RING))] * 2
+    scratch = [
+        pltpu.VMEM((8 * heads, lanes), jnp.float32),
+        pltpu.VMEM((heads, 8, lanes), jnp.bfloat16),
+        pltpu.VMEM((GROUP, heads, 8, lanes), jnp.bfloat16),
+        pltpu.VMEM((2, RING, tall, channels), jnp.bfloat16),
+    ]
+    scratch += [pltpu.SemaphoreType.DMA((2, GROUP))] * 2
+    scratch += [pltpu.SemaphoreType.DMA((1, RING))] * 2
     scratch += [pltpu.SemaphoreType.DMA((RING,))] * 2
     scratch += [pltpu.SemaphoreType.DMA((n_copies,))] * 2
-    return call_exchange(kernel, out_shape, scratch, 1, 2 << 20, bias, rows)
+    return call_exchange(
+        kernel, out_shape, scratch, 1, 2 << 20,
+        pair, weights, same, chain_bias, entries, presence, col_presence,
+    )
 
 
 def compute(kernel, out_shape, *args, scratch=(), limit=40):
@@ -351,71 +418,132 @@
 
 
 def gather_factors(left, right):
-    rows = left.shape[0]
-
-    def kernel(l_ref, r_ref, ol_ref, or_ref, lsend, lrecv, rsend, rrecv):
+    rows, wide = left.shape
+    chips = GROUP // 2
+
+    def kernel(l_ref, r_ref, ol_ref, or_ref, stage, zsend, zrecv, lsend, lrecv, tsend, trecv, fsend, frecv):
+        br, ro, x, z, b, _ = place()
+        core = lax.rem(ro, 2)
+        chip = b // 2
+        twin = (br, ro + 1 - 2 * core, x, z)
         put = lambda ref, k: ref.at[pl.ds(pl.multiple_of(k * rows, rows), rows)]
-        b, c = place()[4:]
-        pushes = Pushes("b", (l_ref,), (ol_ref,), [lambda ref, k: ref], [put], lsend, lrecv)
+        at = lambda ref, k: ref.at[k]
+        pushes = Pushes("z", (r_ref,), (stage,), [lambda ref, k: ref], [at], zsend, zrecv)
+        on_core = lambda k: across(k * 2 + core, x * RING + z)
+        back = lambda d: lax.rem(chip + chips - d, chips)
+        own = br == x
         barrier = pltpu.get_barrier_semaphore()
         pushes.greet(barrier)
 
-        def others(act):
+        def signal(to):
+            pl.semaphore_signal(barrier, inc=1, device_id=to, device_id_type=MESH)
+
+        def greet(d, carry):
+            signal(on_core(lax.rem(chip + d, chips)))
+            return carry
+
+        lax.fori_loop(1, chips, greet, 0)
+        signal(twin)
+
+        def each(act):
             def one(d, carry):
-                k = lax.rem(c + d, GROUP)
-
-                @pl.when(jnp.logical_or(b != c, k != c))
+                for other in range(2):
+                    act(lax.rem(ro + d, RING), other)
+                return carry
+
+            lax.fori_loop(0, RING, one, 0)
+
+        def senders(act):
+            def one(k, other):
+                @pl.when(jnp.logical_not(jnp.logical_and(own, jnp.logical_and(k == ro, br == other))))
                 def _():
-                    act(k)
-
-                return carry
-
-            lax.fori_loop(0, GROUP, one, 0)
-
-        def senders(act):
-            def one(d, carry):
-                k = lax.rem(b + d, GROUP)
-
-                @pl.when(jnp.logical_or(b != c, k != b))
+                    act(k, other)
+
+            each(one)
+
+        senders(lambda k, other: signal((other, k, br, z)))
+        pl.semaphore_wait(
+            barrier, RING - 1 + chips - 1 + 1 + jnp.where(own, GROUP - 1, GROUP)
+        )
+
+        def to_chip(d, coming):
+            block = back(d) * 2 + core if coming else b
+            peer = back(d) if coming else lax.rem(chip + d, chips)
+            return remote(l_ref, put(ol_ref, block), lsend.at[d], lrecv.at[d], on_core(peer))
+
+        def to_twin(d, coming):
+            block = put(ol_ref, back(d) * 2 + (1 - core if coming else core))
+            return remote(block, block, tsend.at[d], trecv.at[d], twin)
+
+        def forward(k, other, src):
+            return remote(src, put(or_ref, b), fsend.at[k, other], frecv.at[b], (x, k, other, z))
+
+        def forward_all(k, src):
+            for other in range(2):
+                mine = jnp.logical_and(own, jnp.logical_and(k == ro, x == other))
+
+                @pl.when(jnp.logical_not(mine))
                 def _():
-                    act(k)
-
-                return carry
-
-            lax.fori_loop(0, GROUP, one, 0)
-
-        others(
-            lambda k: pl.semaphore_signal(
-                barrier, inc=1, device_id=across(c, k), device_id_type=MESH
-            )
-        )
-        senders(
-            lambda k: pl.semaphore_signal(
-                barrier, inc=1, device_id=across(k, b), device_id_type=MESH
-            )
-        )
-        pl.semaphore_wait(barrier, GROUP - 1 + 2 * jnp.where(b == c, GROUP - 1, GROUP))
-
-        def copy(k):
-            return remote(r_ref, put(or_ref, b), rsend.at[k], rrecv.at[b], across(c, k))
-
-        def coming(k):
-            there = put(or_ref, k)
-            return remote(r_ref, there, rsend.at[k], rrecv.at[k], across(k, b))
-
-        others(lambda k: copy(k).start())
-        pushes.start()
-
-        @pl.when(b == c)
-        def _():
-            put(or_ref, b)[...] = r_ref[...]
-
-        pushes.finish()
-        senders(lambda k: coming(k).wait_recv())
-        others(lambda k: copy(k).wait_send())
-
-    shape = jax.ShapeDtypeStruct((GROUP * rows, left.shape[1]), jnp.bfloat16)
-    scratch = [pltpu.SemaphoreType.DMA((1, GROUP))] * 2 + [pltpu.SemaphoreType.DMA((GROUP,))] * 2
+                    forward(k, other, src).start()
+
+                @pl.when(mine)
+                def _():
+                    put(or_ref, b)[...] = src[...]
+
+        def start(d, carry):
+            for copy in pushes.copies(d, False):
+                copy.start()
+            to_chip(d, False).start()
+            return carry
+
+        lax.fori_loop(1, RING, start, 0)
+        first = remote(l_ref, put(ol_ref, b), tsend.at[0], trecv.at[0], twin)
+        first.start()
+        forward_all(z, r_ref)
+        put(ol_ref, b)[...] = l_ref[...]
+
+        def relay(d, carry):
+            pushes.arrive(d)
+            k = pushes.sender(d)
+            forward_all(k, stage.at[k])
+            to_chip(d, True).wait_recv()
+            to_twin(d, False).start()
+            return carry
+
+        lax.fori_loop(1, RING, relay, 0)
+
+        def last(d, carry):
+            pushes.sent(d)
+            to_chip(d, False).wait_send()
+            to_twin(d, True).wait_recv()
+            to_twin(d, False).wait_send()
+            return carry
+
+        lax.fori_loop(1, RING, last, 0)
+        to_twin(0, True).wait_recv()
+        first.wait_send()
+
+        def sent(k, other):
+            mine = jnp.logical_and(own, jnp.logical_and(k == ro, x == other))
+
+            @pl.when(jnp.logical_not(mine))
+            def _():
+                forward(k, other, r_ref).wait_send()
+
+        each(sent)
+
+        def come(k, other):
+            sender = other * RING + k
+            there = put(or_ref, sender)
+            remote(r_ref, there, fsend.at[k, other], frecv.at[sender], (other, k, br, z)).wait_recv()
+
+        senders(come)
+
+    shape = jax.ShapeDtypeStruct((GROUP * rows, wide), jnp.bfloat16)
+    scratch = [pltpu.VMEM((RING, rows, wide), jnp.bfloat16)]
+    scratch += [pltpu.SemaphoreType.DMA((1, RING))] * 2
+    scratch += [pltpu.SemaphoreType.DMA((RING,))] * 4
+    scratch += [pltpu.SemaphoreType.DMA((RING, 2)), pltpu.SemaphoreType.DMA((GROUP,))]
     return call_exchange(kernel, [shape, shape], scratch, 6, 1 << 20, left, right)
 
 
@@ -684,17 +812,6 @@
     residue_keep = residue_presence_mask.astype(jnp.float32)
     keep_here = lax.dynamic_slice_in_dim(residue_keep, row_place * residue_total, residue_total)
     keep_there = lax.dynamic_slice_in_dim(residue_keep, col_place * pair_cols, pair_cols)
-    pair_normed = layer_normalize(pair_representation).astype(jnp.bfloat16)
-    same_chain = (chain_here[:, None] == chain_there[None, :]).astype(jnp.float32)
-    weights = lax.dot_general(
-        pair_bias_matrix,
-        pair_normed.reshape(residue_total * pair_cols, -1),
-        (((0,), (1,)), ((), ())),
-        preferred_element_type=jnp.float32,
-    )
-    bias_tile = (
-        weights + same_chain_bias[:, None] * same_chain.reshape(1, residue_total * pair_cols)
-    ).astype(jnp.bfloat16)
     group_count = GROUP
     residue_piece = residue_total // group_count
     key_presence_mask = alignment_entry_mask.astype(jnp.bfloat16)
@@ -710,21 +827,16 @@
     col_lane = lax.broadcasted_iota(jnp.int32, col_presence.shape, 2) // device_local_rows
     col_presence = jnp.where(col_lane == lax.rem(col_place, 8), col_presence, 0)
     col_presence = jnp.pad(col_presence, ((0, 0), (0, 8 - residue_piece), (0, 0)))
-    bias_blocks, mask_cols = exchange(
-        "b",
-        (bias_tile, col_presence),
-        ((GROUP, *bias_tile.shape), col_presence.shape),
-        [lambda ref, k: ref, lambda ref, k: ref.at[k]],
-        [lambda ref, k: ref.at[k]] * 2,
-        0,
-    )
-    pair_bias = jnp.transpose(
-        bias_blocks.reshape(GROUP, HEADS, residue_total, pair_cols), (1, 2, 0, 3)
-    ).reshape(HEADS, residue_total, GROUP * pair_cols)
-    row_normed_input = layer_normalize(homolog_embedding).astype(jnp.bfloat16)
-    rows_sent = jnp.concatenate([row_normed_input, row_presence], axis=1)
-    full_bias, rows_whole = gather_bias_and_rows(
-        pair_bias, rows_sent.reshape(2, RING, *rows_sent.shape[1:])
+    low_first = jnp.transpose(chain_here.reshape(residue_total // 8, 8))
+    same_chain = (low_first[:, :, None] == chain_there[None, None, :]).astype(jnp.float32)
+    full_bias, rows_whole, mask_cols = gather_bias_and_rows(
+        pair_representation,
+        pair_bias_matrix,
+        same_chain.reshape(8, residue_total // 8 * pair_cols),
+        same_chain_bias[:, None],
+        homolog_embedding,
+        row_presence,
+        col_presence,
     )
     gated_whole = row_attention(rows_whole, full_bias, row_projection_weights)
     along = lambda ref, k: ref.at[:, k]

time: 199 us -> 186 us (0.935)
  Pallas kernels: 177 us -> 169 us
  other arithmetic: 9.13 us -> 2.59 us
  local copies, waits for them, and re-layouts: 7.1 us -> 9.45 us
    pallas_call x10 -> x9, Pallas kernels: 154 us -> 147 us  [call_exchange(): pl.pallas_call(kernel, out_shape=out_shape, in_specs=[pl.BlockSpec(memory...]
    unnamed x31 -> x36, local copies, waits for them, and re-layouts: 0.88 us -> 4.7 us
    reduce_sum x5 -> x3, other arithmetic: 3.26 us -> 0.72 us  [layer_normalize(): spread = jnp.mean(centre * centre, axis=-1, keepdims=True)]
    reshape x4 -> x1, local copies, waits for them, and re-layouts: 2.56 us -> 0.08 us  [on_device(): low_first = jnp.transpose(chain_here.reshape(residue_total // 8, 8))]
    reduce_sum x2 -> x0, other arithmetic: 2.38 us -> none  [layer_normalize(): centre = tensor - jnp.mean(tensor, axis=-1, keepdims=True)]
where the time goes in v4:
time: 186 us
  Pallas kernels  169 us (91%)
  local copies, waits for them, and re-layouts  9.45 us (5%)
  matrix products  3.18 us (2%)
  other arithmetic  2.59 us (1%)
    pallas_call x9, Pallas kernels, call_exchange(): pl.pallas_call(kernel, out_shape=out_shape, in_specs=[pl.BlockSpec(memory...  147 us
    pallas_call x3, Pallas kernels, compute(): pl.pallas_call(kernel, out_shape=out_shape, in_specs=[pl.BlockSpec(memory...  17.6 us
    pallas_call x1, Pallas kernels, pair_front(): pl.pallas_call(kernel, out_shape=[jax.ShapeDtypeStruct((channels, tokens)...  5.14 us
    unnamed x36, local copies, waits for them, and re-layouts  4.7 us

profile of v4, /device:TPU:1, one launch (start us, length us, event | category | flops | bytes accessed | tf_op | source)
XLA Modules:
  0.0 185.8 jit_solution(18112769011466343753)
XLA Ops:
  0.6 0.9 copy.67.w_ref
  1.5 0.8 fusion.27
  2.8 0.7 copy.68.h_ref
  3.5 0.8 fusion.25
  4.8 0.9 copy-done.1
  5.7 0.9 copy-done.3
  6.6 37.7 %shard_map.194 = (bf16[8,256,512]{2,1,0:T(8,128)(2,1)S(1)}, bf16[2,16,40,256]{3,2,1,0:T(8,128)(2,1)S(1)}, bf16[16,8,128]{2,1,0:T(8,128)(2,1)S(1)}) custom-call(bf16[32,32,128]{2,1,0:T(8,128)(2,1)S(1)} %copy-done.1, bf16[128,8]{1,0:T(8,128)(2,1)S(1)} %copy.67.w_ref, f32[8,128]{1,0:T(8,128)S(1)} %compare_convert_fusion.s_ref, f32[8,1]{1,0:T(8,128)S(1)} %copy.68.h_ref, ...), custom_call_target="tpu_custom_call" | custom-call | bytes 4194304 | tf_op jit(solution)/shard_map/pallas_call | solution.py:42
  44.4 1.1 copy-done.5
  45.5 9.8 %shard_map.195.refs_0_ = bf16[2,8,32,256]{3,2,1,0:T(8,128)(2,1)S(1)} custom-call(bf16[2,16,40,256]{3,2,1,0:T(8,128)(2,1)S(1)} %get-tuple-element.15.r_ref, bf16[8,256,512]{2,1,0:T(8,128)(2,1)S(1)} %get-tuple-element.16.b_ref, bf16[256,1024]{1,0:T(8,128)(2,1)S(1)} %copy-done.5), custom_call_target="tpu_custom_call" | custom-call | tf_op jit(solution)/shard_map/pallas_call | solution.py:301
  55.3 14.1 %shard_map.196 = bf16[2,8,32,256]{3,2,1,0:T(8,128)(2,1)S(1)} custom-call(bf16[2,8,32,256]{3,2,1,0:T(8,128)(2,1)S(1)} %shard_map.195.refs_0_), custom_call_target="tpu_custom_call" | custom-call | bytes 524288 | tf_op jit(solution)/shard_map/pallas_call | solution.py:42
  69.4 0.4 fusion.28
  69.8 0.2 multiply_reduce_fusion.4
  70.3 9.4 %shard_map.197.c_ref = bf16[2,256,256]{2,1,0:T(8,128)(2,1)S(1)} custom-call(bf16[32,16,256]{2,1,0:T(8,128)(2,1)S(1)} %fusion.12.refs_0_), custom_call_target="tpu_custom_call" | custom-call | bytes 524288 | tf_op jit(solution)/shard_map/pallas_call | solution.py:42
  79.7 4.0 %shard_map.198.refs_0_ = bf16[2,256,256]{2,1,0:T(8,128)(2,1)S(1)} custom-call(bf16[2,256,256]{2,1,0:T(8,128)(2,1)S(1)} %shard_map.197.c_ref, bf16[16,8,128]{2,1,0:T(8,128)(2,1)S(1)} %get-tuple-element.17.p_ref, bf16[256,1024]{1,0:T(8,128)(2,1)S(1)} %copy-done.6), custom_call_target="tpu_custom_call" | custom-call | tf_op jit(solution)/shard_map/pallas_call | solution.py:301
  83.7 8.5 %shard_map.199 = bf16[32,16,256]{2,1,0:T(8,128)(2,1)S(1)} custom-call(bf16[2,256,256]{2,1,0:T(8,128)(2,1)S(1)} %shard_map.198.refs_0_), custom_call_target="tpu_custom_call" | custom-call | bytes 524288 | tf_op jit(solution)/shard_map/pallas_call | solution.py:42
  92.2 0.3 fusion.29
  92.5 0.2 multiply_reduce_fusion.3
  93.0 0.4 maximum_convert_fusion.1
  93.5 0.8 fusion.30
  94.3 0.2 multiply_reduce_fusion.2
  94.8 0.8 copy.84
  95.6 0.2 fusion.5
  96.4 18.5 %shard_map.200 = (bf16[256,1024]{1,0:T(8,128)(2,1)S(1)}, bf16[256,1024]{1,0:T(8,128)(2,1)S(1)}) custom-call(bf16[16,1024]{1,0:T(8,128)(2,1)S(1)} %reshape.211.l_ref, bf16[16,1024]{1,0:T(8,128)(2,1)S(1)} %reshape.212.r_ref), custom_call_target="tpu_custom_call" | custom-call | bytes 2097152 | tf_op jit(solution)/shard_map/pallas_call | solution.py:42
  115.6 5.1 %shard_map.201 = (f32[128,1024]{1,0:T(8,128)S(1)}, bf16[8,16,1024]{2,1,0:T(8,128)(2,1)S(1)}, bf16[8,16,1024]{2,1,0:T(8,128)(2,1)S(1)}, f32[128,1024]{1,0:T(8,128)S(1)}) custom-call(bf16[256,1024]{1,0:T(8,128)(2,1)S(1)} %get-tuple-element.18.l_ref, bf16[256,1024]{1,0:T(8,128)(2,1)S(1)} %get-tuple-element.19.r_ref, bf16[128,1024]{1,0:T(8,128)(2,1)S(1)} %bitcast.75, ...), custom_call_target="tpu_custom_call" | custom-call | tf_op jit(solution)/shard_map/pallas_call | solution.py:626
  120.7 17.7 %shard_map.202 = (bf16[8,16,1024]{2,1,0:T(8,128)(2,1)S(1)}, bf16[8,16,1024]{2,1,0:T(8,128)(2,1)S(1)}) custom-call(bf16[8,16,1024]{2,1,0:T(8,128)(2,1)S(1)} %get-tuple-element.22.refs_0_, bf16[8,16,1024]{2,1,0:T(8,128)(2,1)S(1)} %get-tuple-element.23.refs_1_), custom_call_target="tpu_custom_call" | custom-call | bytes 524288 | tf_op jit(solution)/shard_map/pallas_call | solution.py:42
  138.8 20.5 %shard_map.203 = (bf16[16,8,1024]{2,1,0:T(8,128)(2,1)S(1)}, bf16[2,16,8,1024]{3,2,1,0:T(8,128)(2,1)S(1)}) custom-call(bf16[16,8,1024]{2,1,0:T(8,128)(2,1)S(1)} %bitcast.71, bf16[16,8,1024]{2,1,0:T(8,128)(2,1)S(1)} %bitcast.72), custom_call_target="tpu_custom_call" | custom-call | bytes 2097152 | tf_op jit(solution)/shard_map/pallas_call | solution.py:42
  159.3 3.9 %shard_map.204.refs_0_ = bf16[16,8,1024]{2,1,0:T(8,128)(2,1)S(1)} custom-call(bf16[16,8,1024]{2,1,0:T(8,128)(2,1)S(1)} %get-tuple-element.26.l_ref, bf16[2,16,8,1024]{3,2,1,0:T(8,128)(2,1)S(1)} %get-tuple-element.27.r_ref), custom_call_target="tpu_custom_call" | custom-call | tf_op jit(solution)/shard_map/pallas_call | solution.py:301
  163.2 8.7 %shard_map.205 = bf16[16,8,1024]{2,1,0:T(8,128)(2,1)S(1)} custom-call(bf16[16,8,1024]{2,1,0:T(8,128)(2,1)S(1)} %shard_map.204.refs_0_), custom_call_target="tpu_custom_call" | custom-call | bytes 524288 | tf_op jit(solution)/shard_map/pallas_call | solution.py:42
  172.2 11.4 %shard_map.206 = bf16[8,16,1024]{2,1,0:T(8,128)(2,1)S(1)} custom-call(bf16[8,16,1024]{2,1,0:T(8,128)(2,1)S(1)} %bitcast.73), custom_call_target="tpu_custom_call" | custom-call | bytes 524288 | tf_op jit(solution)/shard_map/pallas_call | solution.py:42
  183.8 0.3 fusion.31
  184.2 0.7 fusion.4
  184.9 0.8 copy.83
  (82 shorter events, 3.5 us)
Async XLA Ops:
  0.6 92.3 %copy-start = (bf16[256,1024]{1,0:T(8,128)(2,1)S(1)}, bf16[256,1024]{1,0:T(8,128)(2,1)}, u32[]{:S(2)}) copy-start(bf16[256,1024]{1,0:T(8,128)(2,1)} %param.30) | copy-start | bytes 1572868
  4.7 1.0 copy-start.1
  5.7 0.9 copy-start.3
  6.6 62.7 %copy-start.10 = (bf16[256,256]{1,0:T(8,128)(2,1)S(1)}, bf16[256,256]{1,0:T(8,128)(2,1)}, u32[]{:S(2)}) copy-start(bf16[256,256]{1,0:T(8,128)(2,1)} %param.25) | copy-start | bytes 393220
  44.4 25.0 %copy-start.4 = (bf16[16,32,256]{2,1,0:T(8,128)(2,1)S(1)}, bf16[16,32,256]{2,1,0:T(8,128)(2,1)}, u32[]{:S(2)}) copy-start(bf16[16,32,256]{2,1,0:T(8,128)(2,1)} %e_ref.1) | copy-start | bytes 786436
  44.4 1.1 copy-start.5
  55.2 24.4 %copy-start.6 = (bf16[256,1024]{1,0:T(8,128)(2,1)S(1)}, bf16[256,1024]{1,0:T(8,128)(2,1)}, u32[]{:S(2)}) copy-start(bf16[256,1024]{1,0:T(8,128)(2,1)} %w_ref.5) | copy-start | bytes 1572868
  69.4 22.8 %copy-start.11 = (bf16[256,256]{1,0:T(8,128)(2,1)S(1)}, bf16[256,256]{1,0:T(8,128)(2,1)}, u32[]{:S(2)}) copy-start(bf16[256,256]{1,0:T(8,128)(2,1)} %param.29) | copy-start | bytes 393220
  92.2 1.3 copy-start.8
  93.5 2.1 %copy-start.16 = (bf16[256,64]{0,1:T(8,128)(2,1)S(1)}, bf16[256,64]{0,1:T(8,128)(2,1)}, u32[]{:S(2)}) copy-start(bf16[256,64]{0,1:T(8,128)(2,1)} %param.32) | copy-start | bytes 98308
  94.3 20.6 %copy-start.2 = (bf16[32,32,128]{2,1,0:T(8,128)(2,1)S(1)}, bf16[32,32,128]{2,1,0:T(8,128)(2,1)}, u32[]{:S(2)}) copy-start(bf16[32,32,128]{2,1,0:T(8,128)(2,1)} %p_ref.1) | copy-start | bytes 786436
  94.3 20.8 %copy-start.9 = (bf16[1024,128]{1,0:T(8,128)(2,1)S(1)}, bf16[1024,128]{1,0:T(8,128)(2,1)}, u32[]{:S(2)}) copy-start(bf16[1024,128]{1,0:T(8,128)(2,1)} %param.33) | copy-start | bytes 786436
  94.8 20.6 %copy-start.13 = (s32[512]{0:T(512)S(1)}, s32[512]{0:T(512)}, u32[]{:S(2)}) copy-start(s32[512]{0:T(512)} %param.22) | copy-start | bytes 6148
  94.8 20.8 %copy-start.7 = (bf16[128,640]{1,0:T(8,128)(2,1)S(1)}, bf16[128,640]{1,0:T(8,128)(2,1)}, u32[]{:S(2)}) copy-start(bf16[128,640]{1,0:T(8,128)(2,1)} %w_ref.6) | copy-start | bytes 491524
  138.8 45.0 %copy-start.12 = (bf16[128,128]{1,0:T(8,128)(2,1)S(1)}, bf16[128,128]{1,0:T(8,128)(2,1)}, u32[]{:S(2)}) copy-start(bf16[128,128]{1,0:T(8,128)(2,1)} %param.35) | copy-start | bytes 98308
  172.1 12.0 %copy-start.14 = (bf16[512,128]{1,0:T(8,128)(2,1)S(1)}, bf16[512,128]{1,0:T(8,128)(2,1)}, u32[]{:S(2)}) copy-start(bf16[512,128]{1,0:T(8,128)(2,1)} %param.37) | copy-start | bytes 393220
  172.1 12.0 %copy-start.15 = (bf16[128,512]{1,0:T(8,128)(2,1)S(1)}, bf16[128,512]{1,0:T(8,128)(2,1)}, u32[]{:S(2)}) copy-start(bf16[128,512]{1,0:T(8,128)(2,1)} %param.36) | copy-start | bytes 393220

commit v5 on v4

--- a/solution.py
+++ b/solution.py
@@ -417,33 +417,72 @@
     return compute(kernel, out_shape, cols, presence, weights, scratch=scratch)
 
 
-def gather_factors(left, right):
+def norm_channels(x):
+    centre = x - jnp.mean(x, axis=0, keepdims=True)
+    spread = jnp.mean(centre * centre, axis=0, keepdims=True)
+    return centre * lax.rsqrt(spread + EPSILON)
+
+
+def pair_stack(left, right, pair, mix, tri_in, keep, tri_out, up, down):
     rows, wide = left.shape
+    channels, tokens = pair.shape
+    lanes = 128
+    side = PRODUCT_FEATURES
+    per = lanes // side
     chips = GROUP // 2
-
-    def kernel(l_ref, r_ref, ol_ref, or_ref, stage, zsend, zrecv, lsend, lrecv, tsend, trecv, fsend, frecv):
+    few = RING
+    deep = channels // RING
+    chunk = 8 * side
+    chunks = wide // chunk
+    tall = few * side
+    across_k = GROUP * side
+    bf16, f32 = jnp.bfloat16, jnp.float32
+    buffers = {
+        "stage": ((RING, rows, wide), bf16),
+        "all_left": ((GROUP * rows, wide), bf16),
+        "all_right": ((GROUP * rows, wide), bf16),
+        "opm": ((channels, tokens), f32),
+        "gate": ((channels, tokens), f32),
+        "tl": ((RING, deep, tokens), bf16),
+        "tr": ((RING, deep, tokens), bf16),
+        "l1": ((RING, deep, tokens), bf16),
+        "r1": ((RING, deep, tokens), bf16),
+        "turn": ((tokens // lanes, channels, lanes), f32),
+        "l2": ((GROUP, few, tokens), bf16),
+        "r2": ((GROUP, few, tokens), bf16),
+        "l3": ((GROUP, few, tokens), bf16),
+        "r3": ((2, GROUP, few, tokens), bf16),
+        "a": ((tall, across_k), f32),
+        "b": ((2, tall, across_k), f32),
+        "y": ((tall, across_k), f32),
+        "m0": ((GROUP, few, tokens), bf16),
+        "m1": ((GROUP, few, tokens), bf16),
+        "m2": ((RING, deep, tokens), bf16),
+        "m3": ((RING, deep, tokens), bf16),
+    }
+    sems = {
+        "zs": (1, RING), "zr": (1, RING), "ls": (RING,), "lr": (RING,), "ts": (RING,), "tr_": (RING,),
+        "fs": (RING, 2), "fr": (GROUP,), "p1s": (2, chunks, RING), "p1r": (2, chunks, RING),
+        "p2s": (2, GROUP), "p2r": (2, GROUP), "xs": (GROUP,), "xr": (GROUP,),
+        "p3s": (1, GROUP), "p3r": (1, GROUP), "p4s": (1, RING), "p4r": (1, RING),
+    }
+    names = [*buffers, *sems]
+
+    def kernel(l_ref, r_ref, p_ref, mix_ref, in_ref, k_ref, out_ref, up_ref, down_ref, o_ref, *scratch):
+        s = dict(zip(names, scratch))
         br, ro, x, z, b, _ = place()
         core = lax.rem(ro, 2)
         chip = b // 2
         twin = (br, ro + 1 - 2 * core, x, z)
+        cross = crosswise()
         put = lambda ref, k: ref.at[pl.ds(pl.multiple_of(k * rows, rows), rows)]
         at = lambda ref, k: ref.at[k]
-        pushes = Pushes("z", (r_ref,), (stage,), [lambda ref, k: ref], [at], zsend, zrecv)
+        whole = lambda ref, k: ref
+        ol, orr = s["all_left"], s["all_right"]
+        along = Pushes("z", (r_ref,), (s["stage"],), [whole], [at], s["zs"], s["zr"])
         on_core = lambda k: across(k * 2 + core, x * RING + z)
         back = lambda d: lax.rem(chip + chips - d, chips)
         own = br == x
-        barrier = pltpu.get_barrier_semaphore()
-        pushes.greet(barrier)
-
-        def signal(to):
-            pl.semaphore_signal(barrier, inc=1, device_id=to, device_id_type=MESH)
-
-        def greet(d, carry):
-            signal(on_core(lax.rem(chip + d, chips)))
-            return carry
-
-        lax.fori_loop(1, chips, greet, 0)
-        signal(twin)
 
         def each(act):
             def one(d, carry):
@@ -461,22 +500,35 @@
 
             each(one)
 
+        to_channel = Pushes(
+            "b", (s["l2"], s["r2"]), (s["l3"], s["r3"]), [at] * 2, [at, lambda ref, k: ref.at[x, k]],
+            s["p2s"], s["p2r"],
+        )
+        from_channel = Pushes("b", (s["m0"],), (s["m1"],), [at], [at], s["p3s"], s["p3r"])
+        from_ring = Pushes("z", (s["m2"],), (s["m3"],), [at], [at], s["p4s"], s["p4r"])
+
+        barrier = pltpu.get_barrier_semaphore()
+        along.greet(barrier)
+        to_channel.greet(barrier)
+
+        def signal(to):
+            pl.semaphore_signal(barrier, inc=1, device_id=to, device_id_type=MESH)
+
+        signal(cross)
         senders(lambda k, other: signal((other, k, br, z)))
-        pl.semaphore_wait(
-            barrier, RING - 1 + chips - 1 + 1 + jnp.where(own, GROUP - 1, GROUP)
-        )
+        pl.semaphore_wait(barrier, RING - 1 + GROUP - 1 + 1 + jnp.where(own, GROUP - 1, GROUP))
 
         def to_chip(d, coming):
             block = back(d) * 2 + core if coming else b
             peer = back(d) if coming else lax.rem(chip + d, chips)
-            return remote(l_ref, put(ol_ref, block), lsend.at[d], lrecv.at[d], on_core(peer))
+            return remote(l_ref, put(ol, block), s["ls"].at[d], s["lr"].at[d], on_core(peer))
 
         def to_twin(d, coming):
-            block = put(ol_ref, back(d) * 2 + (1 - core if coming else core))
-            return remote(block, block, tsend.at[d], trecv.at[d], twin)
+            block = put(ol, back(d) * 2 + (1 - core if coming else core))
+            return remote(block, block, s["ts"].at[d], s["tr_"].at[d], twin)
 
         def forward(k, other, src):
-            return remote(src, put(or_ref, b), fsend.at[k, other], frecv.at[b], (x, k, other, z))
+            return remote(src, put(orr, b), s["fs"].at[k, other], s["fr"].at[b], (x, k, other, z))
 
         def forward_all(k, src):
             for other in range(2):
@@ -488,289 +540,275 @@
 
                 @pl.when(mine)
                 def _():
-                    put(or_ref, b)[...] = src[...]
+                    put(orr, b)[...] = src[...]
 
         def start(d, carry):
-            for copy in pushes.copies(d, False):
+            for copy in along.copies(d, False):
                 copy.start()
             to_chip(d, False).start()
             return carry
 
         lax.fori_loop(1, RING, start, 0)
-        first = remote(l_ref, put(ol_ref, b), tsend.at[0], trecv.at[0], twin)
+        first = remote(l_ref, put(ol, b), s["ts"].at[0], s["tr_"].at[0], twin)
         first.start()
         forward_all(z, r_ref)
-        put(ol_ref, b)[...] = l_ref[...]
+        put(ol, b)[...] = l_ref[...]
 
         def relay(d, carry):
-            pushes.arrive(d)
-            k = pushes.sender(d)
-            forward_all(k, stage.at[k])
+            along.arrive(d)
+            k = along.sender(d)
+            forward_all(k, s["stage"].at[k])
             to_chip(d, True).wait_recv()
             to_twin(d, False).start()
             return carry
 
         lax.fori_loop(1, RING, relay, 0)
 
-        def last(d, carry):
-            pushes.sent(d)
-            to_chip(d, False).wait_send()
+        def left_in(d, carry):
             to_twin(d, True).wait_recv()
-            to_twin(d, False).wait_send()
-            return carry
-
-        lax.fori_loop(1, RING, last, 0)
-        to_twin(0, True).wait_recv()
-        first.wait_send()
-
-        def sent(k, other):
-            mine = jnp.logical_and(own, jnp.logical_and(k == ro, x == other))
-
-            @pl.when(jnp.logical_not(mine))
-            def _():
-                forward(k, other, r_ref).wait_send()
-
-        each(sent)
+            return carry
+
+        lax.fori_loop(0, RING, left_in, 0)
 
         def come(k, other):
             sender = other * RING + k
-            there = put(or_ref, sender)
-            remote(r_ref, there, fsend.at[k, other], frecv.at[sender], (other, k, br, z)).wait_recv()
+            there = put(orr, sender)
+            remote(r_ref, there, s["fs"].at[k, other], s["fr"].at[sender], (other, k, br, z)).wait_recv()
 
         senders(come)
 
-    shape = jax.ShapeDtypeStruct((GROUP * rows, wide), jnp.bfloat16)
-    scratch = [pltpu.VMEM((RING, rows, wide), jnp.bfloat16)]
-    scratch += [pltpu.SemaphoreType.DMA((1, RING))] * 2
-    scratch += [pltpu.SemaphoreType.DMA((RING,))] * 4
-    scratch += [pltpu.SemaphoreType.DMA((RING, 2)), pltpu.SemaphoreType.DMA((GROUP,))]
-    return call_exchange(kernel, [shape, shape], scratch, 6, 1 << 20, left, right)
-
-
-def norm_channels(x):
-    centre = x - jnp.mean(x, axis=0, keepdims=True)
-    spread = jnp.mean(centre * centre, axis=0, keepdims=True)
-    return centre * lax.rsqrt(spread + EPSILON)
-
-
-def pair_front(left, right, pair, mix, weights, keep):
-    rows, wide = left.shape
-    channels = pair.shape[0]
-    lanes = 128
-    per = lanes // PRODUCT_FEATURES
-    some = 8
-    chunk = some * PRODUCT_FEATURES
-    count = wide // chunk
-    groups = RING
-    deep = channels // groups
-
-    def kernel(l_ref, r_ref, p_ref, m_ref, w_ref, k_ref, opm_ref, tl_ref, tr_ref, gate_ref):
-        lane = lax.broadcasted_iota(jnp.int32, (channels, lanes), 1) // PRODUCT_FEATURES
-
-        def one(g, carry):
+        lane_of = lax.broadcasted_iota(jnp.int32, (channels, lanes), 1) // side
+        contract = (((0,), (0,)), ((), ()))
+
+        def channel_push(k, g, d, coming):
+            src, dst = (s["tl"], s["l1"]) if k == 0 else (s["tr"], s["r1"])
             cols = pl.ds(pl.multiple_of(g * chunk, chunk), chunk)
-            outer = lax.dot_general(
-                l_ref[:, cols], r_ref[...], (((0,), (0,)), ((), ())), preferred_element_type=jnp.float32
+            peer = along.sender(d) if coming else lax.rem(z + d, RING)
+            return remote(
+                src.at[z if coming else peer, :, cols],
+                dst.at[peer if coming else z, :, cols],
+                s["p1s"].at[k, g, d],
+                s["p1r"].at[k, g, d],
+                (br, ro, x, peer),
             )
-            outer = (outer * (1.0 / rows)).astype(jnp.bfloat16)
+
+        def front(g, carry):
+            cols = pl.ds(pl.multiple_of(g * chunk, chunk), chunk)
+            outer = lax.dot_general(ol[:, cols], orr[...], contract, preferred_element_type=f32)
+            outer = (outer * (1.0 / (GROUP * rows))).astype(bf16)
             stacked = jnp.concatenate(
                 [
                     jnp.concatenate(
                         [
-                            outer[
-                                i * PRODUCT_FEATURES : (i + 1) * PRODUCT_FEATURES,
-                                q * lanes : (q + 1) * lanes,
-                            ]
+                            outer[i * side : (i + 1) * side, q * lanes : (q + 1) * lanes]
                             for q in range(wide // lanes)
                         ],
                         axis=0,
                     )
-                    for i in range(some)
+                    for i in range(chunk // side)
                 ],
                 axis=1,
             )
-            mixed = lax.dot_general(
-                m_ref[...], stacked, (((0,), (0,)), ((), ())), preferred_element_type=jnp.float32
-            )
+            mixed = lax.dot_general(mix_ref[...], stacked, contract, preferred_element_type=f32)
             pieces = []
-            for h in range(some // per):
-                piece = jnp.zeros((channels, lanes), jnp.float32)
+            for h in range(chunk // lanes):
+                piece = jnp.zeros((channels, lanes), f32)
                 for i in range(per):
-                    at = (h * per + i) * lanes
+                    at_lane = (h * per + i) * lanes
                     total = None
                     for y in range(per):
-                        part = mixed[y * channels : (y + 1) * channels, at : at + lanes]
-                        shift = (PRODUCT_FEATURES * (i - y)) % lanes
+                        part = mixed[y * channels : (y + 1) * channels, at_lane : at_lane + lanes]
+                        shift = (side * (i - y)) % lanes
                         part = pltpu.roll(part, shift, 1) if shift else part
                         total = part if total is None else total + part
-                    piece = jnp.where(lane == i, total, piece)
+                    piece = jnp.where(lane_of == i, total, piece)
                 pieces.append(piece)
-            opm = p_ref[:, cols].astype(jnp.float32) + jnp.concatenate(pieces, axis=1)
-            opm_ref[:, cols] = opm
-            normed = norm_channels(opm).astype(jnp.bfloat16)
-            projected = lax.dot_general(
-                w_ref[...], normed, (((0,), (0,)), ((), ())), preferred_element_type=jnp.float32
-            )
+            opm = p_ref[:, cols].astype(f32) + jnp.concatenate(pieces, axis=1)
+            s["opm"][:, cols] = opm
+            normed = norm_channels(opm).astype(bf16)
+            projected = lax.dot_general(in_ref[...], normed, contract, preferred_element_type=f32)
             block = lambda k: projected[k * channels : (k + 1) * channels]
             here = k_ref[:, cols]
-            tri_left = (here * jax.nn.sigmoid(block(0)) * block(1)).astype(jnp.bfloat16)
-            tri_right = (here * jax.nn.sigmoid(block(2)) * block(3)).astype(jnp.bfloat16)
-            tl_ref[:, :, cols] = tri_left.reshape(groups, deep, chunk)
-            tr_ref[:, :, cols] = tri_right.reshape(groups, deep, chunk)
-            gate_ref[:, cols] = jax.nn.sigmoid(block(4))
-            return carry
-
-        lax.fori_loop(0, count, one, 0)
-
-    tokens = pair.shape[1]
-    return pl.pallas_call(
-        kernel,
-        out_shape=[
-            jax.ShapeDtypeStruct((channels, tokens), jnp.float32),
-            jax.ShapeDtypeStruct((groups, deep, tokens), jnp.bfloat16),
-            jax.ShapeDtypeStruct((groups, deep, tokens), jnp.bfloat16),
-            jax.ShapeDtypeStruct((channels, tokens), jnp.float32),
-        ],
-        in_specs=[pl.BlockSpec(memory_space=pltpu.VMEM)] * 6,
-        out_specs=[pl.BlockSpec(memory_space=pltpu.VMEM)] * 4,
-        compiler_params=pltpu.CompilerParams(vmem_limit_bytes=40 << 20),
-    )(left, right, pair, mix, weights, keep)
-
-
-def exchange_channels(left, right):
-    channels, few, tokens = left.shape
-
-    def kernel(l_ref, r_ref, ol_ref, or_ref, send, recv, xsend, xrecv):
-        x = place()[2]
-        cross = crosswise()
-        at = lambda ref, k: ref.at[k]
-        here = lambda ref, k: ref.at[x, k]
-        pushes = Pushes("b", (l_ref, r_ref), (ol_ref, or_ref), [at] * 2, [at, here], send, recv)
-        barrier = pltpu.get_barrier_semaphore()
-        pushes.greet(barrier)
-        pl.semaphore_signal(barrier, inc=1, device_id=cross, device_id_type=MESH)
-        pl.semaphore_wait(barrier, GROUP)
+            tri_left = (here * jax.nn.sigmoid(block(0)) * block(1)).astype(bf16)
+            tri_right = (here * jax.nn.sigmoid(block(2)) * block(3)).astype(bf16)
+            s["tl"][:, :, cols] = tri_left.reshape(RING, deep, chunk)
+            s["tr"][:, :, cols] = tri_right.reshape(RING, deep, chunk)
+            s["gate"][:, cols] = jax.nn.sigmoid(block(4))
+
+            def push(d, carry):
+                for k in range(2):
+                    channel_push(k, g, d, False).start()
+                return carry
+
+            lax.fori_loop(1, RING, push, 0)
+            return carry
+
+        lax.fori_loop(0, chunks, front, 0)
+        turn = s["turn"]
+
+        def regroup(src, dst):
+            outer, inner, _ = src.shape
+
+            def one(v, carry):
+                cols = pl.ds(pl.multiple_of(v * lanes, lanes), lanes)
+                for g in range(outer):
+                    turn[v, g * inner : (g + 1) * inner] = src[g, :, cols].astype(f32)
+                for g in range(inner):
+                    dst[g, :, cols] = turn[v, pl.ds(g, outer, stride=inner)].astype(bf16)
+                return carry
+
+            lax.fori_loop(0, tokens // lanes, one, 0)
+
+        s["l1"][z] = s["tl"][z]
+        s["r1"][z] = s["tr"][z]
+        for k, ref in ((0, "l1"), (1, "r1")):
+
+            def arrive(d, carry):
+                for g in range(chunks):
+                    channel_push(k, g, d, True).wait_recv()
+                return carry
+
+            lax.fori_loop(1, RING, arrive, 0)
+            to = s["l2"] if k == 0 else s["r2"]
+            regroup(s[ref], to)
 
         def over(d, coming):
-            there = or_ref.at[1 - x if coming else x, pushes.sender(d)]
-            return remote(there, there, xsend.at[d], xrecv.at[d], cross)
-
-        pushes.start()
-        me = pushes.me
-        first = remote(r_ref.at[me], or_ref.at[x, me], xsend.at[0], xrecv.at[0], cross)
-        first.start()
-
-        def one(d, carry):
-            pushes.arrive(d)
+            there = s["r3"].at[1 - x if coming else x, to_channel.sender(d)]
+            return remote(there, there, s["xs"].at[d], s["xr"].at[d], cross)
+
+        to_channel.start()
+        first_over = remote(s["r2"].at[b], s["r3"].at[x, b], s["xs"].at[0], s["xr"].at[0], cross)
+        first_over.start()
+
+        def hand(d, carry):
+            to_channel.arrive(d)
             over(d, False).start()
             return carry
 
-        lax.fori_loop(1, GROUP, one, 0)
-
-        def last(d, carry):
-            pushes.sent(d)
-            over(d, True).wait_recv()
-            over(d, False).wait_send()
-            return carry
-
-        lax.fori_loop(1, GROUP, last, 0)
-        over(0, True).wait_recv()
-        first.wait_send()
-
-    out_shape = [
-        jax.ShapeDtypeStruct((GROUP, few, tokens), jnp.bfloat16),
-        jax.ShapeDtypeStruct((2, GROUP, few, tokens), jnp.bfloat16),
-    ]
-    scratch = [pltpu.SemaphoreType.DMA((2, GROUP))] * 2 + [pltpu.SemaphoreType.DMA((GROUP,))] * 2
-    return call_exchange(kernel, out_shape, scratch, 8, 1 << 20, left, right)
-
-
-def multiply_channel(left, right):
-    blocks, few, tokens = left.shape
-    side = int(tokens**0.5)
-    lanes = 128
-    per = lanes // side
-    wide = blocks * side
-    tall = few * side
-
-    def kernel(l_ref, r_ref, o_ref, a_ref, b_ref, y_ref):
+        lax.fori_loop(1, GROUP, hand, 0)
         lane = lax.broadcasted_iota(jnp.int32, (few, lanes), 1) // side
 
-        def unfold(block, put):
+        def unfold(block, put_line):
             def one(v, carry):
-                x = block(pl.ds(pl.multiple_of(v * lanes, lanes), lanes)).astype(jnp.float32)
-                x = x.reshape(blocks * few, lanes)
-                turned = [x] + [pltpu.roll(x, side * s, 1) for s in range(1, per)]
+                t = block(pl.ds(pl.multiple_of(v * lanes, lanes), lanes)).astype(f32)
+                t = t.reshape(GROUP * few, lanes)
+                turned = [t] + [pltpu.roll(t, side * n, 1) for n in range(1, per)]
                 for n in range(per):
                     line = []
-                    for q in range(blocks // per):
-                        piece = jnp.zeros((few, lanes), jnp.float32)
+                    for q in range(GROUP // per):
+                        piece = jnp.zeros((few, lanes), f32)
                         for m in range(per):
                             k = (q * per + m) * few
                             piece = jnp.where(lane == m, turned[(m - n) % per][k : k + few], piece)
                         line.append(piece)
-                    put(v * per + n, jnp.concatenate(line, axis=1))
+                    put_line(v * per + n, jnp.concatenate(line, axis=1))
                 return carry
 
             lax.fori_loop(0, side // per, one, 0)
 
+        lines = lambda i: pl.ds(pl.multiple_of(i * few, few), few)
+
         def put_left(i, line):
-            a_ref[pl.ds(pl.multiple_of(i * few, few), few)] = line
-
-        unfold(lambda cols: l_ref[:, :, cols], put_left)
-        for h in range(2):
-
-            def put_right(j, line):
-                b_ref[h, pl.ds(pl.multiple_of(j * few, few), few)] = line
-
-            unfold(lambda cols: r_ref[h, :, :, cols], put_right)
-        a = a_ref[...].astype(jnp.bfloat16)
+            s["a"][lines(i)] = line
+
+        unfold(lambda cols: s["l3"][:, :, cols], put_left)
+        a = s["a"][...].astype(bf16)
         to = lax.broadcasted_iota(jnp.int32, (tall, tall), 0)
         of = lax.broadcasted_iota(jnp.int32, (tall, tall), 1)
-        order = (of == lax.rem(to, side) * few + to // side).astype(jnp.float32).astype(jnp.bfloat16)
-        for h in range(2):
-            b = b_ref[h].astype(jnp.bfloat16)
-            b = jnp.dot(order, b, preferred_element_type=jnp.float32).astype(jnp.bfloat16)
-            y_ref[:, h * tall : (h + 1) * tall] = lax.dot_general(
-                a, b, (((1,), (1,)), ((), ())), preferred_element_type=jnp.float32
+        order = (of == lax.rem(to, side) * few + to // side).astype(f32).astype(bf16)
+
+        def multiply(h, carry):
+            def put_right(j, line):
+                s["b"][h, lines(j)] = line
+
+            unfold(lambda cols: s["r3"][h, :, :, cols], put_right)
+            t = jnp.dot(order, s["b"][h].astype(bf16), preferred_element_type=f32).astype(bf16)
+            s["y"][:, pl.ds(pl.multiple_of(h * tall, tall), tall)] = lax.dot_general(
+                a, t, (((1,), (1,)), ((), ())), preferred_element_type=f32
             )
+            return carry
+
+        multiply(x, 0)
+
+        def over_in(d, carry):
+            over(d, True).wait_recv()
+            return carry
+
+        lax.fori_loop(0, GROUP, over_in, 0)
+        multiply(1 - x, 0)
 
         def fold(v, carry):
             cols = pl.ds(pl.multiple_of(v * lanes, lanes), lanes)
-            y = y_ref[pl.ds(pl.multiple_of(v * per * few, per * few), per * few)]
-            for q in range(wide // lanes):
-                x = y[:, q * lanes : (q + 1) * lanes]
-                turned = [x] + [pltpu.roll(x, side * s, 1) for s in range(1, per)]
+            y = s["y"][pl.ds(pl.multiple_of(v * per * few, per * few), per * few)]
+            for q in range(across_k // lanes):
+                t = y[:, q * lanes : (q + 1) * lanes]
+                turned = [t] + [pltpu.roll(t, side * n, 1) for n in range(1, per)]
                 for m in range(per):
-                    piece = jnp.zeros((few, lanes), jnp.float32)
+                    piece = jnp.zeros((few, lanes), f32)
                     for n in range(per):
                         piece = jnp.where(
                             lane == n, turned[(n - m) % per][n * few : (n + 1) * few], piece
                         )
-                    o_ref[q * per + m, :, cols] = piece.astype(jnp.bfloat16)
+                    s["m0"][q * per + m, :, cols] = piece.astype(bf16)
             return carry
 
         lax.fori_loop(0, side // per, fold, 0)
-
-    out_shape = jax.ShapeDtypeStruct((blocks, few, tokens), jnp.bfloat16)
-    scratch = [
-        pltpu.VMEM((tall, wide), jnp.float32),
-        pltpu.VMEM((2, tall, wide), jnp.float32),
-        pltpu.VMEM((tall, wide), jnp.float32),
-    ]
-    return compute(kernel, out_shape, left, right, scratch=scratch)
-
-
-def triangle(tri_left, tri_right):
-    groups, deep, tokens = tri_left.shape
-    at = lambda ref, k: ref.at[k]
-    left, right = exchange("z", (tri_left, tri_right), (tri_left.shape,) * 2, [at] * 2, [at] * 2, 7)
-    left, right = exchange_channels(jnp.transpose(left, (1, 0, 2)), jnp.transpose(right, (1, 0, 2)))
-    mixed = multiply_channel(left, right)
-    (mixed,) = exchange("b", (mixed,), ((deep, groups, tokens),), [at], [at], 9)
-    mixed = jnp.transpose(mixed, (1, 0, 2))
-    (mixed,) = exchange("z", (mixed,), ((groups, deep, tokens),), [at], [at], 10)
-    return mixed.reshape(groups * deep, tokens)
+        from_channel.start()
+        from_channel.finish()
+        regroup(s["m1"], s["m2"])
+        from_ring.start()
+        from_ring.finish()
+
+        def end(g, carry):
+            cols = pl.ds(pl.multiple_of(g * chunk, chunk), chunk)
+            mixed = s["m3"][:, :, cols].astype(f32).reshape(channels, chunk)
+            mixed = norm_channels(mixed).astype(bf16)
+            mixed = lax.dot_general(out_ref[...], mixed, contract, preferred_element_type=f32)
+            state = s["opm"][:, cols] + s["gate"][:, cols] * mixed
+            normed = norm_channels(state).astype(bf16)
+            hidden = lax.dot_general(up_ref[...], normed, contract, preferred_element_type=f32)
+            hidden = jnp.maximum(hidden, 0.0).astype(bf16)
+            update = lax.dot_general(hidden, down_ref[...], contract, preferred_element_type=f32)
+            o_ref[cols] = (jnp.transpose(state) + update).astype(bf16)
+            return carry
+
+        lax.fori_loop(0, chunks, end, 0)
+
+        def sent(d, carry):
+            along.sent(d)
+            to_chip(d, False).wait_send()
+            to_twin(d, False).wait_send()
+            for k in range(2):
+                for g in range(chunks):
+                    channel_push(k, g, d, False).wait_send()
+            return carry
+
+        lax.fori_loop(1, RING, sent, 0)
+        first.wait_send()
+
+        def forwarded(k, other):
+            mine = jnp.logical_and(own, jnp.logical_and(k == ro, x == other))
+
+            @pl.when(jnp.logical_not(mine))
+            def _():
+                forward(k, other, r_ref).wait_send()
+
+        each(forwarded)
+
+        def handed(d, carry):
+            to_channel.sent(d)
+            over(d, False).wait_send()
+            return carry
+
+        lax.fori_loop(1, GROUP, handed, 0)
+        first_over.wait_send()
+
+    scratch = [pltpu.VMEM(*v) for v in buffers.values()]
+    scratch += [pltpu.SemaphoreType.DMA(v) for v in sems.values()]
+    return call_exchange(
+        kernel, jax.ShapeDtypeStruct((tokens, channels), bf16), scratch, 6, 4 << 20,
+        left, right, pair, mix, tri_in, keep, tri_out, up, down,
+    )
 
 
 def layer_normalize(tensor):
@@ -892,30 +930,23 @@
     right_factor = jnp.transpose(
         factors[..., PRODUCT_FEATURES:].astype(jnp.bfloat16), (0, 2, 1)
     ).reshape(device_local_rows, residue_total * PRODUCT_FEATURES)
-    left_all, right_rows = gather_factors(left_factor, right_factor)
     tokens = residue_total * pair_cols
     pair_first = jnp.transpose(pair_representation.reshape(tokens, CZ))
     mix = jnp.transpose(
         outer_output_matrix.reshape(PRODUCT_FEATURES, PRODUCT_FEATURES // 4, 4 * CZ), (1, 0, 2)
     ).reshape(PRODUCT_FEATURES * PRODUCT_FEATURES // 4, 4 * CZ)
     pair_keep = (keep_here[:, None] * keep_there[None, :]).reshape(1, tokens)
-    pair_opm, tri_left, tri_right, tri_gate = pair_front(
-        left_all, right_rows, pair_first, mix, triangle_input_weights, pair_keep
-    )
-    tri_mixed = triangle(tri_left, tri_right).astype(jnp.float32)
-    contract = (((0,), (0,)), ((), ()))
-    mixed_normed = norm_channels(tri_mixed).astype(jnp.bfloat16)
-    pair_tri = pair_opm + tri_gate * lax.dot_general(
-        triangle_output_matrix, mixed_normed, contract, preferred_element_type=jnp.float32
-    )
-    pair_trans_in = norm_channels(pair_tri).astype(jnp.bfloat16)
-    pair_hidden = jax.nn.relu(
-        lax.dot_general(pair_up_weight, pair_trans_in, contract, preferred_element_type=jnp.float32)
-    ).astype(jnp.bfloat16)
-    updated_pair_state = (
-        jnp.transpose(pair_tri)
-        + lax.dot_general(pair_hidden, pair_down_weight, contract, preferred_element_type=jnp.float32)
-    ).astype(jnp.bfloat16)
+    updated_pair_state = pair_stack(
+        left_factor,
+        right_factor,
+        pair_first,
+        mix,
+        triangle_input_weights,
+        pair_keep,
+        triangle_output_matrix,
+        pair_up_weight,
+        pair_down_weight,
+    )
     updated_pair_state = updated_pair_state.reshape(residue_total, pair_cols, CZ)
     return (alignment_final_state.astype(jnp.bfloat16), updated_pair_state)
 

time: 186 us -> 171 us (0.919)
  Pallas kernels: 169 us -> 156 us
    pallas_call x1 -> x0, Pallas kernels: 5.14 us -> none  [pair_front(): pl.pallas_call(kernel, out_shape=[jax.ShapeDtypeStruct((channels, tokens)...]
    pallas_call x9 -> x5, Pallas kernels: 147 us -> 142 us  [call_exchange(): pl.pallas_call(kernel, out_shape=out_shape, in_specs=[pl.BlockSpec(memory...]
    pallas_call x3 -> x2, Pallas kernels: 17.6 us -> 13.7 us  [compute(): pl.pallas_call(kernel, out_shape=out_shape, in_specs=[pl.BlockSpec(memory...]
    unnamed x36 -> x37, local copies, waits for them, and re-layouts: 4.7 us -> 5.35 us
where the time goes in v5:
time: 171 us; the launch traced here: 170 us
  Pallas kernels  156 us (91%)
  local copies, waits for them, and re-layouts  8.8 us (5%)
  other arithmetic  2.3 us (1%)
  matrix products  2.15 us (1%)
    pallas_call x5, Pallas kernels, call_exchange(): pl.pallas_call(kernel, out_shape=out_shape, in_specs=[pl.BlockSpec(memory...  142 us
    pallas_call x2, Pallas kernels, compute(): pl.pallas_call(kernel, out_shape=out_shape, in_specs=[pl.BlockSpec(memory...  13.7 us
    unnamed x37, local copies, waits for them, and re-layouts  5.35 us

profile of v5, /device:TPU:1, one launch (start us, length us, event | category | flops | bytes accessed | tf_op | source)
XLA Modules:
  0.0 170.3 jit_solution(6300985171431421142)
XLA Ops:
  0.7 0.8 fusion.14
  1.9 0.8 fusion.12
  3.2 0.8 copy.55.w_ref
  4.0 0.7 copy.56.h_ref
  4.7 0.9 copy-done.1
  5.6 0.9 copy-done.3
  6.6 37.7 %shard_map.194 = (bf16[8,256,512]{2,1,0:T(8,128)(2,1)S(1)}, bf16[2,16,40,256]{3,2,1,0:T(8,128)(2,1)S(1)}, bf16[16,8,128]{2,1,0:T(8,128)(2,1)S(1)}) custom-call(bf16[32,32,128]{2,1,0:T(8,128)(2,1)S(1)} %copy-done.1, bf16[128,8]{1,0:T(8,128)(2,1)S(1)} %copy.55.w_ref, f32[8,128]{1,0:T(8,128)S(1)} %compare_convert_fusion.s_ref, f32[8,1]{1,0:T(8,128)S(1)} %copy.56.h_ref, ...), custom_call_target="tpu_custom_call" | custom-call | bytes 4194304 | tf_op jit(solution)/shard_map/pallas_call | solution.py:42
  44.4 1.1 copy-done.5
  45.4 9.8 %shard_map.195.refs_0_ = bf16[2,8,32,256]{3,2,1,0:T(8,128)(2,1)S(1)} custom-call(bf16[2,16,40,256]{3,2,1,0:T(8,128)(2,1)S(1)} %get-tuple-element.5.r_ref, bf16[8,256,512]{2,1,0:T(8,128)(2,1)S(1)} %get-tuple-element.6.b_ref, bf16[256,1024]{1,0:T(8,128)(2,1)S(1)} %copy-done.5), custom_call_target="tpu_custom_call" | custom-call | tf_op jit(solution)/shard_map/pallas_call | solution.py:301
  55.2 14.1 %shard_map.196 = bf16[2,8,32,256]{3,2,1,0:T(8,128)(2,1)S(1)} custom-call(bf16[2,8,32,256]{3,2,1,0:T(8,128)(2,1)S(1)} %shard_map.195.refs_0_), custom_call_target="tpu_custom_call" | custom-call | bytes 524288 | tf_op jit(solution)/shard_map/pallas_call | solution.py:42
  69.3 0.4 fusion.15
  69.8 0.2 multiply_reduce_fusion.2
  70.0 0.2 fusion.4.refs_0_
  70.2 9.4 %shard_map.197.c_ref = bf16[2,256,256]{2,1,0:T(8,128)(2,1)S(1)} custom-call(bf16[32,16,256]{2,1,0:T(8,128)(2,1)S(1)} %fusion.4.refs_0_), custom_call_target="tpu_custom_call" | custom-call | bytes 524288 | tf_op jit(solution)/shard_map/pallas_call | solution.py:42
  79.7 4.0 %shard_map.198.refs_0_ = bf16[2,256,256]{2,1,0:T(8,128)(2,1)S(1)} custom-call(bf16[2,256,256]{2,1,0:T(8,128)(2,1)S(1)} %shard_map.197.c_ref, bf16[16,8,128]{2,1,0:T(8,128)(2,1)S(1)} %get-tuple-element.7.p_ref, bf16[256,1024]{1,0:T(8,128)(2,1)S(1)} %copy-done.6), custom_call_target="tpu_custom_call" | custom-call | tf_op jit(solution)/shard_map/pallas_call | solution.py:301
  83.6 8.5 %shard_map.199 = bf16[32,16,256]{2,1,0:T(8,128)(2,1)S(1)} custom-call(bf16[2,256,256]{2,1,0:T(8,128)(2,1)S(1)} %shard_map.198.refs_0_), custom_call_target="tpu_custom_call" | custom-call | bytes 524288 | tf_op jit(solution)/shard_map/pallas_call | solution.py:42
  92.1 0.3 fusion.16
  92.5 0.2 multiply_reduce_fusion.1
  92.7 0.2 multiply_convert_fusion.1
  92.9 0.4 maximum_convert_fusion
  93.4 0.8 fusion.17
  94.3 0.2 multiply_reduce_fusion
  94.6 0.2 multiply_convert_fusion
  94.8 0.2 fusion
  95.1 0.1 copy.63
  95.3 0.2 reshape.180.r_ref
  95.4 0.2 reshape.179.l_ref
  95.9 0.2 reshape.182
  96.1 0.1 copy.64
  96.3 72.5 %shard_map.200 = bf16[1024,128]{1,0:T(8,128)(2,1)S(1)} custom-call(bf16[16,1024]{1,0:T(8,128)(2,1)S(1)} %reshape.179.l_ref, bf16[16,1024]{1,0:T(8,128)(2,1)S(1)} %reshape.180.r_ref, bf16[128,1024]{1,0:T(8,128)(2,1)S(1)} %bitcast.46, bf16[256,512]{1,0:T(8,128)(2,1)S(1)} %bitcast.45, bf16[128,640]{1,0:T(8,128)(2,1)S(1)} %copy-done.7, ...), custom_call_target="tpu_custom_call" | custom-call | bytes 8388608 | tf_op jit(solution)/shard_map/pallas_call | solution.py:42
  168.8 0.8 copy.66
  169.6 0.7 copy.87
  (63 shorter events, 1.4 us)
Async XLA Ops:
  0.6 92.3 %copy-start = (bf16[256,1024]{1,0:T(8,128)(2,1)S(1)}, bf16[256,1024]{1,0:T(8,128)(2,1)}, u32[]{:S(2)}) copy-start(bf16[256,1024]{1,0:T(8,128)(2,1)} %param.30) | copy-start | bytes 1572868
  4.7 0.9 copy-start.1
  5.6 0.9 copy-start.3
  6.6 62.7 %copy-start.13 = (bf16[256,256]{1,0:T(8,128)(2,1)S(1)}, bf16[256,256]{1,0:T(8,128)(2,1)}, u32[]{:S(2)}) copy-start(bf16[256,256]{1,0:T(8,128)(2,1)} %param.25) | copy-start | bytes 393220
  44.3 25.0 %copy-start.4 = (bf16[16,32,256]{2,1,0:T(8,128)(2,1)S(1)}, bf16[16,32,256]{2,1,0:T(8,128)(2,1)}, u32[]{:S(2)}) copy-start(bf16[16,32,256]{2,1,0:T(8,128)(2,1)} %e_ref.1) | copy-start | bytes 786436
  44.4 1.1 copy-start.5
  55.2 24.5 %copy-start.6 = (bf16[256,1024]{1,0:T(8,128)(2,1)S(1)}, bf16[256,1024]{1,0:T(8,128)(2,1)}, u32[]{:S(2)}) copy-start(bf16[256,1024]{1,0:T(8,128)(2,1)} %w_ref.4) | copy-start | bytes 1572868
  69.3 22.8 %copy-start.14 = (bf16[256,256]{1,0:T(8,128)(2,1)S(1)}, bf16[256,256]{1,0:T(8,128)(2,1)}, u32[]{:S(2)}) copy-start(bf16[256,256]{1,0:T(8,128)(2,1)} %param.29) | copy-start | bytes 393220
  92.1 1.3 copy-start.11
  93.4 1.4 copy-start.16
  94.2 1.4 copy-start.15
  94.2 1.7 copy-start.12
  94.2 1.9 %copy-start.2 = (bf16[32,32,128]{2,1,0:T(8,128)(2,1)S(1)}, bf16[32,32,128]{2,1,0:T(8,128)(2,1)}, u32[]{:S(2)}) copy-start(bf16[32,32,128]{2,1,0:T(8,128)(2,1)} %p_ref.1) | copy-start | bytes 786436
  94.5 1.8 %copy-start.7 = (bf16[128,640]{1,0:T(8,128)(2,1)S(1)}, bf16[128,640]{1,0:T(8,128)(2,1)}, u32[]{:S(2)}) copy-start(bf16[128,640]{1,0:T(8,128)(2,1)} %in_ref.1) | copy-start | bytes 491524
  94.5 1.8 %copy-start.8 = (bf16[128,512]{1,0:T(8,128)(2,1)S(1)}, bf16[128,512]{1,0:T(8,128)(2,1)}, u32[]{:S(2)}) copy-start(bf16[128,512]{1,0:T(8,128)(2,1)} %up_ref.1) | copy-start | bytes 393220
  94.5 1.8 %copy-start.9 = (bf16[512,128]{1,0:T(8,128)(2,1)S(1)}, bf16[512,128]{1,0:T(8,128)(2,1)}, u32[]{:S(2)}) copy-start(bf16[512,128]{1,0:T(8,128)(2,1)} %down_ref.1) | copy-start | bytes 393220
  94.6 1.8 %copy-start.10 = (bf16[128,128]{1,0:T(8,128)(2,1)S(1)}, bf16[128,128]{1,0:T(8,128)(2,1)}, u32[]{:S(2)}) copy-start(bf16[128,128]{1,0:T(8,128)(2,1)} %out_ref.1) | copy-start | bytes 98308

commit v6 on v5

--- a/solution.py
+++ b/solution.py
@@ -38,15 +38,20 @@
     )
 
 
-def call_exchange(kernel, out_shape, scratch, collective_id, sent, *args):
+IN_VMEM = pl.BlockSpec(memory_space=pltpu.VMEM)
+IN_SMEM = pl.BlockSpec(memory_space=pltpu.SMEM)
+IN_PLACE = pl.BlockSpec(memory_space=pl.ANY)
+
+
+def call_exchange(kernel, out_shape, scratch, collective_id, sent, specs, *args):
     return pl.pallas_call(
         kernel,
         out_shape=out_shape,
-        in_specs=[pl.BlockSpec(memory_space=pltpu.VMEM)] * len(args),
-        out_specs=jax.tree.map(lambda _: pl.BlockSpec(memory_space=pltpu.VMEM), out_shape),
+        in_specs=specs,
+        out_specs=jax.tree.map(lambda _: IN_VMEM, out_shape),
         scratch_shapes=scratch,
         compiler_params=pltpu.CompilerParams(
-            collective_id=collective_id, has_side_effects=True, vmem_limit_bytes=48 << 20
+            collective_id=collective_id, has_side_effects=True, vmem_limit_bytes=62 << 20
         ),
         cost_estimate=pl.CostEstimate(flops=0, bytes_accessed=2 * sent, transcendentals=0),
     )(*args)
@@ -113,22 +118,6 @@
         lax.fori_loop(1, self.count, one, 0)
 
 
-def exchange(over, arrays, shapes, picks, puts, collective_id):
-    n = len(arrays)
-
-    def kernel(*refs):
-        pushes = Pushes(over, refs[:n], refs[n : 2 * n], picks, puts, refs[2 * n], refs[2 * n + 1])
-        barrier = pltpu.get_barrier_semaphore()
-        pushes.greet(barrier)
-        pl.semaphore_wait(barrier, SIZES[over] - 1)
-        pushes.start()
-        pushes.finish()
-
-    out_shape = [jax.ShapeDtypeStruct(s, jnp.bfloat16) for s in shapes]
-    scratch = [pltpu.SemaphoreType.DMA((n, GROUP))] * 2
-    return call_exchange(kernel, out_shape, scratch, collective_id, 1 << 18, *arrays)
-
-
 def crosswise():
     br, ro, x, z = place()[:4]
     return (br, ro, 1 - x, z)
@@ -141,9 +130,9 @@
     return (centre * lax.rsqrt(spread + EPSILON)).astype(jnp.bfloat16)
 
 
-def gather_bias_and_rows(pair, weights, same, chain_bias, entries, presence, col_presence):
+def gather_bias_and_rows(pair, weights, same, chain_bias, entries, presence):
     some, others, pair_channels = pair.shape
-    heads = weights.shape[1]
+    heads = weights.shape[0]
     msa_rows, _, channels = entries.shape
     carried = heads // 2
     tall = some + 8
@@ -152,8 +141,8 @@
     n_copies = 32
 
     def kernel(
-        p_ref, w_ref, s_ref, h_ref, e_ref, k_ref, m_ref, ob_ref, or_ref, om_ref,
-        turn, tile, tiles, rows, bsend, brecv, psend, precv, xsend, xrecv, rsend, rrecv,
+        p_in, w_ref, s_ref, h_ref, e_in, k_ref, ob_ref, or_ref, om_ref,
+        p_ref, e_ref, m_ref, load, turn, tile, tiles, rows, bsend, brecv, psend, precv, xsend, xrecv, rsend, rrecv,
     ):
         br, ro, x, z, _, c = place()
         core = lax.rem(ro, 2)
@@ -163,32 +152,59 @@
         cross = crosswise()
         at = lambda ref, k: ref.at[k]
         put = lambda ref, k: ref.at[:, x * RING + k]
-        spread = Pushes("b", (tile, m_ref), (tiles, om_ref), [lambda ref, k: ref, at], [at] * 2, bsend, brecv)
+        spread = Pushes(
+            "b", (tile, m_ref), (tiles, om_ref), [lambda ref, k: ref, lambda ref, k: ref.at[k // 4]], [at] * 2, bsend, brecv
+        )
+        pair_load = pltpu.make_async_copy(p_in, p_ref, load.at[0])
+        entry_load = pltpu.make_async_copy(e_in, e_ref, load.at[1])
+        pair_load.start()
+        entry_load.start()
         pushes = Pushes("z", (rows,), (or_ref,), [lambda ref, k: ref.at[:, k]], [put], psend, precv)
         barrier = pltpu.get_barrier_semaphore()
         spread.greet(barrier)
         pushes.greet(barrier)
         pl.semaphore_signal(barrier, inc=1, device_id=cross, device_id_type=MESH)
 
+        present = k_ref[...].astype(jnp.float32)
+        spot = lax.broadcasted_iota(jnp.int32, (msa_rows, lanes), 0)
+        wide_lane = lax.broadcasted_iota(jnp.int32, (msa_rows, lanes), 1)
+        copies_of = (lax.rem(wide_lane, msa_rows) == spot).astype(jnp.float32)
+        by_residue = lax.dot_general(
+            present, copies_of, (((0,), (0,)), ((), ())), preferred_element_type=jnp.float32
+        )
+        mine = lax.broadcasted_iota(jnp.int32, (some, lanes), 1) // msa_rows == lax.rem(br * 8 + ro, 8)
+        by_residue = jnp.where(mine, by_residue, 0.0).astype(jnp.bfloat16)
+        for k in range(some // 8):
+            m_ref[k] = by_residue[k * 8 : (k + 1) * 8]
+        spot = lax.broadcasted_iota(jnp.int32, (some, channels), 0)
+        wide_lane = lax.broadcasted_iota(jnp.int32, (some, channels), 1)
+        here = jnp.logical_and(lax.rem(wide_lane, some) == spot, wide_lane // some == z)
+        by_row = jnp.dot(present, here.astype(jnp.float32), preferred_element_type=jnp.float32)
+        head_of = lax.broadcasted_iota(jnp.int32, (heads, lanes), 0)
+        chain = jnp.zeros((heads, lanes), jnp.float32)
+        for head in range(heads):
+            chain = jnp.where(head_of == head, h_ref[head], chain)
+        pair_load.wait()
         normed = normal(p_ref[...].reshape(some * others, pair_channels))
         for low in range(8):
             tokens = jnp.concatenate(
                 [normed[(high * 8 + low) * others :][:others] for high in range(fold)], axis=0
             )
             bias = lax.dot_general(
-                w_ref[...], tokens, (((0,), (1,)), ((), ())), preferred_element_type=jnp.float32
+                w_ref[...], tokens, (((1,), (1,)), ((), ())), preferred_element_type=jnp.float32
             )
-            turn[low * heads : (low + 1) * heads] = bias + h_ref[...] * s_ref[low : low + 1]
+            turn[low * heads : (low + 1) * heads] = bias + chain * s_ref[low : low + 1]
         for head in range(heads):
             tile[head] = turn[pl.ds(head, 8, stride=heads)].astype(jnp.bfloat16)
         pl.semaphore_wait(barrier, GROUP - 1 + RING - 1 + 1)
         spread.start()
+        entry_load.wait()
         normed = normal(e_ref[...].reshape(msa_rows * some, channels))
         for half in range(2):
             for k in range(RING):
                 row = half * RING + k
                 rows[half, k, :some] = normed[row * some : (row + 1) * some]
-                rows[half, k, some:] = k_ref[row]
+                rows[half, k, some:] = jnp.broadcast_to(by_row[row : row + 1], (8, channels)).astype(jnp.bfloat16)
         pushes.start()
         first = remote(rows.at[:, z], or_ref.at[:, c], xsend.at[0], xrecv.at[0], cross)
         first.start()
@@ -279,9 +295,13 @@
     out_shape = [
         jax.ShapeDtypeStruct((heads, RING * some, wide), jnp.bfloat16),
         jax.ShapeDtypeStruct((2, GROUP, tall, channels), jnp.bfloat16),
-        jax.ShapeDtypeStruct(col_presence.shape, jnp.bfloat16),
+        jax.ShapeDtypeStruct((GROUP, 8, lanes), jnp.bfloat16),
     ]
     scratch = [
+        pltpu.VMEM(pair.shape, jnp.bfloat16),
+        pltpu.VMEM(entries.shape, jnp.bfloat16),
+        pltpu.VMEM((some // 8, 8, lanes), jnp.bfloat16),
+        pltpu.SemaphoreType.DMA((2,)),
         pltpu.VMEM((8 * heads, lanes), jnp.float32),
         pltpu.VMEM((heads, 8, lanes), jnp.bfloat16),
         pltpu.VMEM((GROUP, heads, 8, lanes), jnp.bfloat16),
@@ -293,19 +313,9 @@
     scratch += [pltpu.SemaphoreType.DMA((n_copies,))] * 2
     return call_exchange(
         kernel, out_shape, scratch, 1, 2 << 20,
-        pair, weights, same, chain_bias, entries, presence, col_presence,
+        [IN_PLACE, IN_VMEM, IN_VMEM, IN_SMEM, IN_PLACE, IN_VMEM],
+        pair, weights, same, chain_bias, entries, presence,
     )
-
-
-def compute(kernel, out_shape, *args, scratch=(), limit=40):
-    return pl.pallas_call(
-        kernel,
-        out_shape=out_shape,
-        in_specs=[pl.BlockSpec(memory_space=pltpu.VMEM)] * len(args),
-        out_specs=jax.tree.map(lambda _: pl.BlockSpec(memory_space=pltpu.VMEM), out_shape),
-        scratch_shapes=list(scratch),
-        compiler_params=pltpu.CompilerParams(vmem_limit_bytes=limit << 20),
-    )(*args)
 
 
 def heads_attend(queries, keys, values, present, bias_of):
@@ -335,97 +345,24 @@
     return jnp.concatenate(blocks, axis=1)
 
 
-def row_attention(rows, bias, weights):
-    pair, blocks, tall, channels = rows.shape
-    some = tall - 8
-    residues = blocks * some
-    step = 128
-
-    def kernel(r_ref, b_ref, w_ref, o_ref, q_ref, g_ref):
-        x = place()[2]
-        for r in range(pair):
-            whole = r_ref[r, :, :some].reshape(residues, channels)
-            keys_values = jnp.dot(
-                whole, w_ref[:, channels : 3 * channels], preferred_element_type=jnp.float32
-            ).astype(jnp.bfloat16)
-            keys, values = keys_values[:, :channels], keys_values[:, channels:]
-            own = r_ref[r, pl.ds(x * RING, RING), :some].reshape(residues // 2, channels)
-            q = jnp.dot(own, w_ref[:, :channels], preferred_element_type=jnp.float32)
-            q_ref[...] = (q * PER_HEAD_WIDTH ** (-0.5)).astype(jnp.bfloat16)
-            gate = jnp.dot(own, w_ref[:, 3 * channels :], preferred_element_type=jnp.float32)
-            g_ref[...] = jax.nn.sigmoid(gate)
-            present = []
-            for half in range(2):
-                total = jnp.zeros((8, channels), jnp.float32)
-                for k in range(RING):
-                    total = total + r_ref[r, half * RING + k, some:].astype(jnp.float32)
-                present.append(total[:1])
-            present = jnp.concatenate(present, axis=1) > 0
-
-            def one(t, carry):
-                at = pl.ds(pl.multiple_of(t * step, step), step)
-                attended = heads_attend(
-                    q_ref[at], keys, values, present, lambda h: b_ref[h, at, :]
-                )
-                gated = (attended * g_ref[at]).astype(jnp.bfloat16)
-                o_ref[r, pl.ds(t * (step // some), step // some)] = gated.reshape(
-                    step // some, some, channels
-                )
-                return carry
-
-            lax.fori_loop(0, residues // 2 // step, one, 0)
-
-    out_shape = jax.ShapeDtypeStruct((pair, RING, some, channels), jnp.bfloat16)
-    scratch = [
-        pltpu.VMEM((residues // 2, channels), jnp.bfloat16),
-        pltpu.VMEM((residues // 2, channels), jnp.float32),
-    ]
-    return compute(kernel, out_shape, rows, bias, weights, scratch=scratch)
-
-
-def column_attention(cols, presence, weights):
-    few, rows, channels = cols.shape
-    step = 128
-
-    def kernel(c_ref, p_ref, w_ref, o_ref, q_ref, g_ref):
-        halves = []
-        for half in range(2):
-            total = jnp.zeros((8, 128), jnp.float32)
-            for k in range(RING):
-                total = total + p_ref[half * RING + k].astype(jnp.float32)
-            halves.append(total)
-        there = jnp.concatenate(halves, axis=1)
-        for r in range(few):
-            whole = c_ref[r]
-            projected = jnp.dot(whole, w_ref[...], preferred_element_type=jnp.float32)
-            q_ref[...] = (projected[:, :channels] * PER_HEAD_WIDTH ** (-0.5)).astype(jnp.bfloat16)
-            keys = projected[:, channels : 2 * channels].astype(jnp.bfloat16)
-            values = projected[:, 2 * channels : 3 * channels].astype(jnp.bfloat16)
-            g_ref[...] = jax.nn.sigmoid(projected[:, 3 * channels :])
-            present = there[r : r + 1] > 0
-
-            def one(t, carry):
-                at = pl.ds(pl.multiple_of(t * step, step), step)
-                attended = heads_attend(q_ref[at], keys, values, present, None)
-                o_ref[r, at] = (attended * g_ref[at]).astype(jnp.bfloat16)
-                return carry
-
-            lax.fori_loop(0, rows // step, one, 0)
-
-    out_shape = jax.ShapeDtypeStruct((few, rows, channels), jnp.bfloat16)
-    scratch = [pltpu.VMEM((rows, channels), jnp.bfloat16), pltpu.VMEM((rows, channels), jnp.float32)]
-    return compute(kernel, out_shape, cols, presence, weights, scratch=scratch)
-
-
 def norm_channels(x):
     centre = x - jnp.mean(x, axis=0, keepdims=True)
     spread = jnp.mean(centre * centre, axis=0, keepdims=True)
     return centre * lax.rsqrt(spread + EPSILON)
 
 
-def pair_stack(left, right, pair, mix, tri_in, keep, tri_out, up, down):
-    rows, wide = left.shape
-    channels, tokens = pair.shape
+def both_stacks(
+    whole_rows, bias, row_weights, row_merge, entries, col_presence, col_weights, col_merge, expand,
+    contract_weights, factor_weights, presence, pair, outer_weights, tri_in, keep, tri_out, up, down,
+):
+    rows, residues, features = entries.shape
+    wide = residues * PRODUCT_FEATURES
+    entry_count = rows * residues
+    columns = residues // GROUP
+    queries = RING * residues
+    keys_count = GROUP * residues
+    step = 128
+    tokens, channels = pair.shape
     lanes = 128
     side = PRODUCT_FEATURES
     per = lanes // side
@@ -437,7 +374,31 @@
     tall = few * side
     across_k = GROUP * side
     bf16, f32 = jnp.bfloat16, jnp.float32
+    inputs = dict(
+        w=whole_rows, wr=row_weights, bias=bias, ow=outer_weights, e=entries, rm=row_merge, cp=col_presence, wc=col_weights,
+        cm=col_merge, ex=expand, co=contract_weights, fw=factor_weights, p=pair, tri_in=tri_in, tri_out=tri_out, up=up,
+        down=down,
+    )
     buffers = {
+        **{"in_" + name: (value.shape, value.dtype) for name, value in inputs.items()},
+        "mix": ((PRODUCT_FEATURES * PRODUCT_FEATURES // 4, 4 * channels), bf16),
+        "outer_f32": (outer_weights.shape, f32),
+        "there": ((8, 2 * lanes), f32),
+        "q": ((queries, features), bf16),
+        "g": ((queries, features), f32),
+        "row_out": ((2, RING, residues, features), bf16),
+        "row_in": ((2, RING, residues, features), bf16),
+        "by_lane": ((features // 128, entry_count, 128), f32),
+        "state": ((entry_count, features), f32),
+        "again": ((entry_count, features), f32),
+        "col_sent": ((residues, rows, features), bf16),
+        "cols": ((columns, GROUP * rows, features), bf16),
+        "col_out": ((columns, GROUP * rows, features), bf16),
+        "col_in": ((residues, rows, features), bf16),
+        "apart": ((rows // 4, PRODUCT_FEATURES, 128), f32),
+        "joined": ((rows * 8, 128), f32),
+        "left": ((rows, wide), bf16),
+        "right": ((rows, wide), bf16),
         "stage": ((RING, rows, wide), bf16),
         "all_left": ((GROUP * rows, wide), bf16),
         "all_right": ((GROUP * rows, wide), bf16),
@@ -461,6 +422,9 @@
         "m3": ((RING, deep, tokens), bf16),
     }
     sems = {
+        "load": (len(inputs),),
+        "rs": (2, RING), "rr": (2, RING), "c1s": (1, GROUP), "c1r": (1, GROUP),
+        "c2s": (1, GROUP), "c2r": (1, GROUP), "c3s": (1, GROUP), "c3r": (1, GROUP),
         "zs": (1, RING), "zr": (1, RING), "ls": (RING,), "lr": (RING,), "ts": (RING,), "tr_": (RING,),
         "fs": (RING, 2), "fr": (GROUP,), "p1s": (2, chunks, RING), "p1r": (2, chunks, RING),
         "p2s": (2, GROUP), "p2r": (2, GROUP), "xs": (GROUP,), "xr": (GROUP,),
@@ -468,8 +432,31 @@
     }
     names = [*buffers, *sems]
 
-    def kernel(l_ref, r_ref, p_ref, mix_ref, in_ref, k_ref, out_ref, up_ref, down_ref, o_ref, *scratch):
+    def kernel(
+        w_in, b_in, wr_in, rm_in, e_in, cp_in, wc_in, cm_in, ex_in, co_in, fw_in, pr_ref,
+        p_in, ow_in, in_in, k_ref, out_in, up_in, down_in, om_ref, o_ref, *scratch,
+    ):
         s = dict(zip(names, scratch))
+        loads = {}
+        for n, (name, ref) in enumerate(
+            dict(
+                w=w_in, wr=wr_in, bias=b_in, ow=ow_in, e=e_in, rm=rm_in, cp=cp_in, wc=wc_in, cm=cm_in, ex=ex_in,
+                co=co_in, fw=fw_in, p=p_in, tri_in=in_in, tri_out=out_in, up=up_in, down=down_in,
+            ).items()
+        ):
+            loads[name] = pltpu.make_async_copy(ref, s["in_" + name], s["load"].at[n])
+            loads[name].start()
+        w_ref, wr_ref, b_ref, ow_ref, e_ref, rm_ref, cp_ref, wc_ref, cm_ref, ex_ref, co_ref, fw_ref, p_ref = (
+            s["in_" + n] for n in ("w", "wr", "bias", "ow", "e", "rm", "cp", "wc", "cm", "ex", "co", "fw", "p")
+        )
+        in_ref, out_ref, up_ref, down_ref = (s["in_" + n] for n in ("tri_in", "tri_out", "up", "down"))
+        mix_ref = s["mix"]
+
+        def ready(*wanted):
+            for name in wanted:
+                loads[name].wait()
+
+        l_ref, r_ref = s["left"], s["right"]
         br, ro, x, z, b, _ = place()
         core = lax.rem(ro, 2)
         chip = b // 2
@@ -516,7 +503,219 @@
 
         signal(cross)
         senders(lambda k, other: signal((other, k, br, z)))
-        pl.semaphore_wait(barrier, RING - 1 + GROUP - 1 + 1 + jnp.where(own, GROUP - 1, GROUP))
+        lane_at = lax.broadcasted_iota(jnp.int32, (1, lanes), 1) // side
+
+        def row_push(r, d, coming):
+            peer = along.sender(d) if coming else lax.rem(z + d, RING)
+            return remote(
+                s["row_out"].at[r, z if coming else peer],
+                s["row_in"].at[r, peer if coming else z],
+                s["rs"].at[r, d],
+                s["rr"].at[r, d],
+                (br, ro, x, peer),
+            )
+
+        ready("w", "wr")
+        for r in range(2):
+            whole_row = w_ref[r, :, :residues].reshape(keys_count, features)
+            keys_values = jnp.dot(
+                whole_row, wr_ref[:, features : 3 * features], preferred_element_type=f32
+            ).astype(bf16)
+            keys, values = keys_values[:, :features], keys_values[:, features:]
+            half_row = w_ref[r, pl.ds(x * RING, RING), :residues].reshape(queries, features)
+            q = jnp.dot(half_row, wr_ref[:, :features], preferred_element_type=f32)
+            s["q"][...] = (q * PER_HEAD_WIDTH ** (-0.5)).astype(bf16)
+            gate = jnp.dot(half_row, wr_ref[:, 3 * features :], preferred_element_type=f32)
+            s["g"][...] = jax.nn.sigmoid(gate)
+            present = []
+            for half in range(2):
+                total = jnp.zeros((8, features), f32)
+                for k in range(RING):
+                    total = total + w_ref[r, half * RING + k, residues:].astype(f32)
+                present.append(total[:1])
+            present = jnp.concatenate(present, axis=1) > 0
+            if r == 0:
+                ready("bias")
+                pl.semaphore_wait(
+                    barrier, RING - 1 + GROUP - 1 + 1 + jnp.where(own, GROUP - 1, GROUP)
+                )
+
+            def row_block(t, carry):
+                t = lax.rem(t + 1 - z // 4, 2)
+                rows_at = pl.ds(pl.multiple_of(t * step, step), step)
+                attended = heads_attend(
+                    s["q"][rows_at], keys, values, present, lambda h: b_ref[h, rows_at, :]
+                )
+                gated = (attended * s["g"][rows_at]).astype(bf16)
+                some = step // residues
+                s["row_out"][r, pl.ds(t * some, some)] = gated.reshape(some, residues, features)
+
+                def push(k, carry):
+                    d = lax.rem(t * some + k - z + RING, RING)
+
+                    @pl.when(d != 0)
+                    def _():
+                        row_push(r, d, False).start()
+
+                    return carry
+
+                lax.fori_loop(0, some, push, 0)
+                return carry
+
+            lax.fori_loop(0, queries // step, row_block, 0)
+            s["row_in"][r, z] = s["row_out"][r, z]
+
+        ready("ow", "e", "rm", "cp", "wc", "fw")
+        s["outer_f32"][...] = ow_ref[...].astype(f32)
+        for q in range(PRODUCT_FEATURES // 4):
+            for y in range(4):
+                mix_ref[q * side : (q + 1) * side, y * channels : (y + 1) * channels] = s["outer_f32"][
+                    pl.ds(q * 4 + y, side, stride=PRODUCT_FEATURES)
+                ].astype(bf16)
+        copied = lax.broadcasted_iota(jnp.int32, (2 * side, lanes), 0)
+        copied_to = lax.rem(lax.broadcasted_iota(jnp.int32, (2 * side, lanes), 1), side)
+        copied = (copied == copied_to).astype(f32).astype(bf16)
+        left_weights = jnp.dot(fw_ref[...], copied, preferred_element_type=f32).astype(bf16)
+        present = pr_ref[...].astype(f32)
+        spot = lax.broadcasted_iota(jnp.int32, (residues, lanes), 0)
+        wide_lane = lax.broadcasted_iota(jnp.int32, (residues, lanes), 1)
+        beside = (lax.rem(wide_lane, residues) == spot).astype(f32)
+        right_presence = jnp.dot(present, beside, preferred_element_type=f32)
+
+        def left_presence(q):
+            spread = jnp.logical_and(spot // per == q, wide_lane // side == lax.rem(spot, per))
+            return jnp.dot(present, spread.astype(f32), preferred_element_type=f32)
+
+        def row_arrive(d, carry):
+            for r in range(2):
+                row_push(r, d, True).wait_recv()
+            return carry
+
+        lax.fori_loop(1, RING, row_arrive, 0)
+
+        part = entry_count // 4
+
+        def merge_rows(g, carry):
+            at_rows = pl.ds(pl.multiple_of(g * part, part), part)
+            few_rows = part // residues
+            half = few_rows * g // RING
+            first_at = lax.rem(few_rows * g, RING)
+            gated = s["row_in"][half, pl.ds(first_at, few_rows)].reshape(part, features)
+            here = e_ref[pl.ds(g * few_rows, few_rows)].reshape(part, features).astype(f32)
+            here = here + jnp.dot(gated, rm_ref[...], preferred_element_type=f32)
+            for k in range(features // lanes):
+                s["by_lane"][k, at_rows] = here[:, k * lanes : (k + 1) * lanes]
+            return carry
+
+        lax.fori_loop(0, 4, merge_rows, 0)
+
+        def turn_rows(g, carry):
+            some = part // rows
+            for i in range(some):
+                at_rows = pl.ds(pl.multiple_of(g * part + i * rows, rows), rows)
+                for k in range(features // lanes):
+                    s["state"][at_rows, k * lanes : (k + 1) * lanes] = s["by_lane"][
+                        k, pl.ds(g * some + i, rows, stride=residues)
+                    ]
+            here = normal(s["state"][pl.ds(pl.multiple_of(g * part, part), part)])
+            s["col_sent"][pl.ds(g * some, some)] = here.reshape(some, rows, features)
+            return carry
+
+        lax.fori_loop(0, 4, turn_rows, 0)
+        pair_of = lambda ref, k: ref.at[pl.ds(k * columns, columns)]
+        rows_of = lambda ref, k: ref.at[:, pl.ds(pl.multiple_of(k * rows, rows), rows)]
+        to_cols = Pushes("b", (s["col_sent"],), (s["cols"],), [pair_of], [rows_of], s["c1s"], s["c1r"])
+        to_cols.start()
+        halves = []
+        for half in range(2):
+            total = jnp.zeros((8, lanes), f32)
+            for k in range(RING):
+                total = total + cp_ref[half * RING + k].astype(f32)
+            halves.append(total)
+        s["there"][...] = jnp.concatenate(halves, axis=1)
+        to_cols.finish()
+        returns = []
+        for r in range(columns):
+            projected = jnp.dot(s["cols"][r], wc_ref[...], preferred_element_type=f32)
+            s["q"][...] = (projected[:, :features] * PER_HEAD_WIDTH ** (-0.5)).astype(bf16)
+            col_keys = projected[:, features : 2 * features].astype(bf16)
+            col_values = projected[:, 2 * features : 3 * features].astype(bf16)
+            s["g"][...] = jax.nn.sigmoid(projected[:, 3 * features :])
+            col_present = s["there"][pl.ds(lax.rem(b, 4) * columns + r, 1)] > 0
+
+            def col_block(t, carry):
+                rows_at = pl.ds(pl.multiple_of(t * step, step), step)
+                attended = heads_attend(s["q"][rows_at], col_keys, col_values, col_present, None)
+                s["col_out"][r, rows_at] = (attended * s["g"][rows_at]).astype(bf16)
+                return carry
+
+            lax.fori_loop(0, GROUP * rows // step, col_block, 0)
+            returns.append(
+                Pushes(
+                    "b",
+                    (s["col_out"],),
+                    (s["col_in"],),
+                    [lambda ref, k, r=r: ref.at[r, pl.ds(pl.multiple_of(k * rows, rows), rows)]],
+                    [lambda ref, k, r=r: ref.at[k * columns + r]],
+                    s["c2s" if r == 0 else "c3s"],
+                    s["c2r" if r == 0 else "c3r"],
+                )
+            )
+            returns[-1].start()
+        for back_again in returns:
+            back_again.finish()
+
+        ready("cm", "ex", "co", "p", "tri_in", "tri_out", "up", "down")
+
+        def transition(g, carry):
+            at_rows = pl.ds(pl.multiple_of(g * part, part), part)
+            some = part // rows
+            gated = s["col_in"][pl.ds(g * some, some)].reshape(part, features)
+            here = s["state"][at_rows] + jnp.dot(gated, cm_ref[...], preferred_element_type=f32)
+            hidden = jnp.dot(normal(here), ex_ref[...], preferred_element_type=f32)
+            hidden = jnp.maximum(hidden, 0.0).astype(bf16)
+            here = here + jnp.dot(hidden, co_ref[...], preferred_element_type=f32)
+            for k in range(features // lanes):
+                s["by_lane"][k, at_rows] = here[:, k * lanes : (k + 1) * lanes]
+            factor = jnp.dot(normal(here), left_weights, preferred_element_type=f32)
+            for q in range(some // per):
+                piece = jnp.zeros((rows, lanes), f32)
+                for m in range(per):
+                    k = (q * per + m) * rows
+                    piece = jnp.where(lane_at == m, factor[k : k + rows], piece)
+                at_q = g * (some // per) + q
+                cols = pl.ds(pl.multiple_of(at_q * lanes, lanes), lanes)
+                l_ref[:, cols] = (piece * left_presence(at_q)).astype(bf16)
+            return carry
+
+        lax.fori_loop(0, 4, transition, 0)
+
+        def turn_back(i, carry):
+            at_rows = pl.ds(pl.multiple_of(i * residues, residues), residues)
+            for k in range(features // lanes):
+                here = s["by_lane"][k, pl.ds(i, residues, stride=rows)]
+                s["again"][at_rows, k * lanes : (k + 1) * lanes] = here
+                om_ref[i, :, k * lanes : (k + 1) * lanes] = here.astype(bf16)
+            return carry
+
+        lax.fori_loop(0, rows, turn_back, 0)
+        for v in range(rows // per):
+            some_rows = s["again"][v * lanes : (v + 1) * lanes]
+            s["apart"][v] = lax.dot_general(
+                fw_ref[...], normal(some_rows), (((0,), (1,)), ((), ())), preferred_element_type=f32
+            )[side:]
+            pieces = [s["apart"][v, pl.ds(m, 8, stride=per)] for m in range(per)]
+            for n in range(per):
+                piece = jnp.zeros((8, lanes), f32)
+                for m in range(per):
+                    shift = (side * (m - n)) % lanes
+                    turned = pltpu.roll(pieces[m], shift, 1) if shift else pieces[m]
+                    piece = jnp.where(lane_at == m, turned, piece)
+                s["joined"][(v * per + n) * 8 : (v * per + n + 1) * 8] = piece
+        for q in range(wide // lanes):
+            cols = slice(q * lanes, (q + 1) * lanes)
+            right = s["joined"][pl.ds(q, rows, stride=8)] * right_presence
+            r_ref[:, cols] = right.astype(bf16)
 
         def to_chip(d, coming):
             block = back(d) * 2 + core if coming else b
@@ -623,7 +822,7 @@
                         total = part if total is None else total + part
                     piece = jnp.where(lane_of == i, total, piece)
                 pieces.append(piece)
-            opm = p_ref[:, cols].astype(f32) + jnp.concatenate(pieces, axis=1)
+            opm = jnp.transpose(p_ref[cols].astype(f32)) + jnp.concatenate(pieces, axis=1)
             s["opm"][:, cols] = opm
             normed = norm_channels(opm).astype(bf16)
             projected = lax.dot_general(in_ref[...], normed, contract, preferred_element_type=f32)
@@ -776,6 +975,8 @@
 
         def sent(d, carry):
             along.sent(d)
+            for r in range(2):
+                row_push(r, d, False).wait_send()
             to_chip(d, False).wait_send()
             to_twin(d, False).wait_send()
             for k in range(2):
@@ -806,16 +1007,13 @@
     scratch = [pltpu.VMEM(*v) for v in buffers.values()]
     scratch += [pltpu.SemaphoreType.DMA(v) for v in sems.values()]
     return call_exchange(
-        kernel, jax.ShapeDtypeStruct((tokens, channels), bf16), scratch, 6, 4 << 20,
-        left, right, pair, mix, tri_in, keep, tri_out, up, down,
+        kernel,
+        [jax.ShapeDtypeStruct(entries.shape, bf16), jax.ShapeDtypeStruct((tokens, channels), bf16)],
+        scratch, 6, 4 << 20,
+        [IN_PLACE] * 11 + [IN_VMEM] + [IN_PLACE] * 3 + [IN_VMEM] + [IN_PLACE] * 3,
+        whole_rows, bias, row_weights, row_merge, entries, col_presence, col_weights, col_merge, expand,
+        contract_weights, factor_weights, presence, pair, outer_weights, tri_in, keep, tri_out, up, down,
     )
-
-
-def layer_normalize(tensor):
-    tensor = tensor.astype(jnp.float32)
-    centre = tensor - jnp.mean(tensor, axis=-1, keepdims=True)
-    spread = jnp.mean(centre * centre, axis=-1, keepdims=True)
-    return centre * lax.rsqrt(spread + EPSILON)
 
 
 def on_device(
@@ -850,97 +1048,33 @@
     residue_keep = residue_presence_mask.astype(jnp.float32)
     keep_here = lax.dynamic_slice_in_dim(residue_keep, row_place * residue_total, residue_total)
     keep_there = lax.dynamic_slice_in_dim(residue_keep, col_place * pair_cols, pair_cols)
-    group_count = GROUP
-    residue_piece = residue_total // group_count
-    key_presence_mask = alignment_entry_mask.astype(jnp.bfloat16)
-    ring_place = lax.axis_index("col_1")
-    row_presence = jnp.tile(key_presence_mask, (1, channel_count // residue_total))
-    row_lane = lax.broadcasted_iota(jnp.int32, row_presence.shape, 1) // residue_total
-    row_presence = jnp.where(row_lane == ring_place, row_presence, 0)
-    row_presence = jnp.pad(row_presence[:, None, :], ((0, 0), (0, 7), (0, 0)))
-    col_presence = jnp.transpose(
-        key_presence_mask.reshape(device_local_rows, group_count, residue_piece), (1, 2, 0)
-    )
-    col_presence = jnp.tile(col_presence, (1, 1, 128 // device_local_rows))
-    col_lane = lax.broadcasted_iota(jnp.int32, col_presence.shape, 2) // device_local_rows
-    col_presence = jnp.where(col_lane == lax.rem(col_place, 8), col_presence, 0)
-    col_presence = jnp.pad(col_presence, ((0, 0), (0, 8 - residue_piece), (0, 0)))
     low_first = jnp.transpose(chain_here.reshape(residue_total // 8, 8))
     same_chain = (low_first[:, :, None] == chain_there[None, None, :]).astype(jnp.float32)
     full_bias, rows_whole, mask_cols = gather_bias_and_rows(
         pair_representation,
-        pair_bias_matrix,
+        jnp.transpose(pair_bias_matrix),
         same_chain.reshape(8, residue_total // 8 * pair_cols),
-        same_chain_bias[:, None],
+        same_chain_bias,
         homolog_embedding,
-        row_presence,
-        col_presence,
+        alignment_entry_mask,
     )
-    gated_whole = row_attention(rows_whole, full_bias, row_projection_weights)
-    along = lambda ref, k: ref.at[:, k]
-    (row_gated,) = exchange("z", (gated_whole,), (gated_whole.shape,), [along], [along], 2)
-    row_gated = row_gated.reshape(device_local_rows, residue_total, channel_count)
-    alignment_row_state = homolog_embedding.astype(jnp.float32) + jnp.dot(
-        row_gated, horizontal_attend_merge, preferred_element_type=jnp.float32
-    )
-    column_normed_input = layer_normalize(alignment_row_state).astype(jnp.bfloat16)
-    split_input = jnp.transpose(column_normed_input, (1, 0, 2))
-    rows_of = lambda ref, k: ref.at[
-        :, pl.ds(pl.multiple_of(k * device_local_rows, device_local_rows), device_local_rows)
-    ]
-    residues_of = lambda ref, k: ref.at[pl.ds(k * residue_piece, residue_piece)]
-    (normed_cols,) = exchange(
-        "b",
-        (split_input,),
-        ((residue_piece, GROUP * device_local_rows, channel_count),),
-        [residues_of],
-        [rows_of],
-        3,
-    )
-    gated = column_attention(normed_cols, mask_cols, column_projection_weights)
-    (returned,) = exchange(
-        "b",
-        (gated,),
-        ((residue_total, device_local_rows, channel_count),),
-        [rows_of],
-        [residues_of],
-        4,
-    )
-    column_gated_output = jnp.transpose(returned, (1, 0, 2))
-    alignment_column_state = alignment_row_state + jnp.dot(
-        column_gated_output, vertical_attend_merge, preferred_element_type=jnp.float32
-    )
-    transition_normed_input = layer_normalize(alignment_column_state).astype(jnp.bfloat16)
-    alignment_hidden_units = jax.nn.relu(
-        jnp.dot(transition_normed_input, homolog_mlp_expand, preferred_element_type=jnp.float32)
-    ).astype(jnp.bfloat16)
-    alignment_final_state = alignment_column_state + jnp.dot(
-        alignment_hidden_units, homolog_mlp_contract, preferred_element_type=jnp.float32
-    )
-    outer_normed_input = layer_normalize(alignment_final_state).astype(jnp.bfloat16)
-    factors = (
-        jnp.dot(outer_normed_input, tensor_product_linear, preferred_element_type=jnp.float32)
-        * alignment_entry_mask.astype(jnp.float32)[:, :, None]
-    )
-    left_factor = (
-        factors[..., :PRODUCT_FEATURES]
-        .astype(jnp.bfloat16)
-        .reshape(device_local_rows, residue_total * PRODUCT_FEATURES)
-    )
-    right_factor = jnp.transpose(
-        factors[..., PRODUCT_FEATURES:].astype(jnp.bfloat16), (0, 2, 1)
-    ).reshape(device_local_rows, residue_total * PRODUCT_FEATURES)
     tokens = residue_total * pair_cols
-    pair_first = jnp.transpose(pair_representation.reshape(tokens, CZ))
-    mix = jnp.transpose(
-        outer_output_matrix.reshape(PRODUCT_FEATURES, PRODUCT_FEATURES // 4, 4 * CZ), (1, 0, 2)
-    ).reshape(PRODUCT_FEATURES * PRODUCT_FEATURES // 4, 4 * CZ)
     pair_keep = (keep_here[:, None] * keep_there[None, :]).reshape(1, tokens)
-    updated_pair_state = pair_stack(
-        left_factor,
-        right_factor,
-        pair_first,
-        mix,
+    msa_out, updated_pair_state = both_stacks(
+        rows_whole,
+        full_bias,
+        row_projection_weights,
+        horizontal_attend_merge,
+        homolog_embedding,
+        mask_cols,
+        column_projection_weights,
+        vertical_attend_merge,
+        homolog_mlp_expand,
+        homolog_mlp_contract,
+        tensor_product_linear,
+        alignment_entry_mask,
+        pair_representation.reshape(tokens, CZ),
+        outer_output_matrix,
         triangle_input_weights,
         pair_keep,
         triangle_output_matrix,
@@ -948,7 +1082,7 @@
         pair_down_weight,
     )
     updated_pair_state = updated_pair_state.reshape(residue_total, pair_cols, CZ)
-    return (alignment_final_state.astype(jnp.bfloat16), updated_pair_state)
+    return (msa_out, updated_pair_state)
 
 
 def solution(mesh):

time: 171 us -> 161 us (0.942)
  Pallas kernels: 156 us -> 152 us
  matrix products: 2.15 us -> 0 us
  local copies, waits for them, and re-layouts: 8.8 us -> 6.81 us
    pallas_call x7 -> x2, Pallas kernels: 156 us -> 152 us  [call_exchange(): pl.pallas_call(kernel, out_shape=out_shape, in_specs=specs, out_specs=jax...]
    dot_general x5 -> x0, matrix products: 2.15 us -> none  [the longest x1 0.79 us: on_device(): jnp.dot(alignment_hidden_units, homolog_mlp_contract, preferred_element_t...]
    unnamed x37 -> x3, local copies, waits for them, and re-layouts: 5.35 us -> 4.83 us
where the time goes in v6:
time: 161 us
  Pallas kernels  152 us (94%)
  local copies, waits for them, and re-layouts  6.81 us (4%)
    pallas_call x2, Pallas kernels, call_exchange(): pl.pallas_call(kernel, out_shape=out_shape, in_specs=specs, out_specs=jax...  152 us
    unnamed x3, local copies, waits for them, and re-layouts  4.83 us

profile of v6, /device:TPU:1, one launch (start us, length us, event | category | flops | bytes accessed | tf_op | source)
XLA Modules:
  0.0 161.1 jit_solution(6728446681731169338)
XLA Ops:
  0.6 0.8 fusion.1
  1.5 0.1 eq.23
  1.6 0.1 reshape.43
  1.6 0.1 copy.21
  1.7 0.7 convert_element_type.8
  2.4 0.1 fusion
  2.5 0.1 eq.20
  2.6 0.1 eq.21
  2.7 0.6 compare_convert_fusion.s_ref
  3.3 0.1 broadcast_multiply_fusion
  3.3 0.7 mul.44.k_ref
  4.0 1.5 copy.22.fw_in
  5.5 40.6 %shard_map.194 = (bf16[8,256,512]{2,1,0:T(8,128)(2,1)}, bf16[2,16,40,256]{3,2,1,0:T(8,128)(2,1)}, bf16[16,8,128]{2,1,0:T(8,128)(2,1)}) custom-call(bf16[32,32,128]{2,1,0:T(8,128)(2,1)} %p_in.1, bf16[8,128]{1,0:T(8,128)(2,1)} %bitcast.7, f32[8,128]{1,0:T(8,128)} %compare_convert_fusion.s_ref, f32[8]{0:T(128)} %h_ref.1, bf16[16,32,256]{2,1,0:T(8,128)(2,1)} %e_in.3, ...), custom_call_target="tpu_custom_call" | custom-call | bytes 4194304 | tf_op jit(solution)/shard_map/pallas_call | solution.py:47
  46.1 111.7 %shard_map.195 = (bf16[16,32,256]{2,1,0:T(8,128)(2,1)}, bf16[1024,128]{1,0:T(8,128)(2,1)}) custom-call(bf16[2,16,40,256]{3,2,1,0:T(8,128)(2,1)} %get-tuple-element.7.w_in, bf16[8,256,512]{2,1,0:T(8,128)(2,1)} %get-tuple-element.8.b_in, bf16[256,1024]{1,0:T(8,128)(2,1)} %wr_in.1, bf16[256,256]{1,0:T(8,128)(2,1)} %rm_in.1, bf16[16,32,256]{2,1,0:T(8,128)(2,1)} %e_in.3, ...), custom_call_target="tpu_custom_call" | custom-call | bytes 8388608 | tf_op jit(solution)/shard_map/pallas_call | solution.py:47
  157.8 1.7 %copy.25 = bf16[16,32,256]{2,1,0:T(8,128)(2,1)} copy(bf16[16,32,256]{2,1,0:T(8,128)(2,1)} %get-tuple-element.18) | data formatting | bytes 524288
  159.4 1.7 %copy.26 = bf16[32,32,128]{2,1,0:T(8,128)(2,1)} copy(bf16[32,32,128]{2,1,0:T(8,128)(2,1)} %bitcast.5) | data formatting | bytes 524288
  (1 shorter events, 0.0 us)

commit v7 on v6

--- a/solution.py
+++ b/solution.py
@@ -130,8 +130,9 @@
     return (centre * lax.rsqrt(spread + EPSILON)).astype(jnp.bfloat16)
 
 
-def gather_bias_and_rows(pair, weights, same, chain_bias, entries, presence):
-    some, others, pair_channels = pair.shape
+def bias_and_rows(pair, weights, entries, residues):
+    some, others = residues, residues
+    pair_channels = pair.shape[1]
     heads = weights.shape[0]
     msa_rows, _, channels = entries.shape
     carried = heads // 2
@@ -141,8 +142,8 @@
     n_copies = 32
 
     def kernel(
-        p_in, w_ref, s_ref, h_ref, e_in, k_ref, ob_ref, or_ref, om_ref,
-        p_ref, e_ref, m_ref, load, turn, tile, tiles, rows, bsend, brecv, psend, precv, xsend, xrecv, rsend, rrecv,
+        p_ref, w_ref, s_ref, h_ref, e_ref, k_ref, pair_ready, entries_ready, entered,
+        ob_ref, or_ref, om_ref, m_ref, turn, tile, tiles, rows, bsend, brecv, psend, precv, xsend, xrecv, rsend, rrecv,
     ):
         br, ro, x, z, _, c = place()
         core = lax.rem(ro, 2)
@@ -155,10 +156,6 @@
         spread = Pushes(
             "b", (tile, m_ref), (tiles, om_ref), [lambda ref, k: ref, lambda ref, k: ref.at[k // 4]], [at] * 2, bsend, brecv
         )
-        pair_load = pltpu.make_async_copy(p_in, p_ref, load.at[0])
-        entry_load = pltpu.make_async_copy(e_in, e_ref, load.at[1])
-        pair_load.start()
-        entry_load.start()
         pushes = Pushes("z", (rows,), (or_ref,), [lambda ref, k: ref.at[:, k]], [put], psend, precv)
         barrier = pltpu.get_barrier_semaphore()
         spread.greet(barrier)
@@ -184,7 +181,7 @@
         chain = jnp.zeros((heads, lanes), jnp.float32)
         for head in range(heads):
             chain = jnp.where(head_of == head, h_ref[head], chain)
-        pair_load.wait()
+        pair_ready()
         normed = normal(p_ref[...].reshape(some * others, pair_channels))
         for low in range(8):
             tokens = jnp.concatenate(
@@ -196,9 +193,9 @@
             turn[low * heads : (low + 1) * heads] = bias + chain * s_ref[low : low + 1]
         for head in range(heads):
             tile[head] = turn[pl.ds(head, 8, stride=heads)].astype(jnp.bfloat16)
-        pl.semaphore_wait(barrier, GROUP - 1 + RING - 1 + 1)
+        entered()
         spread.start()
-        entry_load.wait()
+        entries_ready()
         normed = normal(e_ref[...].reshape(msa_rows * some, channels))
         for half in range(2):
             for k in range(RING):
@@ -292,30 +289,23 @@
             over(d, False).wait_send()
 
     wide = GROUP * others
-    out_shape = [
-        jax.ShapeDtypeStruct((heads, RING * some, wide), jnp.bfloat16),
-        jax.ShapeDtypeStruct((2, GROUP, tall, channels), jnp.bfloat16),
-        jax.ShapeDtypeStruct((GROUP, 8, lanes), jnp.bfloat16),
+    bf16 = jnp.bfloat16
+    arrays = [
+        ((heads, RING * some, wide), bf16),
+        ((2, GROUP, tall, channels), bf16),
+        ((GROUP, 8, lanes), bf16),
+        ((some // 8, 8, lanes), bf16),
+        ((8 * heads, lanes), jnp.float32),
+        ((heads, 8, lanes), bf16),
+        ((GROUP, heads, 8, lanes), bf16),
+        ((2, RING, tall, channels), bf16),
     ]
-    scratch = [
-        pltpu.VMEM(pair.shape, jnp.bfloat16),
-        pltpu.VMEM(entries.shape, jnp.bfloat16),
-        pltpu.VMEM((some // 8, 8, lanes), jnp.bfloat16),
-        pltpu.SemaphoreType.DMA((2,)),
-        pltpu.VMEM((8 * heads, lanes), jnp.float32),
-        pltpu.VMEM((heads, 8, lanes), jnp.bfloat16),
-        pltpu.VMEM((GROUP, heads, 8, lanes), jnp.bfloat16),
-        pltpu.VMEM((2, RING, tall, channels), jnp.bfloat16),
-    ]
+    scratch = [pltpu.VMEM(*v) for v in arrays]
     scratch += [pltpu.SemaphoreType.DMA((2, GROUP))] * 2
     scratch += [pltpu.SemaphoreType.DMA((1, RING))] * 2
     scratch += [pltpu.SemaphoreType.DMA((RING,))] * 2
     scratch += [pltpu.SemaphoreType.DMA((n_copies,))] * 2
-    return call_exchange(
-        kernel, out_shape, scratch, 1, 2 << 20,
-        [IN_PLACE, IN_VMEM, IN_VMEM, IN_SMEM, IN_PLACE, IN_VMEM],
-        pair, weights, same, chain_bias, entries, presence,
-    )
+    return kernel, scratch
 
 
 def heads_attend(queries, keys, values, present, bias_of):
@@ -351,8 +341,8 @@
     return centre * lax.rsqrt(spread + EPSILON)
 
 
-def both_stacks(
-    whole_rows, bias, row_weights, row_merge, entries, col_presence, col_weights, col_merge, expand,
+def whole_block(
+    bias_weights, same, chain_bias, row_weights, row_merge, entries, col_weights, col_merge, expand,
     contract_weights, factor_weights, presence, pair, outer_weights, tri_in, keep, tri_out, up, down,
 ):
     rows, residues, features = entries.shape
@@ -375,8 +365,8 @@
     across_k = GROUP * side
     bf16, f32 = jnp.bfloat16, jnp.float32
     inputs = dict(
-        w=whole_rows, wr=row_weights, bias=bias, ow=outer_weights, e=entries, rm=row_merge, cp=col_presence, wc=col_weights,
-        cm=col_merge, ex=expand, co=contract_weights, fw=factor_weights, p=pair, tri_in=tri_in, tri_out=tri_out, up=up,
+        p=pair, e=entries, wr=row_weights, ow=outer_weights, rm=row_merge, wc=col_weights,
+        cm=col_merge, ex=expand, co=contract_weights, fw=factor_weights, tri_in=tri_in, tri_out=tri_out, up=up,
         down=down,
     )
     buffers = {
@@ -431,24 +421,27 @@
         "p3s": (1, GROUP), "p3r": (1, GROUP), "p4s": (1, RING), "p4r": (1, RING),
     }
     names = [*buffers, *sems]
+    first_part, first_scratch = bias_and_rows(pair, bias_weights, entries, residues)
 
     def kernel(
-        w_in, b_in, wr_in, rm_in, e_in, cp_in, wc_in, cm_in, ex_in, co_in, fw_in, pr_ref,
+        bw_ref, same_ref, chain_ref, wr_in, rm_in, e_in, wc_in, cm_in, ex_in, co_in, fw_in, pr_ref,
         p_in, ow_in, in_in, k_ref, out_in, up_in, down_in, om_ref, o_ref, *scratch,
     ):
         s = dict(zip(names, scratch))
         loads = {}
         for n, (name, ref) in enumerate(
             dict(
-                w=w_in, wr=wr_in, bias=b_in, ow=ow_in, e=e_in, rm=rm_in, cp=cp_in, wc=wc_in, cm=cm_in, ex=ex_in,
-                co=co_in, fw=fw_in, p=p_in, tri_in=in_in, tri_out=out_in, up=up_in, down=down_in,
+                p=p_in, e=e_in, wr=wr_in, ow=ow_in, rm=rm_in, wc=wc_in, cm=cm_in, ex=ex_in,
+                co=co_in, fw=fw_in, tri_in=in_in, tri_out=out_in, up=up_in, down=down_in,
             ).items()
         ):
             loads[name] = pltpu.make_async_copy(ref, s["in_" + name], s["load"].at[n])
             loads[name].start()
-        w_ref, wr_ref, b_ref, ow_ref, e_ref, rm_ref, cp_ref, wc_ref, cm_ref, ex_ref, co_ref, fw_ref, p_ref = (
-            s["in_" + n] for n in ("w", "wr", "bias", "ow", "e", "rm", "cp", "wc", "cm", "ex", "co", "fw", "p")
+        wr_ref, ow_ref, e_ref, rm_ref, wc_ref, cm_ref, ex_ref, co_ref, fw_ref, p_ref = (
+            s["in_" + n] for n in ("wr", "ow", "e", "rm", "wc", "cm", "ex", "co", "fw", "p")
         )
+        of_first = scratch[len(names) :]
+        b_ref, w_ref, cp_ref = of_first[:3]
         in_ref, out_ref, up_ref, down_ref = (s["in_" + n] for n in ("tri_in", "tri_out", "up", "down"))
         mix_ref = s["mix"]
 
@@ -505,6 +498,15 @@
         senders(lambda k, other: signal((other, k, br, z)))
         lane_at = lax.broadcasted_iota(jnp.int32, (1, lanes), 1) // side
 
+        def entered():
+            others = jnp.where(own, GROUP - 1, GROUP)
+            pl.semaphore_wait(barrier, 2 * (RING - 1 + GROUP - 1 + 1) + others)
+
+        first_part(
+            p_ref, bw_ref, same_ref, chain_ref, e_ref, pr_ref,
+            lambda: ready("p"), lambda: ready("e"), entered, *of_first,
+        )
+
         def row_push(r, d, coming):
             peer = along.sender(d) if coming else lax.rem(z + d, RING)
             return remote(
@@ -515,7 +517,7 @@
                 (br, ro, x, peer),
             )
 
-        ready("w", "wr")
+        ready("wr")
         for r in range(2):
             whole_row = w_ref[r, :, :residues].reshape(keys_count, features)
             keys_values = jnp.dot(
@@ -534,11 +536,6 @@
                     total = total + w_ref[r, half * RING + k, residues:].astype(f32)
                 present.append(total[:1])
             present = jnp.concatenate(present, axis=1) > 0
-            if r == 0:
-                ready("bias")
-                pl.semaphore_wait(
-                    barrier, RING - 1 + GROUP - 1 + 1 + jnp.where(own, GROUP - 1, GROUP)
-                )
 
             def row_block(t, carry):
                 t = lax.rem(t + 1 - z // 4, 2)
@@ -565,7 +562,7 @@
             lax.fori_loop(0, queries // step, row_block, 0)
             s["row_in"][r, z] = s["row_out"][r, z]
 
-        ready("ow", "e", "rm", "cp", "wc", "fw")
+        ready("ow", "rm", "wc", "fw")
         s["outer_f32"][...] = ow_ref[...].astype(f32)
         for q in range(PRODUCT_FEATURES // 4):
             for y in range(4):
@@ -575,7 +572,9 @@
         copied = lax.broadcasted_iota(jnp.int32, (2 * side, lanes), 0)
         copied_to = lax.rem(lax.broadcasted_iota(jnp.int32, (2 * side, lanes), 1), side)
         copied = (copied == copied_to).astype(f32).astype(bf16)
-        left_weights = jnp.dot(fw_ref[...], copied, preferred_element_type=f32).astype(bf16)
+        left_weights = lax.dot_general(
+            copied, fw_ref[...], (((0,), (0,)), ((), ())), preferred_element_type=f32
+        ).astype(bf16)
         present = pr_ref[...].astype(f32)
         spot = lax.broadcasted_iota(jnp.int32, (residues, lanes), 0)
         wide_lane = lax.broadcasted_iota(jnp.int32, (residues, lanes), 1)
@@ -665,7 +664,7 @@
         for back_again in returns:
             back_again.finish()
 
-        ready("cm", "ex", "co", "p", "tri_in", "tri_out", "up", "down")
+        ready("cm", "ex", "co", "tri_in", "tri_out", "up", "down")
 
         def transition(g, carry):
             at_rows = pl.ds(pl.multiple_of(g * part, part), part)
@@ -677,7 +676,9 @@
             here = here + jnp.dot(hidden, co_ref[...], preferred_element_type=f32)
             for k in range(features // lanes):
                 s["by_lane"][k, at_rows] = here[:, k * lanes : (k + 1) * lanes]
-            factor = jnp.dot(normal(here), left_weights, preferred_element_type=f32)
+            factor = lax.dot_general(
+                normal(here), left_weights, (((1,), (1,)), ((), ())), preferred_element_type=f32
+            )
             for q in range(some // per):
                 piece = jnp.zeros((rows, lanes), f32)
                 for m in range(per):
@@ -702,7 +703,7 @@
         for v in range(rows // per):
             some_rows = s["again"][v * lanes : (v + 1) * lanes]
             s["apart"][v] = lax.dot_general(
-                fw_ref[...], normal(some_rows), (((0,), (1,)), ((), ())), preferred_element_type=f32
+                fw_ref[...], normal(some_rows), (((1,), (1,)), ((), ())), preferred_element_type=f32
             )[side:]
             pieces = [s["apart"][v, pl.ds(m, 8, stride=per)] for m in range(per)]
             for n in range(per):
@@ -1006,12 +1007,13 @@
 
     scratch = [pltpu.VMEM(*v) for v in buffers.values()]
     scratch += [pltpu.SemaphoreType.DMA(v) for v in sems.values()]
+    scratch += first_scratch
     return call_exchange(
         kernel,
         [jax.ShapeDtypeStruct(entries.shape, bf16), jax.ShapeDtypeStruct((tokens, channels), bf16)],
         scratch, 6, 4 << 20,
-        [IN_PLACE] * 11 + [IN_VMEM] + [IN_PLACE] * 3 + [IN_VMEM] + [IN_PLACE] * 3,
-        whole_rows, bias, row_weights, row_merge, entries, col_presence, col_weights, col_merge, expand,
+        [IN_VMEM] * 2 + [IN_SMEM] + [IN_PLACE] * 8 + [IN_VMEM] + [IN_PLACE] * 3 + [IN_VMEM] + [IN_PLACE] * 3,
+        bias_weights, same, chain_bias, row_weights, row_merge, entries, col_weights, col_merge, expand,
         contract_weights, factor_weights, presence, pair, outer_weights, tri_in, keep, tri_out, up, down,
     )
 
@@ -1050,28 +1052,20 @@
     keep_there = lax.dynamic_slice_in_dim(residue_keep, col_place * pair_cols, pair_cols)
     low_first = jnp.transpose(chain_here.reshape(residue_total // 8, 8))
     same_chain = (low_first[:, :, None] == chain_there[None, None, :]).astype(jnp.float32)
-    full_bias, rows_whole, mask_cols = gather_bias_and_rows(
-        pair_representation,
+    tokens = residue_total * pair_cols
+    pair_keep = (keep_here[:, None] * keep_there[None, :]).reshape(1, tokens)
+    msa_out, updated_pair_state = whole_block(
         jnp.transpose(pair_bias_matrix),
         same_chain.reshape(8, residue_total // 8 * pair_cols),
         same_chain_bias,
-        homolog_embedding,
-        alignment_entry_mask,
-    )
-    tokens = residue_total * pair_cols
-    pair_keep = (keep_here[:, None] * keep_there[None, :]).reshape(1, tokens)
-    msa_out, updated_pair_state = both_stacks(
-        rows_whole,
-        full_bias,
         row_projection_weights,
         horizontal_attend_merge,
         homolog_embedding,
-        mask_cols,
         column_projection_weights,
         vertical_attend_merge,
         homolog_mlp_expand,
         homolog_mlp_contract,
-        tensor_product_linear,
+        jnp.transpose(tensor_product_linear),
         alignment_entry_mask,
         pair_representation.reshape(tokens, CZ),
         outer_output_matrix,

time: 161 us -> 154 us (0.957)
  Pallas kernels: 152 us -> 148 us
  local copies, waits for them, and re-layouts: 6.81 us -> 4.93 us
    pallas_call x2 -> x1, Pallas kernels: 152 us -> 148 us  [call_exchange(): pl.pallas_call(kernel, out_shape=out_shape, in_specs=specs, out_specs=jax...]
    unnamed x3 -> x8, local copies, waits for them, and re-layouts: 4.83 us -> 3.7 us
where the time goes in v7:
time: 154 us
  Pallas kernels  148 us (96%)
  local copies, waits for them, and re-layouts  4.93 us (3%)
    pallas_call x1, Pallas kernels, call_exchange(): pl.pallas_call(kernel, out_shape=out_shape, in_specs=specs, out_specs=jax...  148 us
    unnamed x8, local copies, waits for them, and re-layouts  3.7 us

profile of v7, /device:TPU:1, one launch (start us, length us, event | category | flops | bytes accessed | tf_op | source)
XLA Modules:
  0.0 153.9 jit_solution(11422333318489645763)
XLA Ops:
  0.6 0.0 copy-start.2
  0.6 0.7 copy-done.2
  1.3 0.1 fusion.1
  1.4 0.1 eq.23
  1.5 0.1 reshape.43
  1.6 0.0 copy-start.1
  1.6 0.1 copy.21
  1.7 0.6 copy-done.1
  2.3 0.1 fusion
  2.3 0.1 eq.20
  2.4 0.1 eq.21
  2.5 0.6 compare_convert_fusion.same_ref
  3.1 0.1 broadcast_multiply_fusion
  3.2 0.7 mul.44.k_ref
  3.8 147.6 %shard_map.194 = (bf16[16,32,256]{2,1,0:T(8,128)(2,1)}, bf16[1024,128]{1,0:T(8,128)(2,1)}) custom-call(bf16[8,128]{1,0:T(8,128)(2,1)} %bitcast.9, f32[8,128]{1,0:T(8,128)} %compare_convert_fusion.same_ref, f32[8]{0:T(128)} %chain_ref.1, bf16[256,1024]{1,0:T(8,128)(2,1)} %wr_in.1, bf16[256,256]{1,0:T(8,128)(2,1)} %rm_in.1, bf16[16,32,256]{2,1,0:T(8,128)(2,1)} %e_in.1, ...), custom_call_target="tpu_custom_call" | custom-call | bytes 8388608 | tf_op jit(solution)/shard_map/pallas_call | solution.py:47
  151.5 0.0 copy-start
  151.5 1.7 %copy.24 = bf16[16,32,256]{2,1,0:T(8,128)(2,1)} copy(bf16[16,32,256]{2,1,0:T(8,128)(2,1)} %get-tuple-element.12) | data formatting | bytes 524288
  153.2 0.0 copy-done
  153.2 0.7 copy.25
  (2 shorter events, 0.0 us)
Async XLA Ops:
  0.6 0.7 copy-start.2
  1.6 0.7 copy-start.1
  151.5 1.7 %copy-start = (bf16[1024,128]{1,0:T(8,128)(2,1)S(1)}, bf16[1024,128]{1,0:T(8,128)(2,1)}, u32[]{:S(2)}) copy-start(bf16[1024,128]{1,0:T(8,128)(2,1)} %get-tuple-element.5) | copy-start | bytes 786436

commit v8 on v7

--- a/solution.py
+++ b/solution.py
@@ -97,7 +97,7 @@
                 copy.start()
             return carry
 
-        lax.fori_loop(1, self.count, one, 0)
+        lax.fori_loop(1, self.count, one, 0, unroll=True)
         for src, dst, pick, put in self.parts:
             put(dst, self.me)[...] = pick(src, self.me)[...]
 
@@ -115,7 +115,7 @@
             self.sent(d)
             return carry
 
-        lax.fori_loop(1, self.count, one, 0)
+        lax.fori_loop(1, self.count, one, 0, unroll=True)
 
 
 def crosswise():
@@ -556,7 +556,7 @@
 
                     return carry
 
-                lax.fori_loop(0, some, push, 0)
+                lax.fori_loop(0, some, push, 0, unroll=True)
                 return carry
 
             lax.fori_loop(0, queries // step, row_block, 0)
@@ -748,7 +748,7 @@
             to_chip(d, False).start()
             return carry
 
-        lax.fori_loop(1, RING, start, 0)
+        lax.fori_loop(1, RING, start, 0, unroll=True)
         first = remote(l_ref, put(ol, b), s["ts"].at[0], s["tr_"].at[0], twin)
         first.start()
         forward_all(z, r_ref)
@@ -762,7 +762,7 @@
             to_twin(d, False).start()
             return carry
 
-        lax.fori_loop(1, RING, relay, 0)
+        lax.fori_loop(1, RING, relay, 0, unroll=True)
 
         def left_in(d, carry):
             to_twin(d, True).wait_recv()
@@ -840,7 +840,7 @@
                     channel_push(k, g, d, False).start()
                 return carry
 
-            lax.fori_loop(1, RING, push, 0)
+            lax.fori_loop(1, RING, push, 0, unroll=True)
             return carry
 
         lax.fori_loop(0, chunks, front, 0)
@@ -885,7 +885,7 @@
             over(d, False).start()
             return carry
 
-        lax.fori_loop(1, GROUP, hand, 0)
+        lax.fori_loop(1, GROUP, hand, 0, unroll=True)
         lane = lax.broadcasted_iota(jnp.int32, (few, lanes), 1) // side
 
         def unfold(block, put_line):

time: 154 us -> 153 us (level)
  no operation moved by 1% of the time
where the time goes in v8:
time: 153 us
  Pallas kernels  147 us (96%)
  local copies, waits for them, and re-layouts  4.93 us (3%)
    pallas_call x1, Pallas kernels, call_exchange(): pl.pallas_call(kernel, out_shape=out_shape, in_specs=specs, out_specs=jax...  147 us
    unnamed x8, local copies, waits for them, and re-layouts  3.7 us

profile of v8, /device:TPU:1, one launch (start us, length us, event | category | flops | bytes accessed | tf_op | source)
XLA Modules:
  0.0 152.8 jit_solution(12416025848905669612)
XLA Ops:
  0.6 0.0 copy-start.2
  0.6 0.7 copy-done.2
  1.3 0.1 fusion.1
  1.4 0.1 eq.23
  1.5 0.1 reshape.43
  1.6 0.0 copy-start.1
  1.6 0.1 copy.21
  1.7 0.6 copy-done.1
  2.3 0.1 fusion
  2.3 0.1 eq.20
  2.4 0.1 eq.21
  2.5 0.6 compare_convert_fusion.same_ref
  3.1 0.1 broadcast_multiply_fusion
  3.2 0.7 mul.44.k_ref
  3.8 146.5 %shard_map.194 = (bf16[16,32,256]{2,1,0:T(8,128)(2,1)}, bf16[1024,128]{1,0:T(8,128)(2,1)}) custom-call(bf16[8,128]{1,0:T(8,128)(2,1)} %bitcast.9, f32[8,128]{1,0:T(8,128)} %compare_convert_fusion.same_ref, f32[8]{0:T(128)} %chain_ref.1, bf16[256,1024]{1,0:T(8,128)(2,1)} %wr_in.1, bf16[256,256]{1,0:T(8,128)(2,1)} %rm_in.1, bf16[16,32,256]{2,1,0:T(8,128)(2,1)} %e_in.1, ...), custom_call_target="tpu_custom_call" | custom-call | bytes 8388608 | tf_op jit(solution)/shard_map/pallas_call | solution.py:47
  150.4 0.0 copy-start
  150.4 1.7 %copy.24 = bf16[16,32,256]{2,1,0:T(8,128)(2,1)} copy(bf16[16,32,256]{2,1,0:T(8,128)(2,1)} %get-tuple-element.12) | data formatting | bytes 524288
  152.1 0.0 copy-done
  152.1 0.7 copy.25
  (2 shorter events, 0.0 us)
Async XLA Ops:
  0.6 0.7 copy-start.2
  1.6 0.7 copy-start.1
  150.4 1.7 %copy-start = (bf16[1024,128]{1,0:T(8,128)(2,1)S(1)}, bf16[1024,128]{1,0:T(8,128)(2,1)}, u32[]{:S(2)}) copy-start(bf16[1024,128]{1,0:T(8,128)(2,1)} %get-tuple-element.5) | copy-start | bytes 786436
